TPU v7x, 32 devices: a whole 2x2x4 slice. The times are simulated.
32 devices in a mesh: groups: 2 (over x), mix: 16 (over z, y, core).
Axes of the slice: x: 2, y: 2, z: 4, core: 2. Of those that a mesh axis runs over, the one named last changes fastest.
Arguments:
- resid_in: bfloat16 [4096, 2048], P(('groups', 'mix')), parts along dimension 0, may hold values from -40 to 40
- head_in: bfloat16 [4096, 4096], P('groups', 'mix'), parts along dimension 0, may hold values from -6 to 6
- gate_in: bfloat16 [4096, 4096], P('groups', 'mix'), parts along dimension 0, may hold values from -64 to 64
- in_basis: bfloat16 [4096, 128], P('groups'), parts along dimension 0, may hold values from -6 to 6
- out_basis: bfloat16 [4096, 128], P('groups'), parts along dimension 0, may hold values from -6 to 6
- step_size: float32 [64, 4096], P('mix', 'groups'), parts along dimension 1, may hold values from 0 to 2
- decay_rate: float32 [64], P('mix'), may hold values from 0.5 to 2
- init_state: float32 [16, 64, 64, 128], P('groups', 'mix'), parts along dimension 0, may hold values from -0.6 to 0.6
- lengths: int32 [16], P('groups'), parts along dimension 0, may hold values from 1 to 512, 2048 in all
- norm_gain: float32 [4096], replicated, may hold values from 0.1 to 1.9
- out_proj: bfloat16 [4096, 2048], P('mix'), may hold values from -0.09375 to 0.09375
- moe_gain: float32 [2048], replicated, may hold values from 0.1 to 1.9
- expert_ids: int32 [4096, 8], P(('groups', 'mix')), parts along dimension 0, may hold values from 0 to 31, as said below
- route_weight: float32 [4096, 8], P(('groups', 'mix')), parts along dimension 0, may hold values from 0.1 to 0.4
- placement: int32 [32], replicated, may hold values from 0 to 31, each once
- w_gate: bfloat16 [32, 2048, 768], P('mix'), may hold values from -0.125 to 0.125
- w_up: bfloat16 [32, 2048, 768], P('mix'), may hold values from -0.125 to 0.125
- w_down: bfloat16 [32, 768, 2048], P('mix'), may hold values from -0.21875 to 0.21875
Outputs:
- layer_out: bfloat16 [4096, 2048], P(('groups', 'mix')), parts along dimension 0
There are 2 independent parts, one for each index of `groups`. A program takes and returns all parts, laid end to end along the dimension named above; an argument that names none is the same for every part. Nothing has to cross between parts.
Inputs may be any that keep to these rules, and one draw needn't show every extreme that they name: `expert_ids`: each row names 8 different experts. Within each aligned block of 128 rows (one device's rows), 8 experts appear exactly 64 times each, 8 others 64 / 2 times each and the rest 64 / 4 times each; each of the three sets is the same in every block. `placement`: each slot once. `lengths`: requests fill the 2048 positions in order.
All inputs are finite; a program needn't handle non-finite values.
Results may differ from a plain program's by a relative error of at most 0.013.
Values may be sent and summed in bfloat16 or wider, within the bound.
No kernel may reach another device: no remote copies, remote signals or barrier semaphores. Data moves between devices by JAX's collectives and lax.ppermute only.
A program may use at most 128 MiB of HBM per device.

v0:
```python
import functools

import jax
import jax.numpy as jnp
from jax import lax
from jax.experimental import pallas as pl
from jax.experimental.pallas import tpu as pltpu
from jax.sharding import PartitionSpec as P


epsilon = 1e-05
LANES = 128
NT = (((1,), (1,)), ((), ()))
TN = (((0,), (0,)), ((), ()))


def mm(a, b, dims=(((1,), (0,)), ((), ())), precision=None):
    return lax.dot_general(
        a, b, dims, precision=precision, preferred_element_type=jnp.float32
    )


def scan_kernel(
    starts, place, prep_ref, x_ref, g_ref, b_ref, c_ref, init_ref, same_ref, core_ref, row_ref, far_ref,
    state, src, first_src, *, heads, requests
):
    span, width = x_ref.shape
    tok = same_ref.shape[1]
    head_dim = width // heads
    c0 = pl.program_id(0) * span
    steps = prep_ref[0:8, :]
    run = prep_ref[8:16, :]
    lane = lax.broadcasted_iota(jnp.int32, run.shape, 1)
    shift = 1
    while shift < span:
        run = run + jnp.where(lane >= shift, pltpu.roll(run, shift, 1), 0.0)
        shift *= 2
    before = jnp.zeros_like(run)
    first_last = jnp.int32(0)
    pos = lax.broadcasted_iota(jnp.int32, (span, 1), 0) + c0
    first = jnp.zeros_like(pos)
    inside = []
    for r in range(requests):
        start = starts[r]
        at = start - c0
        here = jnp.logical_and(at >= 0, at < span)
        inside.append(here)
        value = jnp.sum(jnp.where(lane == at - 1, run, 0.0), axis=1, keepdims=True)
        from_here = jnp.where(here, at, span)
        before = jnp.where(lane >= from_here, value, before)
        first_last = jnp.where(at < span, start, first_last)
        first = jnp.where(pos >= start, start, first)
    weight = jnp.exp(run - before)
    last = jnp.where(lane >= first_last - c0, jnp.exp(run[:, span - 1 : span] - run), 0.0)

    spread_row = lax.broadcasted_iota(jnp.int32, (8, width), 0)
    spread_col = lax.broadcasted_iota(jnp.int32, (8, width), 1) // head_dim
    spread = jnp.where(spread_row == spread_col, 1.0, 0.0)

    def widen(rows):
        return mm(rows, spread, TN, lax.Precision.HIGHEST)

    @pl.when(pl.program_id(0) == 0)
    def _():
        state[...] = jnp.zeros_like(state)

    drive = x_ref[...].astype(jnp.float32) * widen(steps)
    drive_low = drive.astype(jnp.bfloat16)
    drive_last = (drive * widen(last)).astype(jnp.bfloat16)
    basis = b_ref[...]
    readout = c_ref[...]
    row = lax.broadcasted_iota(jnp.int32, (span, span), 0)
    col = lax.broadcasted_iota(jnp.int32, (span, span), 1)
    valid = jnp.logical_and(col <= row, col >= first - c0)
    scores = jnp.where(valid, mm(readout, basis, NT), 0.0)

    src[...] = mm(readout, state[...].astype(jnp.bfloat16))
    first_src[...] = state[...]
    for r in range(requests):

        @pl.when(inside[r])
        def _(r=r):
            init = init_ref[r].T
            mine = mm(readout, init.astype(jnp.bfloat16))
            src[...] = jnp.where(first == starts[r], mine, src[...])
            first_src[...] = init

    weight_wide = widen(weight)
    run_cols = run.T
    per_tile = LANES // head_dim
    tile_lane = lax.broadcasted_iota(jnp.int32, (span, LANES), 1) // head_dim
    pieces = []
    for tile in range(heads // per_tile):
        drive_tile = drive_low[:, tile * LANES : (tile + 1) * LANES]
        piece = None
        for j in range(per_tile):
            h = tile * per_tile + j
            gap = jnp.minimum(run_cols[:, h : h + 1] - run[h : h + 1, :], 0.0)
            part = mm((jnp.exp(gap) * scores).astype(jnp.bfloat16), drive_tile)
            piece = part if piece is None else jnp.where(tile_lane == j, part, piece)
        pieces.append(piece)
    inner = pieces[0] if len(pieces) == 1 else jnp.concatenate(pieces, axis=1)
    output = inner + weight_wide * src[...]
    state[...] = mm(basis, drive_last, TN) + weight_wide[span - 1 : span, :] * first_src[...]
    gate = g_ref[...].astype(jnp.float32)
    gated = (output * (gate / (1.0 + jnp.exp(-gate)))).astype(jnp.bfloat16)
    even = place[2] == 0
    mine = jnp.where(even, gated[:tok], gated[tok:])
    other = jnp.where(even, gated[tok:], gated[:tok])
    my_row = lax.rem(pl.program_id(0), 2) == place[1]

    @pl.when(my_row)
    def _():
        same_ref[0] = mine
        core_ref[0] = other

    @pl.when(jnp.logical_not(my_row))
    def _():
        row_ref[0] = mine
        far_ref[0] = other


def scan_heads(head_in, gate_in, in_basis, out_basis, step, rate, init, lengths, place, depth):
    tokens, width = head_in.shape
    heads = step.shape[0]
    requests = lengths.shape[0]
    states = in_basis.shape[1]
    tok = tokens // (4 * depth)
    span = 2 * tok
    ends = jnp.cumsum(lengths)
    starts = (ends - lengths).astype(jnp.int32)
    pad = ((0, 8 - heads), (0, 0))
    prep = jnp.concatenate([jnp.pad(step, pad), jnp.pad(-step * rate[:, None], pad)], axis=0)
    init = init.reshape(requests, width, states)
    cost = pl.CostEstimate(
        flops=2 * tokens * width * (span * 2 + 3 * states),
        bytes_accessed=6 * tokens * width,
        transcendentals=tokens * span * heads,
    )

    def row_block(i, starts, place):
        return (i, 0)

    def out_block(i, starts, place):
        return (lax.rem(place[0] - lax.div(i, 2) + depth, depth), 0, 0)

    return pl.pallas_call(
        functools.partial(scan_kernel, heads=heads, requests=requests),
        out_shape=[jax.ShapeDtypeStruct((depth, tok, width), jnp.bfloat16)] * 4,
        grid_spec=pltpu.PrefetchScalarGridSpec(
            num_scalar_prefetch=2,
            grid=(tokens // span,),
            in_specs=[
                pl.BlockSpec((16, span), lambda i, starts, place: (0, i)),
                pl.BlockSpec((span, width), row_block),
                pl.BlockSpec((span, width), row_block),
                pl.BlockSpec((span, states), row_block),
                pl.BlockSpec((span, states), row_block),
                pl.BlockSpec((requests, width, states), lambda i, starts, place: (0, 0, 0)),
            ],
            out_specs=[pl.BlockSpec((1, tok, width), out_block)] * 4,
            scratch_shapes=[
                pltpu.VMEM((states, width), jnp.float32),
                pltpu.VMEM((span, width), jnp.float32),
                pltpu.VMEM((states, width), jnp.float32),
            ],
        ),
        cost_estimate=cost,
        name="scan",
    )(starts, place, prep, head_in, gate_in, in_basis, out_basis, init)


def project_kernel(*refs, depth, squared):
    acts, weights = refs[:4], refs[4:8]
    outs, squares = refs[8 : 8 + depth], refs[8 + depth :]
    _, tok, width = acts[0].shape
    total = None
    for act, weight in zip(acts, weights):
        part = mm(act[...].reshape(depth * tok, width), weight[...])
        total = part if total is None else total + part
    for dz in range(depth):
        outs[dz][...] = total[dz * tok : (dz + 1) * tok].astype(jnp.bfloat16)
    if squared:

        @pl.when(pl.program_id(0) == 0)
        def _():
            for dz in range(depth):
                wide = [act[dz].astype(jnp.float32) for act in acts]
                summed = sum(jnp.sum(w * w, axis=1, keepdims=True) for w in wide)
                squares[dz][...] = jnp.broadcast_to(summed, (tok, LANES))


def project(acts, weights, half, halves, squared):
    depth, tok, width = acts[0].shape
    model = weights[0].shape[1]
    steps = 2
    columns = model // halves // steps
    cost = pl.CostEstimate(
        flops=8 * depth * tok * width * model // halves,
        bytes_accessed=2 * (4 * width * model + depth * tok * (model + 4 * width)) // halves,
        transcendentals=0,
    )
    out_shape = [jax.ShapeDtypeStruct((tok, columns * steps), jnp.bfloat16)] * depth
    out_specs = [pl.BlockSpec((tok, columns), lambda i: (0, i))] * depth
    if squared:
        out_shape += [jax.ShapeDtypeStruct((tok, LANES), jnp.float32)] * depth
        out_specs += [pl.BlockSpec((tok, LANES), lambda i: (0, 0))] * depth
    out = pl.pallas_call(
        functools.partial(project_kernel, depth=depth, squared=squared),
        out_shape=out_shape,
        grid=(steps,),
        in_specs=[pl.BlockSpec((depth, tok, width), lambda i: (0, 0, 0))] * 4
        + [pl.BlockSpec((width, columns), lambda i: (0, half * steps + i))] * 4,
        out_specs=out_specs,
        cost_estimate=cost,
        name="project",
    )(*acts, *weights)
    return out[:depth], out[depth:]


def expert_kernel(place, *refs, blocks, cap, slots):
    x_refs = refs[:blocks]
    gate_ref, up_ref, down_ref = refs[blocks : blocks + 3]
    outs = refs[blocks + 3 : 2 * blocks + 3]
    rows, total, combine, results = refs[2 * blocks + 3 :]
    expert, part = pl.program_id(0), pl.program_id(1)
    tok, model = outs[0].shape
    count = rows.shape[0]
    wide = count * cap

    @pl.when(jnp.logical_and(expert == 0, part == 0))
    def _():
        here = place[3] * count + lax.broadcasted_iota(jnp.int32, (LANES, wide), 1) // cap
        source = lax.broadcasted_iota(jnp.int32, (LANES, wide), 0)
        pick = jnp.where(jnp.logical_or(source == here, source == here + slots), 1.0, 0.0)
        pick = pick.astype(jnp.bfloat16)
        below = lax.broadcasted_iota(jnp.int32, (tok, tok), 0)
        across = lax.broadcasted_iota(jnp.int32, (tok, tok), 1)
        earlier = jnp.where(across < below, 1.0, 0.0).astype(jnp.bfloat16)
        slot = (lax.broadcasted_iota(jnp.int32, (tok, wide), 1) % cap).astype(jnp.float32)
        for b in range(blocks):
            weight = mm(x_refs[b][:, model : model + LANES], pick)
            chosen = weight > 0.0
            rank = mm(earlier, jnp.where(chosen, 1.0, 0.0).astype(jnp.bfloat16))
            match = jnp.logical_and(chosen, rank == slot)
            select = jnp.where(match, 1.0, 0.0).astype(jnp.bfloat16)
            picked = mm(select, x_refs[b][:, :model], TN).astype(jnp.bfloat16)
            for e in range(count):
                rows[e, b * cap : (b + 1) * cap, :] = picked[e * cap : (e + 1) * cap]
            weight = jnp.where(match, weight, 0.0)
            high = weight.astype(jnp.bfloat16)
            low = (weight - high.astype(jnp.float32)).astype(jnp.bfloat16)
            combine[b] = jnp.concatenate([high, low], axis=1)

    x = rows[expert]
    gate = mm(x, gate_ref[0])
    up = mm(x, up_ref[0])
    act = (gate / (1.0 + jnp.exp(-gate)) * up).astype(jnp.bfloat16)
    down = mm(act, down_ref[0])

    @pl.when(part == 0)
    def _():
        total[...] = down

    @pl.when(part > 0)
    def _():
        total[...] += down

    @pl.when(part == pl.num_programs(1) - 1)
    def _():
        for b in range(blocks):
            value = total[b * cap : (b + 1) * cap, :].astype(jnp.bfloat16)
            results[b, pl.ds(pl.multiple_of(expert * cap, cap), cap), :] = value
            results[b, pl.ds(pl.multiple_of(wide + expert * cap, cap), cap), :] = value

    @pl.when(jnp.logical_and(expert == count - 1, part == pl.num_programs(1) - 1))
    def _():
        for b in range(blocks):
            outs[b][...] = mm(combine[b], results[b]).astype(jnp.bfloat16)


def run_experts(xs, w_gate, w_up, w_down, place, cap, slots, parts):
    blocks = len(xs)
    tok, extended = xs[0].shape
    count, model, hidden = w_gate.shape
    tile = hidden // parts
    cost = pl.CostEstimate(
        flops=6 * count * blocks * cap * model * hidden,
        bytes_accessed=6 * count * model * hidden + 4 * blocks * tok * model,
        transcendentals=count * blocks * cap * hidden,
    )
    return pl.pallas_call(
        functools.partial(expert_kernel, blocks=blocks, cap=cap, slots=slots),
        out_shape=[jax.ShapeDtypeStruct((tok, model), jnp.bfloat16)] * blocks,
        grid_spec=pltpu.PrefetchScalarGridSpec(
            num_scalar_prefetch=1,
            grid=(count, parts),
            in_specs=[pl.BlockSpec((tok, extended), lambda e, f, place: (0, 0))] * blocks
            + [
                pl.BlockSpec((1, model, tile), lambda e, f, place: (e, 0, f)),
                pl.BlockSpec((1, model, tile), lambda e, f, place: (e, 0, f)),
                pl.BlockSpec((1, tile, model), lambda e, f, place: (e, f, 0)),
            ],
            out_specs=[pl.BlockSpec((tok, model), lambda e, f, place: (0, 0))] * blocks,
            scratch_shapes=[
                pltpu.VMEM((count, blocks * cap, model), jnp.bfloat16),
                pltpu.VMEM((blocks * cap, model), jnp.float32),
                pltpu.VMEM((blocks, tok, 2 * count * cap), jnp.bfloat16),
                pltpu.VMEM((blocks, 2 * count * cap, model), jnp.bfloat16),
            ],
        ),
        compiler_params=pltpu.CompilerParams(vmem_limit_bytes=40 * 1024 * 1024),
        cost_estimate=cost,
        name="experts",
    )(place, *xs, w_gate, w_up, w_down)


def add_low(a, b):
    return (a.astype(jnp.float32) + b.astype(jnp.float32)).astype(jnp.bfloat16)


def local(
    resid_in, head_in, gate_in, in_basis, out_basis, step_size, decay_rate, init_state, lengths,
    norm_gain, out_proj, moe_gain, expert_ids, route_weight, placement, w_gate, w_up, w_down,
):
    devices = lax.axis_size("mix")
    depth = devices // 4
    me = lax.axis_index("mix")
    place = jnp.stack([me // 4, (me // 2) % 2, me % 2, me]).astype(jnp.int32)
    tokens = head_in.shape[0]
    tok = tokens // devices
    width = head_in.shape[1]

    def cross(x, mask):
        return lax.ppermute(x, "mix", [(i, i ^ mask) for i in range(devices)])

    def onward(x):
        return lax.ppermute(x, "mix", [(i, (i + 4) % devices) for i in range(devices)])

    gain = lax.dynamic_slice(norm_gain, (me * width,), (width,))
    proj = (out_proj.astype(jnp.float32) * gain[:, None]).astype(jnp.bfloat16)
    proj_y = cross(proj, 2)

    slots = placement.shape[0]
    slot_of = jnp.sum(
        jnp.where(
            expert_ids[:, :, None] == jnp.arange(slots, dtype=jnp.int32), placement[None, None, :], 0
        ),
        axis=2,
    )
    route = jnp.sum(
        jnp.where(
            slot_of[:, :, None] == jnp.arange(slots, dtype=jnp.int32), route_weight[:, :, None], 0.0
        ),
        axis=1,
    )
    route_high = lax.reduce_precision(route, 8, 7)
    table = jnp.concatenate([route_high, route - route_high], axis=1)
    table = jnp.pad(table, ((0, 0), (0, LANES - 2 * slots))).astype(jnp.bfloat16)

    gated = scan_heads(
        head_in, gate_in, in_basis, out_basis, step_size, decay_rate, init_state, lengths,
        place, depth,
    )
    projs = [proj, cross(proj, 1), proj_y, cross(proj_y, 1)]
    acts = [gated[0], cross(gated[1], 1), cross(gated[2], 2), cross(gated[3], 3)]
    halves = 2
    sums = []
    for half in range(halves):
        mixed, squares = project(acts, projs, half, halves, half == 0)
        total = mixed[1]
        if half == 0:
            norm = squares[1]
        for dz in range(2, depth):
            total = add_low(onward(total), mixed[dz])
            if half == 0:
                norm = onward(norm) + squares[dz]
        total = onward(total).astype(jnp.float32) + mixed[0].astype(jnp.float32)
        if half == 0:
            norm = (onward(norm) + squares[0])[:, 0:1]
        sums.append(total)
    mixer_sum = jnp.concatenate(sums, axis=1)
    hidden = resid_in.astype(jnp.float32) + mixer_sum * lax.rsqrt(norm / (devices * width) + epsilon)
    normed = (
        hidden * lax.rsqrt(jnp.mean(hidden * hidden, axis=1, keepdims=True) + epsilon) * moe_gain
    ).astype(jnp.bfloat16)
    mine = jnp.concatenate([normed, table], axis=1)

    cap = 2 * tok * expert_ids.shape[1] // slots
    sums = []
    for dz in range(depth):
        if dz > 0:
            mine = onward(mine)
        other = cross(mine, 2)
        block = [mine, cross(mine, 1), other, cross(other, 1)]
        outs = run_experts(block, w_gate, w_up, w_down, place, cap, slots, 1)
        near = add_low(outs[0], cross(outs[1], 1))
        far = add_low(outs[2], cross(outs[3], 1))
        sums.append(add_low(near, cross(far, 2)))
    total = sums[1]
    for dz in range(2, depth):
        total = add_low(onward(total), sums[dz])
    expert_sum = onward(total).astype(jnp.float32) + sums[0].astype(jnp.float32)
    return (hidden + expert_sum).astype(jnp.bfloat16)


def solution(mesh):
    return jax.shard_map(
        local,
        mesh=mesh,
        in_specs=(
            P(("groups", "mix"), None),
            P("groups", "mix"),
            P("groups", "mix"),
            P("groups", None),
            P("groups", None),
            P("mix", "groups"),
            P("mix"),
            P("groups", "mix", None, None),
            P("groups"),
            P(),
            P("mix", None),
            P(),
            P(("groups", "mix"), None),
            P(("groups", "mix"), None),
            P(),
            P("mix", None, None),
            P("mix", None, None),
            P("mix", None, None),
        ),
        out_specs=P(("groups", "mix"), None),
        check_vma=False,
    )
```

profile of v0, /device:TPU:0, one launch (start us, length us, event | category | flops | bytes accessed | tf_op | source)
XLA Modules:
  0.0 259.8 jit_solution(15362882069760378815)
XLA Ops:
  2.3 3.1 %collective-permute-start.4 = (bf16[256,2048]{1,0:T(8,128)(2,1)S(1)}, bf16[256,2048]{1,0:T(8,128)(2,1)S(1)}, u32[]{:S(2)}, u32[]{:S(2)}) collective-permute-start(bf16[256,2048]{1,0:T(8,128)(2,1)S(1)} %multiply_convert_fusion.refs_4_), channel_id=1, source_target_pairs={{0,2},{1,3},{2,0},{3,1},{4,6},{5,7},{6,4},{7,5},{8,10},{9,11},{10,... | collective-permute-start | bytes 3145736 | tf_op jit(solution)/shard_map/ppermute | solution.py:335
  6.1 22.4 %collective-permute-done.4.refs_6_ = bf16[256,2048]{1,0:T(8,128)(2,1)S(1)} collective-permute-done((bf16[256,2048]{1,0:T(8,128)(2,1)S(1)}, bf16[256,2048]{1,0:T(8,128)(2,1)S(1)}, u32[]{:S(2)}, u32[]{:S(2)}) %collective-permute-start.4) | collective-permute-done | bytes 1048608 | tf_op jit(solution)/shard_map/ppermute | solution.py:335
  30.0 22.7 %scan.1 = (bf16[4,128,256]{2,1,0:T(8,128)(2,1)}, bf16[4,128,256]{2,1,0:T(8,128)(2,1)}, bf16[4,128,256]{2,1,0:T(8,128)(2,1)}, bf16[4,128,256]{2,1,0:T(8,128)(2,1)}) custom-call(s32[8]{0:T(128)} %bitcast_subtract_fusion.starts, s32[4]{0:T(128)} %pad_add_fusion.place, f32[16,2048]{1,0:T(8,128)} %select_maximum_fusion.prep_ref, bf16[2048,256]{1,0:T(8,128)(2,1)} %x_ref.1, ...), custom_call_target="tpu_custom_call" | custom-call | flops 939524096 | bytes 3145728 | tf_op jit(solution)/shard_map/scan/pallas_call | solution.py:147
  55.3 7.4 %collective-permute-done.1.refs_2_ = bf16[4,128,256]{2,1,0:T(8,128)(2,1)} collective-permute-done((bf16[4,128,256]{2,1,0:T(8,128)(2,1)}, bf16[4,128,256]{2,1,0:T(8,128)(2,1)}, u32[]{:S(2)}, u32[]{:S(2)}) %collective-permute-start.1) | collective-permute-done | bytes 262176 | tf_op jit(solution)/shard_map/ppermute | solution.py:335
  62.7 4.0 %collective-permute-done.2.refs_3_ = bf16[4,128,256]{2,1,0:T(8,128)(2,1)} collective-permute-done((bf16[4,128,256]{2,1,0:T(8,128)(2,1)}, bf16[4,128,256]{2,1,0:T(8,128)(2,1)}, u32[]{:S(2)}, u32[]{:S(2)}) %collective-permute-start.2) | collective-permute-done | bytes 262176 | tf_op jit(solution)/shard_map/ppermute | solution.py:335
  67.7 3.8 %project.3 = (bf16[128,1024]{1,0:T(8,128)(2,1)}, bf16[128,1024]{1,0:T(8,128)(2,1)}, bf16[128,1024]{1,0:T(8,128)(2,1)}, bf16[128,1024]{1,0:T(8,128)(2,1)}) custom-call(bf16[4,128,256]{2,1,0:T(8,128)(2,1)} %get-tuple-element.37.refs_0_, bf16[4,128,256]{2,1,0:T(8,128)(2,1)} %copy-done.5, bf16[4,128,256]{2,1,0:T(8,128)(2,1)} %collective-permute-done.1.refs_2_, ...), custom_call_target="tpu_custom_call" | custom-call | flops 1073741824 | bytes 3670016 | tf_op jit(solution)/shard_map/project/pallas_call | solution.py:208
  73.3 4.5 %project.2 = (bf16[128,1024]{1,0:T(8,128)(2,1)}, bf16[128,1024]{1,0:T(8,128)(2,1)}, bf16[128,1024]{1,0:T(8,128)(2,1)}, bf16[128,1024]{1,0:T(8,128)(2,1)}, f32[12...) custom-call(bf16[4,128,256]{2,1,0:T(8,128)(2,1)} %get-tuple-element.37.refs_0_, ...), custom_call_target="tpu_custom_call" | custom-call | flops 1073741824 | bytes 3670016 | tf_op jit(solution)/shard_map/project/pallas_call | solution.py:208
  81.0 3.4 %collective-permute-done.12 = f32[128,128]{1,0:T(8,128)S(1)} collective-permute-done((f32[128,128]{1,0:T(8,128)}, f32[128,128]{1,0:T(8,128)S(1)}, u32[]{:S(2)}, u32[]{:S(2)}) %collective-permute-start.12) | collective-permute-done | bytes 65568 | tf_op jit(solution)/shard_map/ppermute | solution.py:338
  87.2 3.4 %collective-permute-done.6 = bf16[128,1024]{1,0:T(8,128)(2,1)S(1)} collective-permute-done((bf16[128,1024]{1,0:T(8,128)(2,1)}, bf16[128,1024]{1,0:T(8,128)(2,1)S(1)}, u32[]{:S(2)}, u32[]{:S(2)}) %collective-permute-start.6) | collective-permute-done | bytes 262176 | tf_op jit(solution)/shard_map/ppermute | solution.py:338
  93.1 4.6 %collective-permute-done.10 = bf16[128,1024]{1,0:T(8,128)(2,1)S(1)} collective-permute-done((bf16[128,1024]{1,0:T(8,128)(2,1)S(1)}, bf16[128,1024]{1,0:T(8,128)(2,1)S(1)}, u32[]{:S(2)}, u32[]{:S(2)}) %collective-permute-start.10) | collective-permute-done | bytes 262176 | tf_op jit(solution)/shard_map/ppermute | solution.py:338
  97.8 5.5 %collective-permute-done.7 = bf16[128,1024]{1,0:T(8,128)(2,1)S(1)} collective-permute-done((bf16[128,1024]{1,0:T(8,128)(2,1)S(1)}, bf16[128,1024]{1,0:T(8,128)(2,1)S(1)}, u32[]{:S(2)}, u32[]{:S(2)}) %collective-permute-start.7) | collective-permute-done | bytes 262176 | tf_op jit(solution)/shard_map/ppermute | solution.py:338
  104.8 5.5 %collective-permute-done.11 = bf16[128,1024]{1,0:T(8,128)(2,1)S(1)} collective-permute-done((bf16[128,1024]{1,0:T(8,128)(2,1)S(1)}, bf16[128,1024]{1,0:T(8,128)(2,1)S(1)}, u32[]{:S(2)}, u32[]{:S(2)}) %collective-permute-start.11) | collective-permute-done | bytes 262176 | tf_op jit(solution)/shard_map/ppermute | solution.py:338
  110.4 4.8 %collective-permute-done.8 = bf16[128,1024]{1,0:T(8,128)(2,1)S(1)} collective-permute-done((bf16[128,1024]{1,0:T(8,128)(2,1)S(1)}, bf16[128,1024]{1,0:T(8,128)(2,1)S(1)}, u32[]{:S(2)}, u32[]{:S(2)}) %collective-permute-start.8) | collective-permute-done | bytes 262176 | tf_op jit(solution)/shard_map/ppermute | solution.py:338
  116.0 15.7 %collective-permute-done.15.refs_0_ = bf16[128,2176]{1,0:T(8,128)(2,1)S(1)} collective-permute-done((bf16[128,2176]{1,0:T(8,128)(2,1)S(1)}, bf16[128,2176]{1,0:T(8,128)(2,1)S(1)}, u32[]{:S(2)}, u32[]{:S(2)}) %collective-permute-start.15) | collective-permute-done | bytes 557088 | tf_op jit(solution)/shard_map/ppermute | solution.py:338
  133.2 11.5 %collective-permute-done.17.refs_2_ = bf16[128,2176]{1,0:T(8,128)(2,1)S(1)} collective-permute-done((bf16[128,2176]{1,0:T(8,128)(2,1)S(1)}, bf16[128,2176]{1,0:T(8,128)(2,1)S(1)}, u32[]{:S(2)}, u32[]{:S(2)}) %collective-permute-start.17) | collective-permute-done | bytes 557088 | tf_op jit(solution)/shard_map/ppermute | solution.py:335
  148.4 11.5 %experts.4 = (bf16[128,2048]{1,0:T(8,128)(2,1)S(1)}, bf16[128,2048]{1,0:T(8,128)(2,1)S(1)}, bf16[128,2048]{1,0:T(8,128)(2,1)S(1)}, bf16[128,2048]{1,0:T(8,128)(2,1)S(1)}) custom-call(s32[4]{0:T(128)S(1)} %copy-done, bf16[128,2176]{1,0:T(8,128)(2,1)S(1)} %collective-permute-done.15.refs_0_, bf16[128,2176]{1,0:T(8,128)(2,1)S(1)} %collective-permute-done.16.refs_1_, ...), custom_call_target="tpu_custom_call" | custom-call | flops 4831838208 | bytes 23068672 | tf_op jit(solution)/shard_map/experts/pallas_call | solution.py:292
  165.1 11.5 %experts.5 = (bf16[128,2048]{1,0:T(8,128)(2,1)S(1)}, bf16[128,2048]{1,0:T(8,128)(2,1)S(1)}, bf16[128,2048]{1,0:T(8,128)(2,1)S(1)}, bf16[128,2048]{1,0:T(8,128)(2,1)S(1)}) custom-call(s32[4]{0:T(128)S(1)} %copy-done, bf16[128,2176]{1,0:T(8,128)(2,1)S(1)} %collective-permute-done.23.refs_0_, bf16[128,2176]{1,0:T(8,128)(2,1)S(1)} %collective-permute-done.24.refs_1_, ...), custom_call_target="tpu_custom_call" | custom-call | flops 4831838208 | bytes 23068672 | tf_op jit(solution)/shard_map/experts/pallas_call | solution.py:292
  177.3 10.7 %collective-permute-done.33.refs_2_ = bf16[128,2176]{1,0:T(8,128)(2,1)S(1)} collective-permute-done((bf16[128,2176]{1,0:T(8,128)(2,1)S(1)}, bf16[128,2176]{1,0:T(8,128)(2,1)S(1)}, u32[]{:S(2)}, u32[]{:S(2)}) %collective-permute-start.33) | collective-permute-done | bytes 557088 | tf_op jit(solution)/shard_map/ppermute | solution.py:335
  188.0 10.7 %collective-permute-done.21 = bf16[128,2048]{1,0:T(8,128)(2,1)S(1)} collective-permute-done((bf16[128,2048]{1,0:T(8,128)(2,1)S(1)}, bf16[128,2048]{1,0:T(8,128)(2,1)S(1)}, u32[]{:S(2)}, u32[]{:S(2)}) %collective-permute-start.21) | collective-permute-done | bytes 524320 | tf_op jit(solution)/shard_map/ppermute | solution.py:335
  202.1 11.5 %experts.6 = (bf16[128,2048]{1,0:T(8,128)(2,1)S(1)}, bf16[128,2048]{1,0:T(8,128)(2,1)S(1)}, bf16[128,2048]{1,0:T(8,128)(2,1)S(1)}, bf16[128,2048]{1,0:T(8,128)(2,1)S(1)}) custom-call(s32[4]{0:T(128)S(1)} %copy-done, bf16[128,2176]{1,0:T(8,128)(2,1)S(1)} %collective-permute-done.31.refs_0_, bf16[128,2176]{1,0:T(8,128)(2,1)S(1)} %collective-permute-done.32.refs_1_, ...), custom_call_target="tpu_custom_call" | custom-call | flops 4831838208 | bytes 23068672 | tf_op jit(solution)/shard_map/experts/pallas_call | solution.py:292
  213.7 11.5 %experts.7 = (bf16[128,2048]{1,0:T(8,128)(2,1)S(1)}, bf16[128,2048]{1,0:T(8,128)(2,1)S(1)}, bf16[128,2048]{1,0:T(8,128)(2,1)S(1)}, bf16[128,2048]{1,0:T(8,128)(2,1)S(1)}) custom-call(s32[4]{0:T(128)S(1)} %copy-done, bf16[128,2176]{1,0:T(8,128)(2,1)S(1)} %pad_maximum_fusion.refs_0_, bf16[128,2176]{1,0:T(8,128)(2,1)S(1)} %collective-permute-done.39.refs_1_, ...), custom_call_target="tpu_custom_call" | custom-call | flops 4831838208 | bytes 23068672 | tf_op jit(solution)/shard_map/experts/pallas_call | solution.py:292
  228.9 13.7 %collective-permute-done.30 = bf16[128,2048]{1,0:T(8,128)(2,1)S(1)} collective-permute-done((bf16[128,2048]{1,0:T(8,128)(2,1)S(1)}, bf16[128,2048]{1,0:T(8,128)(2,1)S(1)}, u32[]{:S(2)}, u32[]{:S(2)}) %collective-permute-start.30) | collective-permute-done | bytes 524320 | tf_op jit(solution)/shard_map/ppermute | solution.py:338
  245.9 6.1 %collective-permute-done.44 = bf16[128,2048]{1,0:T(8,128)(2,1)S(1)} collective-permute-done((bf16[128,2048]{1,0:T(8,128)(2,1)S(1)}, bf16[128,2048]{1,0:T(8,128)(2,1)S(1)}, u32[]{:S(2)}, u32[]{:S(2)}) %collective-permute-start.44) | collective-permute-done | bytes 524320 | tf_op jit(solution)/shard_map/ppermute | solution.py:335
  252.0 6.5 %collective-permute-done.38 = bf16[128,2048]{1,0:T(8,128)(2,1)S(1)} collective-permute-done((bf16[128,2048]{1,0:T(8,128)(2,1)S(1)}, bf16[128,2048]{1,0:T(8,128)(2,1)S(1)}, u32[]{:S(2)}, u32[]{:S(2)}) %collective-permute-start.38) | collective-permute-done | bytes 524320 | tf_op jit(solution)/shard_map/ppermute | solution.py:338
  (153 shorter events, 43.2 us)
Async XLA Ops:
  2.3 26.2 %collective-permute-start.4 = (bf16[256,2048]{1,0:T(8,128)(2,1)S(1)}, bf16[256,2048]{1,0:T(8,128)(2,1)S(1)}, u32[]{:S(2)}, u32[]{:S(2)}) collective-permute-start(bf16[256,2048]{1,0:T(8,128)(2,1)S(1)} %multiply_convert_fusion.refs_4_), channel_id=1, source_target_pairs={{0,2},{1,3},{2,0},{3,1},{4,6},{5,7},{6,4},{7,5},{8,10},{9,11},{10,... | collective-permute-start | bytes 3145736 | tf_op jit(solution)/shard_map/ppermute | solution.py:335
  5.3 61.4 %collective-permute-start.3 = (bf16[256,2048]{1,0:T(8,128)(2,1)S(1)}, bf16[256,2048]{1,0:T(8,128)(2,1)S(1)}, u32[]{:S(2)}, u32[]{:S(2)}) collective-permute-start(bf16[256,2048]{1,0:T(8,128)(2,1)S(1)} %multiply_convert_fusion.refs_4_), channel_id=1, source_target_pairs={{0,1},{1,0},{2,3},{3,2},{4,5},{5,4},{6,7},{7,6},{8,9},{9,8},{10,11... | collective-permute-start | bytes 3145736 | tf_op jit(solution)/shard_map/ppermute | solution.py:335
  28.5 38.2 %collective-permute-start.5 = (bf16[256,2048]{1,0:T(8,128)(2,1)S(1)}, bf16[256,2048]{1,0:T(8,128)(2,1)}, u32[]{:S(2)}, u32[]{:S(2)}) collective-permute-start(bf16[256,2048]{1,0:T(8,128)(2,1)S(1)} %collective-permute-done.4.refs_6_), channel_id=1, source_target_pairs={{0,1},{1,0},{2,3},{3,2},{4,5},{5,4},{6,7},{7,6},{8,9},{9,8},{10,11... | collective-permute-start | bytes 3145736 | tf_op jit(solution)/shard_map/ppermute | solution.py:335
  71.5 13.8 %collective-permute-start.9 = (bf16[128,1024]{1,0:T(8,128)(2,1)}, bf16[128,1024]{1,0:T(8,128)(2,1)S(1)}, u32[]{:S(2)}, u32[]{:S(2)}) collective-permute-start(bf16[128,1024]{1,0:T(8,128)(2,1)} %get-tuple-element.45), channel_id=1, source_target_pairs={{0,4},{1,5},{2,6},{3,7},{4,8},{5,9},{6,10},{7,11},{8,12},{9,13},{1... | collective-permute-start | bytes 786440 | tf_op jit(solution)/shard_map/ppermute | solution.py:338
  116.0 15.7 %collective-permute-start.15 = (bf16[128,2176]{1,0:T(8,128)(2,1)S(1)}, bf16[128,2176]{1,0:T(8,128)(2,1)S(1)}, u32[]{:S(2)}, u32[]{:S(2)}) collective-permute-start(bf16[128,2176]{1,0:T(8,128)(2,1)S(1)} %pad_maximum_fusion.refs_0_), channel_id=1, source_target_pairs={{0,4},{1,5},{2,6},{3,7},{4,8},{5,9},{6,10},{7,11},{8,12},{9,13},{1... | collective-permute-start | bytes 1671176 | tf_op jit(solution)/shard_map/ppermute | solution.py:338
  131.7 13.0 %collective-permute-start.17 = (bf16[128,2176]{1,0:T(8,128)(2,1)S(1)}, bf16[128,2176]{1,0:T(8,128)(2,1)S(1)}, u32[]{:S(2)}, u32[]{:S(2)}) collective-permute-start(bf16[128,2176]{1,0:T(8,128)(2,1)S(1)} %collective-permute-done.15.refs_0_), channel_id=1, source_target_pairs={{0,2},{1,3},{2,0},{3,1},{4,6},{5,7},{6,4},{7,5},{8,10},{9,11},{10,... | collective-permute-start | bytes 1671176 | tf_op jit(solution)/shard_map/ppermute | solution.py:335
  133.2 14.6 %collective-permute-start.23 = (bf16[128,2176]{1,0:T(8,128)(2,1)S(1)}, bf16[128,2176]{1,0:T(8,128)(2,1)S(1)}, u32[]{:S(2)}, u32[]{:S(2)}) collective-permute-start(bf16[128,2176]{1,0:T(8,128)(2,1)S(1)} %collective-permute-done.15.refs_0_), channel_id=1, source_target_pairs={{0,4},{1,5},{2,6},{3,7},{4,8},{5,9},{6,10},{7,11},{8,12},{9,13},{1... | collective-permute-start | bytes 1671176 | tf_op jit(solution)/shard_map/ppermute | solution.py:338
  133.2 15.1 %collective-permute-start.16 = (bf16[128,2176]{1,0:T(8,128)(2,1)S(1)}, bf16[128,2176]{1,0:T(8,128)(2,1)S(1)}, u32[]{:S(2)}, u32[]{:S(2)}) collective-permute-start(bf16[128,2176]{1,0:T(8,128)(2,1)S(1)} %collective-permute-done.15.refs_0_), channel_id=1, source_target_pairs={{0,1},{1,0},{2,3},{3,2},{4,5},{5,4},{6,7},{7,6},{8,9},{9,8},{10,11... | collective-permute-start | bytes 1671176 | tf_op jit(solution)/shard_map/ppermute | solution.py:335
  148.3 14.5 %collective-permute-start.31 = (bf16[128,2176]{1,0:T(8,128)(2,1)S(1)}, bf16[128,2176]{1,0:T(8,128)(2,1)S(1)}, u32[]{:S(2)}, u32[]{:S(2)}) collective-permute-start(bf16[128,2176]{1,0:T(8,128)(2,1)S(1)} %collective-permute-done.23.refs_0_), channel_id=1, source_target_pairs={{0,4},{1,5},{2,6},{3,7},{4,8},{5,9},{6,10},{7,11},{8,12},{9,13},{1... | collective-permute-start | bytes 1671176 | tf_op jit(solution)/shard_map/ppermute | solution.py:338
  160.5 16.1 %collective-permute-start.40 = (bf16[128,2176]{1,0:T(8,128)(2,1)S(1)}, bf16[128,2176]{1,0:T(8,128)(2,1)S(1)}, u32[]{:S(2)}, u32[]{:S(2)}) collective-permute-start(bf16[128,2176]{1,0:T(8,128)(2,1)S(1)} %pad_maximum_fusion.refs_0_), channel_id=1, source_target_pairs={{0,2},{1,3},{2,0},{3,1},{4,6},{5,7},{6,4},{7,5},{8,10},{9,11},{10,... | collective-permute-start | bytes 1671176 | tf_op jit(solution)/shard_map/ppermute | solution.py:335
  162.8 14.3 %collective-permute-start.19 = (bf16[128,2048]{1,0:T(8,128)(2,1)S(1)}, bf16[128,2048]{1,0:T(8,128)(2,1)S(1)}, u32[]{:S(2)}, u32[]{:S(2)}) collective-permute-start(bf16[128,2048]{1,0:T(8,128)(2,1)S(1)} %get-tuple-element.54), channel_id=1, source_target_pairs={{0,1},{1,0},{2,3},{3,2},{4,5},{5,4},{6,7},{7,6},{8,9},{9,8},{10,11... | collective-permute-start | bytes 1572872 | tf_op jit(solution)/shard_map/ppermute | solution.py:335
  162.8 25.1 %collective-permute-start.33 = (bf16[128,2176]{1,0:T(8,128)(2,1)S(1)}, bf16[128,2176]{1,0:T(8,128)(2,1)S(1)}, u32[]{:S(2)}, u32[]{:S(2)}) collective-permute-start(bf16[128,2176]{1,0:T(8,128)(2,1)S(1)} %collective-permute-done.31.refs_0_), channel_id=1, source_target_pairs={{0,2},{1,3},{2,0},{3,1},{4,6},{5,7},{6,4},{7,5},{8,10},{9,11},{10,... | collective-permute-start | bytes 1671176 | tf_op jit(solution)/shard_map/ppermute | solution.py:335
  163.5 35.2 %collective-permute-start.21 = (bf16[128,2048]{1,0:T(8,128)(2,1)S(1)}, bf16[128,2048]{1,0:T(8,128)(2,1)S(1)}, u32[]{:S(2)}, u32[]{:S(2)}) collective-permute-start(bf16[128,2048]{1,0:T(8,128)(2,1)S(1)} %add_convert_fusion.13), channel_id=1, source_target_pairs={{0,2},{1,3},{2,0},{3,1},{4,6},{5,7},{6,4},{7,5},{8,10},{9,11},{10,... | collective-permute-start | bytes 1572872 | tf_op jit(solution)/shard_map/ppermute | solution.py:335
  176.6 22.3 %collective-permute-start.28 = (bf16[128,2048]{1,0:T(8,128)(2,1)S(1)}, bf16[128,2048]{1,0:T(8,128)(2,1)S(1)}, u32[]{:S(2)}, u32[]{:S(2)}) collective-permute-start(bf16[128,2048]{1,0:T(8,128)(2,1)S(1)} %get-tuple-element.60), channel_id=1, source_target_pairs={{0,1},{1,0},{2,3},{3,2},{4,5},{5,4},{6,7},{7,6},{8,9},{9,8},{10,11... | collective-permute-start | bytes 1572872 | tf_op jit(solution)/shard_map/ppermute | solution.py:335
  176.7 37.0 %collective-permute-start.39 = (bf16[128,2176]{1,0:T(8,128)(2,1)S(1)}, bf16[128,2176]{1,0:T(8,128)(2,1)S(1)}, u32[]{:S(2)}, u32[]{:S(2)}) collective-permute-start(bf16[128,2176]{1,0:T(8,128)(2,1)S(1)} %pad_maximum_fusion.refs_0_), channel_id=1, source_target_pairs={{0,1},{1,0},{2,3},{3,2},{4,5},{5,4},{6,7},{7,6},{8,9},{9,8},{10,11... | collective-permute-start | bytes 1671176 | tf_op jit(solution)/shard_map/ppermute | solution.py:335
  177.2 36.6 %collective-permute-start.41 = (bf16[128,2176]{1,0:T(8,128)(2,1)S(1)}, bf16[128,2176]{1,0:T(8,128)(2,1)S(1)}, u32[]{:S(2)}, u32[]{:S(2)}) collective-permute-start(bf16[128,2176]{1,0:T(8,128)(2,1)S(1)} %collective-permute-done.40.refs_2_), channel_id=1, source_target_pairs={{0,1},{1,0},{2,3},{3,2},{4,5},{5,4},{6,7},{7,6},{8,9},{9,8},{10,11... | collective-permute-start | bytes 1671176 | tf_op jit(solution)/shard_map/ppermute | solution.py:335
  198.9 26.9 %collective-permute-start.27 = (bf16[128,2048]{1,0:T(8,128)(2,1)S(1)}, bf16[128,2048]{1,0:T(8,128)(2,1)S(1)}, u32[]{:S(2)}, u32[]{:S(2)}) collective-permute-start(bf16[128,2048]{1,0:T(8,128)(2,1)S(1)} %get-tuple-element.58), channel_id=1, source_target_pairs={{0,1},{1,0},{2,3},{3,2},{4,5},{5,4},{6,7},{7,6},{8,9},{9,8},{10,11... | collective-permute-start | bytes 1572872 | tf_op jit(solution)/shard_map/ppermute | solution.py:335
  199.6 26.2 %collective-permute-start.22 = (bf16[128,2048]{1,0:T(8,128)(2,1)S(1)}, bf16[128,2048]{1,0:T(8,128)(2,1)S(1)}, u32[]{:S(2)}, u32[]{:S(2)}) collective-permute-start(bf16[128,2048]{1,0:T(8,128)(2,1)S(1)} %add_convert_fusion.12), channel_id=1, source_target_pairs={{0,4},{1,5},{2,6},{3,7},{4,8},{5,9},{6,10},{7,11},{8,12},{9,13},{1... | collective-permute-start | bytes 1572872 | tf_op jit(solution)/shard_map/ppermute | solution.py:338
  200.6 25.3 %collective-permute-start.29 = (bf16[128,2048]{1,0:T(8,128)(2,1)S(1)}, bf16[128,2048]{1,0:T(8,128)(2,1)S(1)}, u32[]{:S(2)}, u32[]{:S(2)}) collective-permute-start(bf16[128,2048]{1,0:T(8,128)(2,1)S(1)} %add_convert_fusion.10), channel_id=1, source_target_pairs={{0,2},{1,3},{2,0},{3,1},{4,6},{5,7},{6,4},{7,5},{8,10},{9,11},{10,... | collective-permute-start | bytes 1572872 | tf_op jit(solution)/shard_map/ppermute | solution.py:335
  226.2 16.4 %collective-permute-start.30 = (bf16[128,2048]{1,0:T(8,128)(2,1)S(1)}, bf16[128,2048]{1,0:T(8,128)(2,1)S(1)}, u32[]{:S(2)}, u32[]{:S(2)}) collective-permute-start(bf16[128,2048]{1,0:T(8,128)(2,1)S(1)} %add_convert_fusion.8), channel_id=1, source_target_pairs={{0,4},{1,5},{2,6},{3,7},{4,8},{5,9},{6,10},{7,11},{8,12},{9,13},{1... | collective-permute-start | bytes 1572872 | tf_op jit(solution)/shard_map/ppermute | solution.py:338
  226.5 16.2 %collective-permute-start.37 = (bf16[128,2048]{1,0:T(8,128)(2,1)S(1)}, bf16[128,2048]{1,0:T(8,128)(2,1)S(1)}, u32[]{:S(2)}, u32[]{:S(2)}) collective-permute-start(bf16[128,2048]{1,0:T(8,128)(2,1)S(1)} %add_convert_fusion.6), channel_id=1, source_target_pairs={{0,2},{1,3},{2,0},{3,1},{4,6},{5,7},{6,4},{7,5},{8,10},{9,11},{10,... | collective-permute-start | bytes 1572872 | tf_op jit(solution)/shard_map/ppermute | solution.py:335
  227.0 18.9 %collective-permute-start.42 = (bf16[128,2048]{1,0:T(8,128)(2,1)S(1)}, bf16[128,2048]{1,0:T(8,128)(2,1)S(1)}, u32[]{:S(2)}, u32[]{:S(2)}) collective-permute-start(bf16[128,2048]{1,0:T(8,128)(2,1)S(1)} %get-tuple-element.66), channel_id=1, source_target_pairs={{0,1},{1,0},{2,3},{3,2},{4,5},{5,4},{6,7},{7,6},{8,9},{9,8},{10,11... | collective-permute-start | bytes 1572872 | tf_op jit(solution)/shard_map/ppermute | solution.py:335
  227.5 24.5 %collective-permute-start.44 = (bf16[128,2048]{1,0:T(8,128)(2,1)S(1)}, bf16[128,2048]{1,0:T(8,128)(2,1)S(1)}, u32[]{:S(2)}, u32[]{:S(2)}) collective-permute-start(bf16[128,2048]{1,0:T(8,128)(2,1)S(1)} %add_convert_fusion.2), channel_id=1, source_target_pairs={{0,2},{1,3},{2,0},{3,1},{4,6},{5,7},{6,4},{7,5},{8,10},{9,11},{10,... | collective-permute-start | bytes 1572872 | tf_op jit(solution)/shard_map/ppermute | solution.py:335
  243.0 15.5 %collective-permute-start.38 = (bf16[128,2048]{1,0:T(8,128)(2,1)S(1)}, bf16[128,2048]{1,0:T(8,128)(2,1)S(1)}, u32[]{:S(2)}, u32[]{:S(2)}) collective-permute-start(bf16[128,2048]{1,0:T(8,128)(2,1)S(1)} %add_convert_fusion.4), channel_id=1, source_target_pairs={{0,4},{1,5},{2,6},{3,7},{4,8},{5,9},{6,10},{7,11},{8,12},{9,13},{1... | collective-permute-start | bytes 1572872 | tf_op jit(solution)/shard_map/ppermute | solution.py:338
  (43 other events, 751.3 us)
where the time goes:
time: 260 us
  waiting for transfers between devices  142 us (55%)
  Pallas kernels  77 us (30%)
  starting transfers between devices  28.4 us (11%)
  other arithmetic  9.6 us (4%)
    ppermute x30, waiting for transfers between devices, cross(): return lax.ppermute(x, 'mix', [(i, i ^ mask) for i in range(devices)])  73.7 us
    ppermute x15, waiting for transfers between devices, onward(): lax.ppermute(x, 'mix', [(i, (i + 4) % devices) for i in range(devices)])  68.4 us
    pallas_call x4, Pallas kernels, run_experts(): pl.pallas_call(functools.partial(expert_kernel, blocks=blocks, cap=cap, s...  46 us
    pallas_call x1, Pallas kernels, scan_heads(): pl.pallas_call(functools.partial(scan_kernel, heads=heads, requests=reque...  22.7 us
    ppermute x30, starting transfers between devices, cross(): return lax.ppermute(x, 'mix', [(i, i ^ mask) for i in range(devices)])  17.2 us
    ppermute x15, starting transfers between devices, onward(): lax.ppermute(x, 'mix', [(i, (i + 4) % devices) for i in range(devices)])  11.3 us
    pallas_call x2, Pallas kernels, project(): pl.pallas_call(functools.partial(project_kernel, depth=depth, squared=squ...  8.34 us
  transfers between devices with their start and end apart: 45, of which 22 were waited for; matrix products, arithmetic and copies ran while one was open for 2% of the time, Pallas kernels for 28%

commit v1 on v0

--- a/solution.py
+++ b/solution.py
@@ -21,11 +21,11 @@
 
 
 def scan_kernel(
-    starts, place, prep_ref, x_ref, g_ref, b_ref, c_ref, init_ref, same_ref, core_ref, row_ref, far_ref,
-    state, src, first_src, *, heads, requests
+    starts, place, prep_ref, x_ref, g_ref, b_ref, c_ref, init_ref, *refs, heads, requests
 ):
+    out_refs, (state, src, first_src) = refs[:8], refs[8:]
     span, width = x_ref.shape
-    tok = same_ref.shape[1]
+    tok = out_refs[0].shape[1]
     head_dim = width // heads
     c0 = pl.program_id(0) * span
     steps = prep_ref[0:8, :]
@@ -104,20 +104,16 @@
     state[...] = mm(basis, drive_last, TN) + weight_wide[span - 1 : span, :] * first_src[...]
     gate = g_ref[...].astype(jnp.float32)
     gated = (output * (gate / (1.0 + jnp.exp(-gate)))).astype(jnp.bfloat16)
-    even = place[2] == 0
+    even = lax.rem(place[0], 2) == 0
     mine = jnp.where(even, gated[:tok], gated[tok:])
     other = jnp.where(even, gated[tok:], gated[:tok])
-    my_row = lax.rem(pl.program_id(0), 2) == place[1]
-
-    @pl.when(my_row)
-    def _():
-        same_ref[0] = mine
-        core_ref[0] = other
-
-    @pl.when(jnp.logical_not(my_row))
-    def _():
-        row_ref[0] = mine
-        far_ref[0] = other
+    pair = lax.rem(pl.program_id(0), 4) ^ lax.div(lax.rem(place[0], 8), 2)
+    for way in range(4):
+
+        @pl.when(pair == way)
+        def _(way=way):
+            out_refs[2 * way][0] = mine
+            out_refs[2 * way + 1][0] = other
 
 
 def scan_heads(head_in, gate_in, in_basis, out_basis, step, rate, init, lengths, place, depth):
@@ -125,7 +121,7 @@
     heads = step.shape[0]
     requests = lengths.shape[0]
     states = in_basis.shape[1]
-    tok = tokens // (4 * depth)
+    tok = tokens // (8 * depth)
     span = 2 * tok
     ends = jnp.cumsum(lengths)
     starts = (ends - lengths).astype(jnp.int32)
@@ -142,11 +138,11 @@
         return (i, 0)
 
     def out_block(i, starts, place):
-        return (lax.rem(place[0] - lax.div(i, 2) + depth, depth), 0, 0)
+        return (lax.rem(lax.div(place[0], 8) - lax.div(i, 4) + depth, depth), 0, 0)
 
     return pl.pallas_call(
         functools.partial(scan_kernel, heads=heads, requests=requests),
-        out_shape=[jax.ShapeDtypeStruct((depth, tok, width), jnp.bfloat16)] * 4,
+        out_shape=[jax.ShapeDtypeStruct((depth, tok, width), jnp.bfloat16)] * 8,
         grid_spec=pltpu.PrefetchScalarGridSpec(
             num_scalar_prefetch=2,
             grid=(tokens // span,),
@@ -158,7 +154,7 @@
                 pl.BlockSpec((span, states), row_block),
                 pl.BlockSpec((requests, width, states), lambda i, starts, place: (0, 0, 0)),
             ],
-            out_specs=[pl.BlockSpec((1, tok, width), out_block)] * 4,
+            out_specs=[pl.BlockSpec((1, tok, width), out_block)] * 8,
             scratch_shapes=[
                 pltpu.VMEM((states, width), jnp.float32),
                 pltpu.VMEM((span, width), jnp.float32),
@@ -171,12 +167,19 @@
 
 
 def project_kernel(*refs, depth, squared):
-    acts, weights = refs[:4], refs[4:8]
-    outs, squares = refs[8 : 8 + depth], refs[8 + depth :]
+    gain_ref, acts, refs = refs[0], refs[1:9], refs[9:]
+    weights, refs = refs[:10], refs[10:]
+    outs, squares = refs[:depth], refs[depth:]
     _, tok, width = acts[0].shape
     total = None
-    for act, weight in zip(acts, weights):
-        part = mm(act[...].reshape(depth * tok, width), weight[...])
+    for mask, act in enumerate(acts):
+        rows = act[...].reshape(depth * tok, width).astype(jnp.float32)
+        rows = (rows * gain_ref[mask : mask + 1, :]).astype(jnp.bfloat16)
+        if mask < 6:
+            part = mm(rows, weights[mask][...])
+        else:
+            halves = weights[6 + mask % 2], weights[8 + mask % 2]
+            part = mm(rows, jnp.concatenate([h[...] for h in halves], axis=0))
         total = part if total is None else total + part
     for dz in range(depth):
         outs[dz][...] = total[dz * tok : (dz + 1) * tok].astype(jnp.bfloat16)
@@ -190,14 +193,14 @@
                 squares[dz][...] = jnp.broadcast_to(summed, (tok, LANES))
 
 
-def project(acts, weights, half, halves, squared):
+def project(gains, acts, weights, half, halves, squared):
     depth, tok, width = acts[0].shape
     model = weights[0].shape[1]
     steps = 2
     columns = model // halves // steps
     cost = pl.CostEstimate(
-        flops=8 * depth * tok * width * model // halves,
-        bytes_accessed=2 * (4 * width * model + depth * tok * (model + 4 * width)) // halves,
+        flops=16 * depth * tok * width * model // halves,
+        bytes_accessed=2 * (8 * width * model + depth * tok * (model + 8 * width)) // halves,
         transcendentals=0,
     )
     out_shape = [jax.ShapeDtypeStruct((tok, columns * steps), jnp.bfloat16)] * depth
@@ -209,12 +212,13 @@
         functools.partial(project_kernel, depth=depth, squared=squared),
         out_shape=out_shape,
         grid=(steps,),
-        in_specs=[pl.BlockSpec((depth, tok, width), lambda i: (0, 0, 0))] * 4
-        + [pl.BlockSpec((width, columns), lambda i: (0, half * steps + i))] * 4,
+        in_specs=[pl.BlockSpec((8, width), lambda i: (0, 0))]
+        + [pl.BlockSpec((depth, tok, width), lambda i: (0, 0, 0))] * 8
+        + [pl.BlockSpec((w.shape[0], columns), lambda i: (0, half * steps + i)) for w in weights],
         out_specs=out_specs,
         cost_estimate=cost,
         name="project",
-    )(*acts, *weights)
+    )(gains, *acts, *weights)
     return out[:depth], out[depth:]
 
 
@@ -230,7 +234,7 @@
 
     @pl.when(jnp.logical_and(expert == 0, part == 0))
     def _():
-        here = place[3] * count + lax.broadcasted_iota(jnp.int32, (LANES, wide), 1) // cap
+        here = place[0] * count + lax.broadcasted_iota(jnp.int32, (LANES, wide), 1) // cap
         source = lax.broadcasted_iota(jnp.int32, (LANES, wide), 0)
         pick = jnp.where(jnp.logical_or(source == here, source == here + slots), 1.0, 0.0)
         pick = pick.astype(jnp.bfloat16)
@@ -326,7 +330,7 @@
     devices = lax.axis_size("mix")
     depth = devices // 4
     me = lax.axis_index("mix")
-    place = jnp.stack([me // 4, (me // 2) % 2, me % 2, me]).astype(jnp.int32)
+    place = me.astype(jnp.int32)[None]
     tokens = head_in.shape[0]
     tok = tokens // devices
     width = head_in.shape[1]
@@ -334,12 +338,12 @@
     def cross(x, mask):
         return lax.ppermute(x, "mix", [(i, i ^ mask) for i in range(devices)])
 
-    def onward(x):
-        return lax.ppermute(x, "mix", [(i, (i + 4) % devices) for i in range(devices)])
-
-    gain = lax.dynamic_slice(norm_gain, (me * width,), (width,))
-    proj = (out_proj.astype(jnp.float32) * gain[:, None]).astype(jnp.bfloat16)
-    proj_y = cross(proj, 2)
+    def onward(x, stride=4):
+        return lax.ppermute(x, "mix", [(i, (i + stride) % devices) for i in range(devices)])
+
+    proj_y, proj_z = cross(out_proj, 2), cross(out_proj, 4)
+    proj_yz = (cross(proj_y[: width // 2], 4), cross(proj_z[width // 2 :], 2))
+    gains = jnp.take(norm_gain.reshape(devices, width), me ^ jnp.arange(8), axis=0)
 
     slots = placement.shape[0]
     slot_of = jnp.sum(
@@ -360,24 +364,26 @@
 
     gated = scan_heads(
         head_in, gate_in, in_basis, out_basis, step_size, decay_rate, init_state, lengths,
-        place, depth,
-    )
-    projs = [proj, cross(proj, 1), proj_y, cross(proj_y, 1)]
-    acts = [gated[0], cross(gated[1], 1), cross(gated[2], 2), cross(gated[3], 3)]
+        place, depth // 2,
+    )
+    projs = []
+    for block in (out_proj, proj_y, proj_z, *proj_yz):
+        projs += [block, cross(block, 1)]
+    acts = [gated[0]] + [cross(gated[mask], mask) for mask in range(1, 8)]
     halves = 2
     sums = []
     for half in range(halves):
-        mixed, squares = project(acts, projs, half, halves, half == 0)
+        mixed, squares = project(gains, acts, projs, half, halves, half == 0)
         total = mixed[1]
         if half == 0:
             norm = squares[1]
-        for dz in range(2, depth):
-            total = add_low(onward(total), mixed[dz])
+        for dz in range(2, depth // 2):
+            total = add_low(onward(total, 8), mixed[dz])
             if half == 0:
-                norm = onward(norm) + squares[dz]
-        total = onward(total).astype(jnp.float32) + mixed[0].astype(jnp.float32)
+                norm = onward(norm, 8) + squares[dz]
+        total = onward(total, 8).astype(jnp.float32) + mixed[0].astype(jnp.float32)
         if half == 0:
-            norm = (onward(norm) + squares[0])[:, 0:1]
+            norm = (onward(norm, 8) + squares[0])[:, 0:1]
         sums.append(total)
     mixer_sum = jnp.concatenate(sums, axis=1)
     hidden = resid_in.astype(jnp.float32) + mixer_sum * lax.rsqrt(norm / (devices * width) + epsilon)
@@ -391,7 +397,7 @@
     for dz in range(depth):
         if dz > 0:
             mine = onward(mine)
-        other = cross(mine, 2)
+        other = cross(mine, 2) if dz < depth - 1 else onward(other)
         block = [mine, cross(mine, 1), other, cross(other, 1)]
         outs = run_experts(block, w_gate, w_up, w_down, place, cap, slots, 1)
         near = add_low(outs[0], cross(outs[1], 1))

time: 260 us -> 237 us (0.912)
  waiting for transfers between devices: 142 us -> 106 us
  local copies, waits for them, and re-layouts: 2.03 us -> 9.21 us
  other arithmetic: 9.6 us -> 14.7 us
    ppermute x30 -> x39, waiting for transfers between devices: 73.7 us -> 36.4 us  [cross(): return lax.ppermute(x, 'mix', [(i, i ^ mask) for i in range(devices)])]
    ppermute x30 -> x39, starting transfers between devices: 17.2 us -> 23.5 us  [cross(): return lax.ppermute(x, 'mix', [(i, i ^ mask) for i in range(devices)])]
    ppermute x15 -> x10, starting transfers between devices: 11.3 us -> 6.59 us  [onward(): lax.ppermute(x, 'mix', [(i, (i + stride) % devices) for i in range(device...]
    ppermute x15 -> x10, waiting for transfers between devices: 68.4 us -> 69.2 us  [onward(): lax.ppermute(x, 'mix', [(i, (i + stride) % devices) for i in range(device...]
  transfers between devices with their start and end apart: 45 -> 49, of which waited for: 22 -> 19; matrix products, arithmetic and copies ran while one was open for 2% -> 7% of each run, Pallas kernels for 28% -> 30%
where the time goes in v1:
time: 237 us
  waiting for transfers between devices  106 us (45%)
  Pallas kernels  76.5 us (32%)
  starting transfers between devices  30.1 us (13%)
  other arithmetic  14.7 us (6%)
  local copies, waits for them, and re-layouts  9.21 us (4%)
    ppermute x10, waiting for transfers between devices, onward(): lax.ppermute(x, 'mix', [(i, (i + stride) % devices) for i in range(device...  69.2 us
    pallas_call x4, Pallas kernels, run_experts(): pl.pallas_call(functools.partial(expert_kernel, blocks=blocks, cap=cap, s...  44.1 us
    ppermute x39, waiting for transfers between devices, cross(): return lax.ppermute(x, 'mix', [(i, i ^ mask) for i in range(devices)])  36.4 us
    ppermute x39, starting transfers between devices, cross(): return lax.ppermute(x, 'mix', [(i, i ^ mask) for i in range(devices)])  23.5 us
    pallas_call x1, Pallas kernels, scan_heads(): pl.pallas_call(functools.partial(scan_kernel, heads=heads, requests=reque...  23.2 us
    pallas_call x2, Pallas kernels, project(): pl.pallas_call(functools.partial(project_kernel, depth=depth, squared=squ...  9.17 us
    ppermute x10, starting transfers between devices, onward(): lax.ppermute(x, 'mix', [(i, (i + stride) % devices) for i in range(device...  6.59 us
  transfers between devices with their start and end apart: 49, of which 19 were waited for; matrix products, arithmetic and copies ran while one was open for 7% of the time, Pallas kernels for 30%

profile of v1, /device:TPU:0, one launch (start us, length us, event | category | flops | bytes accessed | tf_op | source)
XLA Modules:
  0.0 236.6 jit_solution(7561051846645920135)
XLA Ops:
  0.0 3.1 %collective-permute-start.8 = (bf16[256,2048]{1,0:T(8,128)(2,1)}, bf16[256,2048]{1,0:T(8,128)(2,1)S(1)}, u32[]{:S(2)}, u32[]{:S(2)}) collective-permute-start(bf16[256,2048]{1,0:T(8,128)(2,1)} %refs_9_.3), channel_id=1, source_target_pairs={{0,2},{1,3},{2,0},{3,1},{4,6},{5,7},{6,4},{7,5},{8,10},{9,11},{10,... | collective-permute-start | bytes 3145736 | tf_op jit(solution)/shard_map/ppermute | solution.py:339
  8.9 23.2 %scan.1 = (bf16[2,128,256]{2,1,0:T(8,128)(2,1)}, bf16[2,128,256]{2,1,0:T(8,128)(2,1)}, bf16[2,128,256]{2,1,0:T(8,128)(2,1)}, bf16[2,128,256]{2,1,0:T(8,128)(2,1)...) custom-call(s32[8]{0:T(128)} %bitcast_subtract_fusion.starts, ...), custom_call_target="tpu_custom_call" | custom-call | flops 939524096 | bytes 3145728 | tf_op jit(solution)/shard_map/scan/pallas_call | solution.py:143
  34.5 4.4 %collective-permute-done.1.refs_3_ = bf16[2,128,256]{2,1,0:T(8,128)(2,1)S(1)} collective-permute-done((bf16[2,128,256]{2,1,0:T(8,128)(2,1)}, bf16[2,128,256]{2,1,0:T(8,128)(2,1)S(1)}, u32[]{:S(2)}, u32[]{:S(2)}) %collective-permute-start.1) | collective-permute-done | bytes 131104 | tf_op jit(solution)/shard_map/ppermute | solution.py:339
  47.1 3.0 %collective-permute-done.6.refs_8_ = bf16[2,128,256]{2,1,0:T(8,128)(2,1)S(1)} collective-permute-done((bf16[2,128,256]{2,1,0:T(8,128)(2,1)}, bf16[2,128,256]{2,1,0:T(8,128)(2,1)S(1)}, u32[]{:S(2)}, u32[]{:S(2)}) %collective-permute-start.6) | collective-permute-done | bytes 131104 | tf_op jit(solution)/shard_map/ppermute | solution.py:339
  56.8 3.5 %collective-permute-done.12.refs_15_ = bf16[128,2048]{1,0:T(8,128)(2,1)} collective-permute-done((bf16[128,2048]{1,0:T(8,128)(2,1)}, bf16[128,2048]{1,0:T(8,128)(2,1)}, u32[]{:S(2)}, u32[]{:S(2)}) %collective-permute-start.12) | collective-permute-done | bytes 524320 | tf_op jit(solution)/shard_map/ppermute | solution.py:339
  64.1 4.4 %project.3 = (bf16[128,1024]{1,0:T(8,128)(2,1)}, bf16[128,1024]{1,0:T(8,128)(2,1)}) custom-call(f32[8,256]{1,0:T(8,128)} %broadcast_select_fusion.refs_0_, bf16[2,128,256]{2,1,0:T(8,128)(2,1)} %get-tuple-element.35.refs_1_, bf16[2,128,256]{2,1,0:T(8,128)(2,1)} %copy-done.6, bf16[2,128,256]{2,1,0:T(8,128)(2,1)} %copy-done.7, bf16[2,128,256]{2,1,0:T(8,128)(2,1)} %copy-done.8, ...), custom_call_target="tpu_custom_call" | custom-call | flops 1073741824 | bytes 5242880 | tf_op jit(solution)/shard_map/project/pallas_call | solution.py:211
  68.5 2.6 %collective-permute-start.17 = (bf16[128,1024]{1,0:T(8,128)(2,1)}, bf16[128,1024]{1,0:T(8,128)(2,1)S(1)}, u32[]{:S(2)}, u32[]{:S(2)}) collective-permute-start(bf16[128,1024]{1,0:T(8,128)(2,1)} %get-tuple-element.45), channel_id=1, source_target_pairs={{0,8},{1,9},{2,10},{3,11},{4,12},{5,13},{6,14},{7,15},{8,0},{9,1},... | collective-permute-start | bytes 786440 | tf_op jit(solution)/shard_map/ppermute | solution.py:342
  71.2 4.8 %project.2 = (bf16[128,1024]{1,0:T(8,128)(2,1)}, bf16[128,1024]{1,0:T(8,128)(2,1)}, f32[128,128]{1,0:T(8,128)}, f32[128,128]{1,0:T(8,128)}) custom-call(f32[8,256]{1,0:T(8,128)} %broadcast_select_fusion.refs_0_, bf16[2,128,256]{2,1,0:T(8,128)(2,1)} %get-tuple-element.35.refs_1_, bf16[2,128,256]{2,1,0:T(8,128)(2,1)} %copy-done.6, ...), custom_call_target="tpu_custom_call" | custom-call | flops 1073741824 | bytes 5242880 | tf_op jit(solution)/shard_map/project/pallas_call | solution.py:211
  76.5 2.6 %collective-permute-start.16 = (bf16[128,1024]{1,0:T(8,128)(2,1)}, bf16[128,1024]{1,0:T(8,128)(2,1)S(1)}, u32[]{:S(2)}, u32[]{:S(2)}) collective-permute-start(bf16[128,1024]{1,0:T(8,128)(2,1)} %get-tuple-element.43), channel_id=1, source_target_pairs={{0,8},{1,9},{2,10},{3,11},{4,12},{5,13},{6,14},{7,15},{8,0},{9,1},... | collective-permute-start | bytes 786440 | tf_op jit(solution)/shard_map/ppermute | solution.py:342
  79.1 13.8 %collective-permute-done.18 = f32[128,128]{1,0:T(8,128)S(1)} collective-permute-done((f32[128,128]{1,0:T(8,128)}, f32[128,128]{1,0:T(8,128)S(1)}, u32[]{:S(2)}, u32[]{:S(2)}) %collective-permute-start.18) | collective-permute-done | bytes 65568 | tf_op jit(solution)/shard_map/ppermute | solution.py:342
  94.0 4.1 %collective-permute-done.16 = bf16[128,1024]{1,0:T(8,128)(2,1)S(1)} collective-permute-done((bf16[128,1024]{1,0:T(8,128)(2,1)}, bf16[128,1024]{1,0:T(8,128)(2,1)S(1)}, u32[]{:S(2)}, u32[]{:S(2)}) %collective-permute-start.16) | collective-permute-done | bytes 262176 | tf_op jit(solution)/shard_map/ppermute | solution.py:342
  100.4 15.5 %collective-permute-done.19.refs_0_ = bf16[128,2176]{1,0:T(8,128)(2,1)S(1)} collective-permute-done((bf16[128,2176]{1,0:T(8,128)(2,1)S(1)}, bf16[128,2176]{1,0:T(8,128)(2,1)S(1)}, u32[]{:S(2)}, u32[]{:S(2)}) %collective-permute-start.19) | collective-permute-done | bytes 557088 | tf_op jit(solution)/shard_map/ppermute | solution.py:342
  117.2 12.0 %collective-permute-done.21.refs_2_ = bf16[128,2176]{1,0:T(8,128)(2,1)S(1)} collective-permute-done((bf16[128,2176]{1,0:T(8,128)(2,1)S(1)}, bf16[128,2176]{1,0:T(8,128)(2,1)S(1)}, u32[]{:S(2)}, u32[]{:S(2)}) %collective-permute-start.21) | collective-permute-done | bytes 557088 | tf_op jit(solution)/shard_map/ppermute | solution.py:339
  129.2 2.9 %collective-permute-done.27.refs_0_ = bf16[128,2176]{1,0:T(8,128)(2,1)S(1)} collective-permute-done((bf16[128,2176]{1,0:T(8,128)(2,1)S(1)}, bf16[128,2176]{1,0:T(8,128)(2,1)S(1)}, u32[]{:S(2)}, u32[]{:S(2)}) %collective-permute-start.27) | collective-permute-done | bytes 557088 | tf_op jit(solution)/shard_map/ppermute | solution.py:342
  132.7 2.8 %copy-done = bf16[2,2048,768]{2,1,0:T(8,128)(2,1)S(1)} copy-done((bf16[2,2048,768]{2,1,0:T(8,128)(2,1)S(1)}, bf16[2,2048,768]{2,1,0:T(8,128)(2,1)}, u32[]{:S(2)}) %copy-start) | copy-done | bytes 6291480
  135.5 11.0 %experts.4 = (bf16[128,2048]{1,0:T(8,128)(2,1)S(1)}, bf16[128,2048]{1,0:T(8,128)(2,1)S(1)}, bf16[128,2048]{1,0:T(8,128)(2,1)S(1)}, bf16[128,2048]{1,0:T(8,128)(2,1)S(1)}) custom-call(s32[1]{0:T(128)} %bitcast.3.place, bf16[128,2176]{1,0:T(8,128)(2,1)S(1)} %collective-permute-done.19.refs_0_, bf16[128,2176]{1,0:T(8,128)(2,1)S(1)} %collective-permute-done.20.refs_1_, ...), custom_call_target="tpu_custom_call" | custom-call | flops 4831838208 | bytes 23068672 | tf_op jit(solution)/shard_map/experts/pallas_call | solution.py:296
  150.7 11.0 %experts.5 = (bf16[128,2048]{1,0:T(8,128)(2,1)S(1)}, bf16[128,2048]{1,0:T(8,128)(2,1)S(1)}, bf16[128,2048]{1,0:T(8,128)(2,1)S(1)}, bf16[128,2048]{1,0:T(8,128)(2,1)S(1)}) custom-call(s32[1]{0:T(128)} %bitcast.3.place, bf16[128,2176]{1,0:T(8,128)(2,1)S(1)} %collective-permute-done.27.refs_0_, bf16[128,2176]{1,0:T(8,128)(2,1)S(1)} %collective-permute-done.28.refs_1_, ...), custom_call_target="tpu_custom_call" | custom-call | flops 4831838208 | bytes 23068672 | tf_op jit(solution)/shard_map/experts/pallas_call | solution.py:296
  162.6 3.1 %collective-permute-done.35.refs_0_ = bf16[128,2176]{1,0:T(8,128)(2,1)S(1)} collective-permute-done((bf16[128,2176]{1,0:T(8,128)(2,1)S(1)}, bf16[128,2176]{1,0:T(8,128)(2,1)S(1)}, u32[]{:S(2)}, u32[]{:S(2)}) %collective-permute-start.35) | collective-permute-done | bytes 557088 | tf_op jit(solution)/shard_map/ppermute | solution.py:342
  166.3 10.4 %collective-permute-done.37.refs_2_ = bf16[128,2176]{1,0:T(8,128)(2,1)S(1)} collective-permute-done((bf16[128,2176]{1,0:T(8,128)(2,1)S(1)}, bf16[128,2176]{1,0:T(8,128)(2,1)S(1)}, u32[]{:S(2)}, u32[]{:S(2)}) %collective-permute-start.37) | collective-permute-done | bytes 557088 | tf_op jit(solution)/shard_map/ppermute | solution.py:342
  180.4 11.0 %experts.6 = (bf16[128,2048]{1,0:T(8,128)(2,1)S(1)}, bf16[128,2048]{1,0:T(8,128)(2,1)S(1)}, bf16[128,2048]{1,0:T(8,128)(2,1)S(1)}, bf16[128,2048]{1,0:T(8,128)(2,1)S(1)}) custom-call(s32[1]{0:T(128)} %bitcast.3.place, bf16[128,2176]{1,0:T(8,128)(2,1)S(1)} %collective-permute-done.35.refs_0_, bf16[128,2176]{1,0:T(8,128)(2,1)S(1)} %collective-permute-done.36.refs_1_, ...), custom_call_target="tpu_custom_call" | custom-call | flops 4831838208 | bytes 23068672 | tf_op jit(solution)/shard_map/experts/pallas_call | solution.py:296
  191.5 11.0 %experts.7 = (bf16[128,2048]{1,0:T(8,128)(2,1)S(1)}, bf16[128,2048]{1,0:T(8,128)(2,1)S(1)}, bf16[128,2048]{1,0:T(8,128)(2,1)S(1)}, bf16[128,2048]{1,0:T(8,128)(2,1)S(1)}) custom-call(s32[1]{0:T(128)} %bitcast.3.place, bf16[128,2176]{1,0:T(8,128)(2,1)S(1)} %pad_maximum_fusion.refs_0_, bf16[128,2176]{1,0:T(8,128)(2,1)S(1)} %collective-permute-done.43.refs_1_, ...), custom_call_target="tpu_custom_call" | custom-call | flops 4831838208 | bytes 23068672 | tf_op jit(solution)/shard_map/experts/pallas_call | solution.py:296
  206.2 13.5 %collective-permute-done.34 = bf16[128,2048]{1,0:T(8,128)(2,1)S(1)} collective-permute-done((bf16[128,2048]{1,0:T(8,128)(2,1)S(1)}, bf16[128,2048]{1,0:T(8,128)(2,1)S(1)}, u32[]{:S(2)}, u32[]{:S(2)}) %collective-permute-start.34) | collective-permute-done | bytes 524320 | tf_op jit(solution)/shard_map/ppermute | solution.py:342
  220.1 9.2 %collective-permute-done.48 = bf16[128,2048]{1,0:T(8,128)(2,1)S(1)} collective-permute-done((bf16[128,2048]{1,0:T(8,128)(2,1)S(1)}, bf16[128,2048]{1,0:T(8,128)(2,1)S(1)}, u32[]{:S(2)}, u32[]{:S(2)}) %collective-permute-start.48) | collective-permute-done | bytes 524320 | tf_op jit(solution)/shard_map/ppermute | solution.py:339
  229.3 5.9 %collective-permute-done.42 = bf16[128,2048]{1,0:T(8,128)(2,1)S(1)} collective-permute-done((bf16[128,2048]{1,0:T(8,128)(2,1)S(1)}, bf16[128,2048]{1,0:T(8,128)(2,1)S(1)}, u32[]{:S(2)}, u32[]{:S(2)}) %collective-permute-start.42) | collective-permute-done | bytes 524320 | tf_op jit(solution)/shard_map/ppermute | solution.py:342
  (153 shorter events, 47.2 us)
Async XLA Ops:
  0.0 38.8 %collective-permute-start.8 = (bf16[256,2048]{1,0:T(8,128)(2,1)}, bf16[256,2048]{1,0:T(8,128)(2,1)S(1)}, u32[]{:S(2)}, u32[]{:S(2)}) collective-permute-start(bf16[256,2048]{1,0:T(8,128)(2,1)} %refs_9_.3), channel_id=1, source_target_pairs={{0,2},{1,3},{2,0},{3,1},{4,6},{5,7},{6,4},{7,5},{8,10},{9,11},{10,... | collective-permute-start | bytes 3145736 | tf_op jit(solution)/shard_map/ppermute | solution.py:339
  3.1 36.4 %collective-permute-start.10 = (bf16[256,2048]{1,0:T(8,128)(2,1)}, bf16[256,2048]{1,0:T(8,128)(2,1)S(1)}, u32[]{:S(2)}, u32[]{:S(2)}) collective-permute-start(bf16[256,2048]{1,0:T(8,128)(2,1)} %refs_9_.3), channel_id=1, source_target_pairs={{0,4},{1,5},{2,6},{3,7},{4,0},{5,1},{6,2},{7,3},{8,12},{9,13},{10,... | collective-permute-start | bytes 3145736 | tf_op jit(solution)/shard_map/ppermute | solution.py:339
  43.3 16.9 %collective-permute-start.12 = (bf16[128,2048]{1,0:T(8,128)(2,1)}, bf16[128,2048]{1,0:T(8,128)(2,1)}, u32[]{:S(2)}, u32[]{:S(2)}) collective-permute-start(bf16[128,2048]{1,0:T(8,128)(2,1)} %slice.14), channel_id=1, source_target_pairs={{0,4},{1,5},{2,6},{3,7},{4,0},{5,1},{6,2},{7,3},{8,12},{9,13},{10,... | collective-permute-start | bytes 1572872 | tf_op jit(solution)/shard_map/ppermute | solution.py:339
  44.9 16.2 %collective-permute-start.14 = (bf16[128,2048]{1,0:T(8,128)(2,1)}, bf16[128,2048]{1,0:T(8,128)(2,1)}, u32[]{:S(2)}, u32[]{:S(2)}) collective-permute-start(bf16[128,2048]{1,0:T(8,128)(2,1)} %slice.15), channel_id=1, source_target_pairs={{0,2},{1,3},{2,0},{3,1},{4,6},{5,7},{6,4},{7,5},{8,10},{9,11},{10,... | collective-permute-start | bytes 1572872 | tf_op jit(solution)/shard_map/ppermute | solution.py:339
  45.4 18.6 %collective-permute-start.7 = (bf16[256,2048]{1,0:T(8,128)(2,1)S(1)}, bf16[256,2048]{1,0:T(8,128)(2,1)}, u32[]{:S(2)}, u32[]{:S(2)}) collective-permute-start(bf16[256,2048]{1,0:T(8,128)(2,1)S(1)} %copy-done.5), channel_id=1, source_target_pairs={{0,1},{1,0},{2,3},{3,2},{4,5},{5,4},{6,7},{7,6},{8,9},{9,8},{10,11... | collective-permute-start | bytes 3145736 | tf_op jit(solution)/shard_map/ppermute | solution.py:339
  46.4 17.6 %collective-permute-start.9 = (bf16[256,2048]{1,0:T(8,128)(2,1)S(1)}, bf16[256,2048]{1,0:T(8,128)(2,1)}, u32[]{:S(2)}, u32[]{:S(2)}) collective-permute-start(bf16[256,2048]{1,0:T(8,128)(2,1)S(1)} %collective-permute-done.8.refs_11_), channel_id=1, source_target_pairs={{0,1},{1,0},{2,3},{3,2},{4,5},{5,4},{6,7},{7,6},{8,9},{9,8},{10,11... | collective-permute-start | bytes 3145736 | tf_op jit(solution)/shard_map/ppermute | solution.py:339
  68.5 25.4 %collective-permute-start.17 = (bf16[128,1024]{1,0:T(8,128)(2,1)}, bf16[128,1024]{1,0:T(8,128)(2,1)S(1)}, u32[]{:S(2)}, u32[]{:S(2)}) collective-permute-start(bf16[128,1024]{1,0:T(8,128)(2,1)} %get-tuple-element.45), channel_id=1, source_target_pairs={{0,8},{1,9},{2,10},{3,11},{4,12},{5,13},{6,14},{7,15},{8,0},{9,1},... | collective-permute-start | bytes 786440 | tf_op jit(solution)/shard_map/ppermute | solution.py:342
  75.9 17.0 %collective-permute-start.18 = (f32[128,128]{1,0:T(8,128)}, f32[128,128]{1,0:T(8,128)S(1)}, u32[]{:S(2)}, u32[]{:S(2)}) collective-permute-start(f32[128,128]{1,0:T(8,128)} %get-tuple-element.47), channel_id=1, source_target_pairs={{0,8},{1,9},{2,10},{3,11},{4,12},{5,13},{6,14},{7,15},{8,0},{9,1},... | collective-permute-start | bytes 196616 | tf_op jit(solution)/shard_map/ppermute | solution.py:342
  76.5 21.6 %collective-permute-start.16 = (bf16[128,1024]{1,0:T(8,128)(2,1)}, bf16[128,1024]{1,0:T(8,128)(2,1)S(1)}, u32[]{:S(2)}, u32[]{:S(2)}) collective-permute-start(bf16[128,1024]{1,0:T(8,128)(2,1)} %get-tuple-element.43), channel_id=1, source_target_pairs={{0,8},{1,9},{2,10},{3,11},{4,12},{5,13},{6,14},{7,15},{8,0},{9,1},... | collective-permute-start | bytes 786440 | tf_op jit(solution)/shard_map/ppermute | solution.py:342
  99.8 16.0 %collective-permute-start.19 = (bf16[128,2176]{1,0:T(8,128)(2,1)S(1)}, bf16[128,2176]{1,0:T(8,128)(2,1)S(1)}, u32[]{:S(2)}, u32[]{:S(2)}) collective-permute-start(bf16[128,2176]{1,0:T(8,128)(2,1)S(1)} %pad_maximum_fusion.refs_0_), channel_id=1, source_target_pairs={{0,4},{1,5},{2,6},{3,7},{4,8},{5,9},{6,10},{7,11},{8,12},{9,13},{1... | collective-permute-start | bytes 1671176 | tf_op jit(solution)/shard_map/ppermute | solution.py:342
  117.2 15.5 %collective-permute-start.20 = (bf16[128,2176]{1,0:T(8,128)(2,1)S(1)}, bf16[128,2176]{1,0:T(8,128)(2,1)S(1)}, u32[]{:S(2)}, u32[]{:S(2)}) collective-permute-start(bf16[128,2176]{1,0:T(8,128)(2,1)S(1)} %collective-permute-done.19.refs_0_), channel_id=1, source_target_pairs={{0,1},{1,0},{2,3},{3,2},{4,5},{5,4},{6,7},{7,6},{8,9},{9,8},{10,11... | collective-permute-start | bytes 1671176 | tf_op jit(solution)/shard_map/ppermute | solution.py:339
  132.1 16.4 %collective-permute-start.28 = (bf16[128,2176]{1,0:T(8,128)(2,1)S(1)}, bf16[128,2176]{1,0:T(8,128)(2,1)S(1)}, u32[]{:S(2)}, u32[]{:S(2)}) collective-permute-start(bf16[128,2176]{1,0:T(8,128)(2,1)S(1)} %collective-permute-done.27.refs_0_), channel_id=1, source_target_pairs={{0,1},{1,0},{2,3},{3,2},{4,5},{5,4},{6,7},{7,6},{8,9},{9,8},{10,11... | collective-permute-start | bytes 1671176 | tf_op jit(solution)/shard_map/ppermute | solution.py:339
  148.5 17.3 %collective-permute-start.35 = (bf16[128,2176]{1,0:T(8,128)(2,1)S(1)}, bf16[128,2176]{1,0:T(8,128)(2,1)S(1)}, u32[]{:S(2)}, u32[]{:S(2)}) collective-permute-start(bf16[128,2176]{1,0:T(8,128)(2,1)S(1)} %collective-permute-done.27.refs_0_), channel_id=1, source_target_pairs={{0,4},{1,5},{2,6},{3,7},{4,8},{5,9},{6,10},{7,11},{8,12},{9,13},{1... | collective-permute-start | bytes 1671176 | tf_op jit(solution)/shard_map/ppermute | solution.py:342
  148.5 17.3 %collective-permute-start.23 = (bf16[128,2048]{1,0:T(8,128)(2,1)S(1)}, bf16[128,2048]{1,0:T(8,128)(2,1)S(1)}, u32[]{:S(2)}, u32[]{:S(2)}) collective-permute-start(bf16[128,2048]{1,0:T(8,128)(2,1)S(1)} %get-tuple-element.50), channel_id=1, source_target_pairs={{0,1},{1,0},{2,3},{3,2},{4,5},{5,4},{6,7},{7,6},{8,9},{9,8},{10,11... | collective-permute-start | bytes 1572872 | tf_op jit(solution)/shard_map/ppermute | solution.py:339
  148.5 28.2 %collective-permute-start.37 = (bf16[128,2176]{1,0:T(8,128)(2,1)S(1)}, bf16[128,2176]{1,0:T(8,128)(2,1)S(1)}, u32[]{:S(2)}, u32[]{:S(2)}) collective-permute-start(bf16[128,2176]{1,0:T(8,128)(2,1)S(1)} %collective-permute-done.29.refs_2_), channel_id=1, source_target_pairs={{0,4},{1,5},{2,6},{3,7},{4,8},{5,9},{6,10},{7,11},{8,12},{9,13},{1... | collective-permute-start | bytes 1671176 | tf_op jit(solution)/shard_map/ppermute | solution.py:342
  149.3 27.4 %collective-permute-start.25 = (bf16[128,2048]{1,0:T(8,128)(2,1)S(1)}, bf16[128,2048]{1,0:T(8,128)(2,1)S(1)}, u32[]{:S(2)}, u32[]{:S(2)}) collective-permute-start(bf16[128,2048]{1,0:T(8,128)(2,1)S(1)} %add_convert_fusion.13), channel_id=1, source_target_pairs={{0,2},{1,3},{2,0},{3,1},{4,6},{5,7},{6,4},{7,5},{8,10},{9,11},{10,... | collective-permute-start | bytes 1572872 | tf_op jit(solution)/shard_map/ppermute | solution.py:339
  165.8 25.6 %collective-permute-start.43 = (bf16[128,2176]{1,0:T(8,128)(2,1)S(1)}, bf16[128,2176]{1,0:T(8,128)(2,1)S(1)}, u32[]{:S(2)}, u32[]{:S(2)}) collective-permute-start(bf16[128,2176]{1,0:T(8,128)(2,1)S(1)} %pad_maximum_fusion.refs_0_), channel_id=1, source_target_pairs={{0,1},{1,0},{2,3},{3,2},{4,5},{5,4},{6,7},{7,6},{8,9},{9,8},{10,11... | collective-permute-start | bytes 1671176 | tf_op jit(solution)/shard_map/ppermute | solution.py:339
  165.8 25.7 %collective-permute-start.45 = (bf16[128,2176]{1,0:T(8,128)(2,1)S(1)}, bf16[128,2176]{1,0:T(8,128)(2,1)S(1)}, u32[]{:S(2)}, u32[]{:S(2)}) collective-permute-start(bf16[128,2176]{1,0:T(8,128)(2,1)S(1)} %collective-permute-done.44.refs_2_), channel_id=1, source_target_pairs={{0,1},{1,0},{2,3},{3,2},{4,5},{5,4},{6,7},{7,6},{8,9},{9,8},{10,11... | collective-permute-start | bytes 1671176 | tf_op jit(solution)/shard_map/ppermute | solution.py:339
  177.5 25.6 %collective-permute-start.31 = (bf16[128,2048]{1,0:T(8,128)(2,1)S(1)}, bf16[128,2048]{1,0:T(8,128)(2,1)S(1)}, u32[]{:S(2)}, u32[]{:S(2)}) collective-permute-start(bf16[128,2048]{1,0:T(8,128)(2,1)S(1)} %get-tuple-element.54), channel_id=1, source_target_pairs={{0,1},{1,0},{2,3},{3,2},{4,5},{5,4},{6,7},{7,6},{8,9},{9,8},{10,11... | collective-permute-start | bytes 1572872 | tf_op jit(solution)/shard_map/ppermute | solution.py:339
  178.7 24.5 %collective-permute-start.26 = (bf16[128,2048]{1,0:T(8,128)(2,1)S(1)}, bf16[128,2048]{1,0:T(8,128)(2,1)S(1)}, u32[]{:S(2)}, u32[]{:S(2)}) collective-permute-start(bf16[128,2048]{1,0:T(8,128)(2,1)S(1)} %add_convert_fusion.12), channel_id=1, source_target_pairs={{0,4},{1,5},{2,6},{3,7},{4,8},{5,9},{6,10},{7,11},{8,12},{9,13},{1... | collective-permute-start | bytes 1572872 | tf_op jit(solution)/shard_map/ppermute | solution.py:342
  179.5 23.7 %collective-permute-start.33 = (bf16[128,2048]{1,0:T(8,128)(2,1)S(1)}, bf16[128,2048]{1,0:T(8,128)(2,1)S(1)}, u32[]{:S(2)}, u32[]{:S(2)}) collective-permute-start(bf16[128,2048]{1,0:T(8,128)(2,1)S(1)} %add_convert_fusion.10), channel_id=1, source_target_pairs={{0,2},{1,3},{2,0},{3,1},{4,6},{5,7},{6,4},{7,5},{8,10},{9,11},{10,... | collective-permute-start | bytes 1572872 | tf_op jit(solution)/shard_map/ppermute | solution.py:339
  203.6 16.1 %collective-permute-start.34 = (bf16[128,2048]{1,0:T(8,128)(2,1)S(1)}, bf16[128,2048]{1,0:T(8,128)(2,1)S(1)}, u32[]{:S(2)}, u32[]{:S(2)}) collective-permute-start(bf16[128,2048]{1,0:T(8,128)(2,1)S(1)} %add_convert_fusion.8), channel_id=1, source_target_pairs={{0,4},{1,5},{2,6},{3,7},{4,8},{5,9},{6,10},{7,11},{8,12},{9,13},{1... | collective-permute-start | bytes 1572872 | tf_op jit(solution)/shard_map/ppermute | solution.py:342
  203.8 15.9 %collective-permute-start.41 = (bf16[128,2048]{1,0:T(8,128)(2,1)S(1)}, bf16[128,2048]{1,0:T(8,128)(2,1)S(1)}, u32[]{:S(2)}, u32[]{:S(2)}) collective-permute-start(bf16[128,2048]{1,0:T(8,128)(2,1)S(1)} %add_convert_fusion.6), channel_id=1, source_target_pairs={{0,2},{1,3},{2,0},{3,1},{4,6},{5,7},{6,4},{7,5},{8,10},{9,11},{10,... | collective-permute-start | bytes 1572872 | tf_op jit(solution)/shard_map/ppermute | solution.py:339
  205.2 24.1 %collective-permute-start.48 = (bf16[128,2048]{1,0:T(8,128)(2,1)S(1)}, bf16[128,2048]{1,0:T(8,128)(2,1)S(1)}, u32[]{:S(2)}, u32[]{:S(2)}) collective-permute-start(bf16[128,2048]{1,0:T(8,128)(2,1)S(1)} %add_convert_fusion.2), channel_id=1, source_target_pairs={{0,2},{1,3},{2,0},{3,1},{4,6},{5,7},{6,4},{7,5},{8,10},{9,11},{10,... | collective-permute-start | bytes 1572872 | tf_op jit(solution)/shard_map/ppermute | solution.py:339
  (44 other events, 654.3 us)

commit v2 on v1

--- a/solution.py
+++ b/solution.py
@@ -21,99 +21,123 @@
 
 
 def scan_kernel(
-    starts, place, prep_ref, x_ref, g_ref, b_ref, c_ref, init_ref, *refs, heads, requests
+    lengths, place, rates, step_ref, x_ref, g_ref, b_ref, c_ref, init_ref, *refs, span, chunks
 ):
-    out_refs, (state, src, first_src) = refs[:8], refs[8:]
-    span, width = x_ref.shape
+    out_refs, (runs, rows, state, src, first_src) = refs[:8], refs[8:]
+    heads, tokens = step_ref.shape
+    requests, width, _ = init_ref.shape
     tok = out_refs[0].shape[1]
     head_dim = width // heads
-    c0 = pl.program_id(0) * span
-    steps = prep_ref[0:8, :]
-    run = prep_ref[8:16, :]
-    lane = lax.broadcasted_iota(jnp.int32, run.shape, 1)
-    shift = 1
-    while shift < span:
-        run = run + jnp.where(lane >= shift, pltpu.roll(run, shift, 1), 0.0)
-        shift *= 2
-    before = jnp.zeros_like(run)
-    first_last = jnp.int32(0)
-    pos = lax.broadcasted_iota(jnp.int32, (span, 1), 0) + c0
-    first = jnp.zeros_like(pos)
-    inside = []
-    for r in range(requests):
-        start = starts[r]
-        at = start - c0
-        here = jnp.logical_and(at >= 0, at < span)
-        inside.append(here)
-        value = jnp.sum(jnp.where(lane == at - 1, run, 0.0), axis=1, keepdims=True)
-        from_here = jnp.where(here, at, span)
-        before = jnp.where(lane >= from_here, value, before)
-        first_last = jnp.where(at < span, start, first_last)
-        first = jnp.where(pos >= start, start, first)
-    weight = jnp.exp(run - before)
-    last = jnp.where(lane >= first_last - c0, jnp.exp(run[:, span - 1 : span] - run), 0.0)
-
-    spread_row = lax.broadcasted_iota(jnp.int32, (8, width), 0)
-    spread_col = lax.broadcasted_iota(jnp.int32, (8, width), 1) // head_dim
-    spread = jnp.where(spread_row == spread_col, 1.0, 0.0)
-
-    def widen(rows):
-        return mm(rows, spread, TN, lax.Precision.HIGHEST)
+    starts = [jnp.int32(0)]
+    for r in range(requests - 1):
+        starts.append(starts[-1] + lengths[r])
 
     @pl.when(pl.program_id(0) == 0)
     def _():
         state[...] = jnp.zeros_like(state)
-
-    drive = x_ref[...].astype(jnp.float32) * widen(steps)
-    drive_low = drive.astype(jnp.bfloat16)
-    drive_last = (drive * widen(last)).astype(jnp.bfloat16)
-    basis = b_ref[...]
-    readout = c_ref[...]
+        runs[...] = jnp.zeros_like(runs)
+        for h in range(heads):
+            runs[h : h + 1, :] = -step_ref[h : h + 1, :] * rates[h]
+        run = runs[...]
+        lane = lax.broadcasted_iota(jnp.int32, run.shape, 1)
+        inner = lane % span
+        shift = 1
+        while shift < span:
+            run = run + jnp.where(inner >= shift, pltpu.roll(run, shift, 1), 0.0)
+            shift *= 2
+        runs[...] = run
+        final = lane - inner + (span - 1)
+        before = jnp.zeros_like(run)
+        first_last = jnp.zeros_like(lane)
+        for start in starts:
+            end = start - start % span + span
+            inside = jnp.logical_and(lane == start - 1, start % span > 0)
+            value = jnp.sum(jnp.where(inside, run, 0.0), axis=1, keepdims=True)
+            before = jnp.where(jnp.logical_and(lane >= start, lane < end), value, before)
+            first_last = jnp.where(final >= start, start, first_last)
+        weight = jnp.exp(run - before)
+        ends = [
+            jnp.broadcast_to(run[:, at + span - 1 : at + span], (8, span))
+            for at in range(0, tokens, span)
+        ]
+        ends = jnp.concatenate(ends, axis=1)
+        last = jnp.where(lane >= first_last, jnp.exp(ends - run), 0.0)
+        zeros = jnp.zeros_like(run)
+        steps = jnp.concatenate([step_ref[...], zeros[heads:]], axis=0)
+        for i, value in enumerate((steps, last, weight)):
+            high = value.astype(jnp.bfloat16)
+            low = (value - high.astype(jnp.float32)).astype(jnp.bfloat16)
+            rows[16 * i : 16 * i + 16, :] = jnp.concatenate([high, low], axis=0)
+
+    spread_row = lax.broadcasted_iota(jnp.int32, (48, 3 * width), 0)
+    spread_col = lax.broadcasted_iota(jnp.int32, (48, 3 * width), 1)
+    spread = jnp.logical_and(
+        spread_row // 16 == spread_col // width, spread_row % 8 == spread_col % width // head_dim
+    )
+    spread = jnp.where(spread, 1.0, 0.0).astype(jnp.bfloat16)
     row = lax.broadcasted_iota(jnp.int32, (span, span), 0)
     col = lax.broadcasted_iota(jnp.int32, (span, span), 1)
-    valid = jnp.logical_and(col <= row, col >= first - c0)
-    scores = jnp.where(valid, mm(readout, basis, NT), 0.0)
-
-    src[...] = mm(readout, state[...].astype(jnp.bfloat16))
-    first_src[...] = state[...]
-    for r in range(requests):
-
-        @pl.when(inside[r])
-        def _(r=r):
-            init = init_ref[r].T
-            mine = mm(readout, init.astype(jnp.bfloat16))
-            src[...] = jnp.where(first == starts[r], mine, src[...])
-            first_src[...] = init
-
-    weight_wide = widen(weight)
-    run_cols = run.T
+    causal = col <= row
     per_tile = LANES // head_dim
     tile_lane = lax.broadcasted_iota(jnp.int32, (span, LANES), 1) // head_dim
-    pieces = []
-    for tile in range(heads // per_tile):
-        drive_tile = drive_low[:, tile * LANES : (tile + 1) * LANES]
-        piece = None
-        for j in range(per_tile):
-            h = tile * per_tile + j
-            gap = jnp.minimum(run_cols[:, h : h + 1] - run[h : h + 1, :], 0.0)
-            part = mm((jnp.exp(gap) * scores).astype(jnp.bfloat16), drive_tile)
-            piece = part if piece is None else jnp.where(tile_lane == j, part, piece)
-        pieces.append(piece)
-    inner = pieces[0] if len(pieces) == 1 else jnp.concatenate(pieces, axis=1)
-    output = inner + weight_wide * src[...]
-    state[...] = mm(basis, drive_last, TN) + weight_wide[span - 1 : span, :] * first_src[...]
-    gate = g_ref[...].astype(jnp.float32)
-    gated = (output * (gate / (1.0 + jnp.exp(-gate)))).astype(jnp.bfloat16)
-    even = lax.rem(place[0], 2) == 0
-    mine = jnp.where(even, gated[:tok], gated[tok:])
-    other = jnp.where(even, gated[tok:], gated[:tok])
-    pair = lax.rem(pl.program_id(0), 4) ^ lax.div(lax.rem(place[0], 8), 2)
-    for way in range(4):
-
-        @pl.when(pair == way)
-        def _(way=way):
-            out_refs[2 * way][0] = mine
-            out_refs[2 * way + 1][0] = other
+    local_pos = lax.broadcasted_iota(jnp.int32, (span, 1), 0)
+
+    for u in range(chunks):
+        chunk = pl.program_id(0) * chunks + u
+        c0 = pl.multiple_of(chunk * span, span)
+        here = pl.ds(u * span, span)
+        run = runs[:, pl.ds(c0, span)]
+        pos = local_pos + c0
+        first = jnp.zeros_like(pos)
+        for start in starts:
+            first = jnp.where(pos >= start, start, first)
+        spread_all = mm(rows[:, pl.ds(c0, span)], spread, TN)
+        weight_wide = spread_all[:, 2 * width :]
+        drive = x_ref[here, :].astype(jnp.float32) * spread_all[:, :width]
+        drive_low = drive.astype(jnp.bfloat16)
+        drive_last = (drive * spread_all[:, width : 2 * width]).astype(jnp.bfloat16)
+        basis = b_ref[here, :]
+        readout = c_ref[here, :]
+        valid = jnp.logical_and(causal, col >= first - c0)
+        scores = jnp.where(valid, mm(readout, basis, NT), 0.0)
+
+        src[...] = mm(readout, state[...].astype(jnp.bfloat16))
+        first_src[...] = state[...]
+        for r, start in enumerate(starts):
+
+            @pl.when(jnp.logical_and(start >= c0, start < c0 + span))
+            def _(r=r, start=start):
+                init = init_ref[r].T
+                mine = mm(readout, init.astype(jnp.bfloat16))
+                src[...] = jnp.where(first == start, mine, src[...])
+                first_src[...] = init
+
+        run_cols = run.T
+        pieces = []
+        for tile in range(heads // per_tile):
+            drive_tile = drive_low[:, tile * LANES : (tile + 1) * LANES]
+            piece = None
+            for j in range(per_tile):
+                h = tile * per_tile + j
+                gap = jnp.minimum(run_cols[:, h : h + 1] - run[h : h + 1, :], 0.0)
+                part = mm((jnp.exp(gap) * scores).astype(jnp.bfloat16), drive_tile)
+                piece = part if piece is None else jnp.where(tile_lane == j, part, piece)
+            pieces.append(piece)
+        within = pieces[0] if len(pieces) == 1 else jnp.concatenate(pieces, axis=1)
+        output = within + weight_wide * src[...]
+        state[...] = mm(basis, drive_last, TN) + weight_wide[span - 1 : span, :] * first_src[...]
+        gate = g_ref[here, :].astype(jnp.float32)
+        gated = (output * (gate / (1.0 + jnp.exp(-gate)))).astype(jnp.bfloat16)
+        even = lax.rem(place[0], 2) == 0
+        mine = jnp.where(even, gated[:tok], gated[tok:])
+        other = jnp.where(even, gated[tok:], gated[:tok])
+        pair = lax.rem(chunk, 4) ^ lax.div(lax.rem(place[0], 8), 2)
+        for way in range(4):
+
+            @pl.when(pair == way)
+            def _(way=way, mine=mine, other=other):
+                out_refs[2 * way][0] = mine
+                out_refs[2 * way + 1][0] = other
 
 
 def scan_heads(head_in, gate_in, in_basis, out_basis, step, rate, init, lengths, place, depth):
@@ -123,10 +147,8 @@
     states = in_basis.shape[1]
     tok = tokens // (8 * depth)
     span = 2 * tok
-    ends = jnp.cumsum(lengths)
-    starts = (ends - lengths).astype(jnp.int32)
-    pad = ((0, 8 - heads), (0, 0))
-    prep = jnp.concatenate([jnp.pad(step, pad), jnp.pad(-step * rate[:, None], pad)], axis=0)
+    chunks = 2
+    block = chunks * span
     init = init.reshape(requests, width, states)
     cost = pl.CostEstimate(
         flops=2 * tokens * width * (span * 2 + 3 * states),
@@ -134,28 +156,30 @@
         transcendentals=tokens * span * heads,
     )
 
-    def row_block(i, starts, place):
+    def row_block(i, lengths, place, rates):
         return (i, 0)
 
-    def out_block(i, starts, place):
-        return (lax.rem(lax.div(place[0], 8) - lax.div(i, 4) + depth, depth), 0, 0)
+    def out_block(i, lengths, place, rates):
+        return (lax.rem(lax.div(place[0], 8) - lax.div(i * chunks, 4) + depth, depth), 0, 0)
 
     return pl.pallas_call(
-        functools.partial(scan_kernel, heads=heads, requests=requests),
+        functools.partial(scan_kernel, span=span, chunks=chunks),
         out_shape=[jax.ShapeDtypeStruct((depth, tok, width), jnp.bfloat16)] * 8,
         grid_spec=pltpu.PrefetchScalarGridSpec(
-            num_scalar_prefetch=2,
-            grid=(tokens // span,),
+            num_scalar_prefetch=3,
+            grid=(tokens // block,),
             in_specs=[
-                pl.BlockSpec((16, span), lambda i, starts, place: (0, i)),
-                pl.BlockSpec((span, width), row_block),
-                pl.BlockSpec((span, width), row_block),
-                pl.BlockSpec((span, states), row_block),
-                pl.BlockSpec((span, states), row_block),
-                pl.BlockSpec((requests, width, states), lambda i, starts, place: (0, 0, 0)),
+                pl.BlockSpec((heads, tokens), lambda i, lengths, place, rates: (0, 0)),
+                pl.BlockSpec((block, width), row_block),
+                pl.BlockSpec((block, width), row_block),
+                pl.BlockSpec((block, states), row_block),
+                pl.BlockSpec((block, states), row_block),
+                pl.BlockSpec((requests, width, states), lambda i, lengths, place, rates: (0, 0, 0)),
             ],
             out_specs=[pl.BlockSpec((1, tok, width), out_block)] * 8,
             scratch_shapes=[
+                pltpu.VMEM((8, tokens), jnp.float32),
+                pltpu.VMEM((48, tokens), jnp.bfloat16),
                 pltpu.VMEM((states, width), jnp.float32),
                 pltpu.VMEM((span, width), jnp.float32),
                 pltpu.VMEM((states, width), jnp.float32),
@@ -163,7 +187,7 @@
         ),
         cost_estimate=cost,
         name="scan",
-    )(starts, place, prep, head_in, gate_in, in_basis, out_basis, init)
+    )(lengths, place, rate, step, head_in, gate_in, in_basis, out_basis, init)
 
 
 def project_kernel(*refs, depth, squared):

time: 237 us -> 231 us (0.975)
  Pallas kernels: 76.5 us -> 67.9 us
  waiting for transfers between devices: 106 us -> 114 us
  other arithmetic: 14.7 us -> 10.4 us
    pallas_call x1, Pallas kernels: 23.2 us -> 14.6 us  [scan_heads(): pl.pallas_call(functools.partial(scan_kernel, span=span, chunks=chunks),...]
    ppermute x39, waiting for transfers between devices: 36.4 us -> 44.9 us  [cross(): return lax.ppermute(x, 'mix', [(i, i ^ mask) for i in range(devices)])]
  transfers between devices with their start and end apart: 49 -> 49, of which waited for: 19 -> 20; matrix products, arithmetic and copies ran while one was open for 7% -> 6% of each run, Pallas kernels for 30% -> 28%
where the time goes in v2:
time: 231 us
  waiting for transfers between devices  114 us (49%)
  Pallas kernels  67.9 us (29%)
  starting transfers between devices  28.8 us (12%)
  other arithmetic  10.4 us (5%)
  local copies, waits for them, and re-layouts  9.21 us (4%)
    ppermute x10, waiting for transfers between devices, onward(): lax.ppermute(x, 'mix', [(i, (i + stride) % devices) for i in range(device...  68.9 us
    ppermute x39, waiting for transfers between devices, cross(): return lax.ppermute(x, 'mix', [(i, i ^ mask) for i in range(devices)])  44.9 us
    pallas_call x4, Pallas kernels, run_experts(): pl.pallas_call(functools.partial(expert_kernel, blocks=blocks, cap=cap, s...  44.1 us
    ppermute x39, starting transfers between devices, cross(): return lax.ppermute(x, 'mix', [(i, i ^ mask) for i in range(devices)])  22.9 us
    pallas_call x1, Pallas kernels, scan_heads(): pl.pallas_call(functools.partial(scan_kernel, span=span, chunks=chunks),...  14.6 us
    pallas_call x2, Pallas kernels, project(): pl.pallas_call(functools.partial(project_kernel, depth=depth, squared=squ...  9.18 us
    ppermute x10, starting transfers between devices, onward(): lax.ppermute(x, 'mix', [(i, (i + stride) % devices) for i in range(device...  5.88 us
  transfers between devices with their start and end apart: 49, of which 20 were waited for; matrix products, arithmetic and copies ran while one was open for 6% of the time, Pallas kernels for 28%

profile of v2, /device:TPU:0, one launch (start us, length us, event | category | flops | bytes accessed | tf_op | source)
XLA Modules:
  0.0 230.5 jit_solution(6620795653040274523)
XLA Ops:
  0.0 3.1 %collective-permute-start.8 = (bf16[256,2048]{1,0:T(8,128)(2,1)}, bf16[256,2048]{1,0:T(8,128)(2,1)S(1)}, u32[]{:S(2)}, u32[]{:S(2)}) collective-permute-start(bf16[256,2048]{1,0:T(8,128)(2,1)} %refs_9_.3), channel_id=1, source_target_pairs={{0,2},{1,3},{2,0},{3,1},{4,6},{5,7},{6,4},{7,5},{8,10},{9,11},{10,... | collective-permute-start | bytes 3145736 | tf_op jit(solution)/shard_map/ppermute | solution.py:363
  4.6 14.6 %scan.1 = (bf16[2,128,256]{2,1,0:T(8,128)(2,1)}, bf16[2,128,256]{2,1,0:T(8,128)(2,1)}, bf16[2,128,256]{2,1,0:T(8,128)(2,1)}, bf16[2,128,256]{2,1,0:T(8,128)(2,1)...) custom-call(s32[8]{0:T(128)} %lengths.1, ...), custom_call_target="tpu_custom_call" | custom-call | flops 939524096 | bytes 3145728 | tf_op jit(solution)/shard_map/scan/pallas_call | solution.py:165
  21.6 8.5 %collective-permute-done.1.refs_3_ = bf16[2,128,256]{2,1,0:T(8,128)(2,1)S(1)} collective-permute-done((bf16[2,128,256]{2,1,0:T(8,128)(2,1)}, bf16[2,128,256]{2,1,0:T(8,128)(2,1)S(1)}, u32[]{:S(2)}, u32[]{:S(2)}) %collective-permute-start.1) | collective-permute-done | bytes 131104 | tf_op jit(solution)/shard_map/ppermute | solution.py:363
  30.1 3.1 %collective-permute-start.5 = (bf16[2,128,256]{2,1,0:T(8,128)(2,1)}, bf16[2,128,256]{2,1,0:T(8,128)(2,1)S(1)}, u32[]{:S(2)}, u32[]{:S(2)}) collective-permute-start(bf16[2,128,256]{2,1,0:T(8,128)(2,1)} %get-tuple-element.41), channel_id=1, source_target_pairs={{0,6},{1,7},{2,4},{3,5},{4,2},{5,3},{6,0},{7,1},{8,14},{9,15},{10,... | collective-permute-start | bytes 393224 | tf_op jit(solution)/shard_map/ppermute | solution.py:363
  40.6 2.5 %collective-permute-done.6.refs_8_ = bf16[2,128,256]{2,1,0:T(8,128)(2,1)S(1)} collective-permute-done((bf16[2,128,256]{2,1,0:T(8,128)(2,1)}, bf16[2,128,256]{2,1,0:T(8,128)(2,1)S(1)}, u32[]{:S(2)}, u32[]{:S(2)}) %collective-permute-start.6) | collective-permute-done | bytes 131104 | tf_op jit(solution)/shard_map/ppermute | solution.py:363
  49.9 3.2 %collective-permute-done.12.refs_15_ = bf16[128,2048]{1,0:T(8,128)(2,1)} collective-permute-done((bf16[128,2048]{1,0:T(8,128)(2,1)}, bf16[128,2048]{1,0:T(8,128)(2,1)}, u32[]{:S(2)}, u32[]{:S(2)}) %collective-permute-start.12) | collective-permute-done | bytes 524320 | tf_op jit(solution)/shard_map/ppermute | solution.py:363
  57.6 4.4 %project.3 = (bf16[128,1024]{1,0:T(8,128)(2,1)}, bf16[128,1024]{1,0:T(8,128)(2,1)}) custom-call(f32[8,256]{1,0:T(8,128)} %broadcast_select_fusion.refs_0_, bf16[2,128,256]{2,1,0:T(8,128)(2,1)} %get-tuple-element.35.refs_1_, bf16[2,128,256]{2,1,0:T(8,128)(2,1)} %copy-done.6, bf16[2,128,256]{2,1,0:T(8,128)(2,1)} %copy-done.7, bf16[2,128,256]{2,1,0:T(8,128)(2,1)} %copy-done.8, ...), custom_call_target="tpu_custom_call" | custom-call | flops 1073741824 | bytes 5242880 | tf_op jit(solution)/shard_map/project/pallas_call | solution.py:235
  62.0 2.6 %collective-permute-start.17 = (bf16[128,1024]{1,0:T(8,128)(2,1)}, bf16[128,1024]{1,0:T(8,128)(2,1)S(1)}, u32[]{:S(2)}, u32[]{:S(2)}) collective-permute-start(bf16[128,1024]{1,0:T(8,128)(2,1)} %get-tuple-element.45), channel_id=1, source_target_pairs={{0,8},{1,9},{2,10},{3,11},{4,12},{5,13},{6,14},{7,15},{8,0},{9,1},... | collective-permute-start | bytes 786440 | tf_op jit(solution)/shard_map/ppermute | solution.py:366
  64.7 4.8 %project.2 = (bf16[128,1024]{1,0:T(8,128)(2,1)}, bf16[128,1024]{1,0:T(8,128)(2,1)}, f32[128,128]{1,0:T(8,128)}, f32[128,128]{1,0:T(8,128)}) custom-call(f32[8,256]{1,0:T(8,128)} %broadcast_select_fusion.refs_0_, bf16[2,128,256]{2,1,0:T(8,128)(2,1)} %get-tuple-element.35.refs_1_, bf16[2,128,256]{2,1,0:T(8,128)(2,1)} %copy-done.6, ...), custom_call_target="tpu_custom_call" | custom-call | flops 1073741824 | bytes 5242880 | tf_op jit(solution)/shard_map/project/pallas_call | solution.py:235
  70.0 2.6 %collective-permute-start.16 = (bf16[128,1024]{1,0:T(8,128)(2,1)}, bf16[128,1024]{1,0:T(8,128)(2,1)S(1)}, u32[]{:S(2)}, u32[]{:S(2)}) collective-permute-start(bf16[128,1024]{1,0:T(8,128)(2,1)} %get-tuple-element.43), channel_id=1, source_target_pairs={{0,8},{1,9},{2,10},{3,11},{4,12},{5,13},{6,14},{7,15},{8,0},{9,1},... | collective-permute-start | bytes 786440 | tf_op jit(solution)/shard_map/ppermute | solution.py:366
  72.6 13.5 %collective-permute-done.18 = f32[128,128]{1,0:T(8,128)S(1)} collective-permute-done((f32[128,128]{1,0:T(8,128)}, f32[128,128]{1,0:T(8,128)S(1)}, u32[]{:S(2)}, u32[]{:S(2)}) %collective-permute-start.18) | collective-permute-done | bytes 65568 | tf_op jit(solution)/shard_map/ppermute | solution.py:366
  87.1 4.5 %collective-permute-done.16 = bf16[128,1024]{1,0:T(8,128)(2,1)S(1)} collective-permute-done((bf16[128,1024]{1,0:T(8,128)(2,1)}, bf16[128,1024]{1,0:T(8,128)(2,1)S(1)}, u32[]{:S(2)}, u32[]{:S(2)}) %collective-permute-start.16) | collective-permute-done | bytes 262176 | tf_op jit(solution)/shard_map/ppermute | solution.py:366
  93.3 16.3 %collective-permute-done.19.refs_0_ = bf16[128,2176]{1,0:T(8,128)(2,1)S(1)} collective-permute-done((bf16[128,2176]{1,0:T(8,128)(2,1)S(1)}, bf16[128,2176]{1,0:T(8,128)(2,1)S(1)}, u32[]{:S(2)}, u32[]{:S(2)}) %collective-permute-start.19) | collective-permute-done | bytes 557088 | tf_op jit(solution)/shard_map/ppermute | solution.py:366
  110.3 13.1 %collective-permute-done.21.refs_2_ = bf16[128,2176]{1,0:T(8,128)(2,1)S(1)} collective-permute-done((bf16[128,2176]{1,0:T(8,128)(2,1)S(1)}, bf16[128,2176]{1,0:T(8,128)(2,1)S(1)}, u32[]{:S(2)}, u32[]{:S(2)}) %collective-permute-start.21) | collective-permute-done | bytes 557088 | tf_op jit(solution)/shard_map/ppermute | solution.py:363
  126.9 2.8 %copy-done = bf16[2,2048,768]{2,1,0:T(8,128)(2,1)S(1)} copy-done((bf16[2,2048,768]{2,1,0:T(8,128)(2,1)S(1)}, bf16[2,2048,768]{2,1,0:T(8,128)(2,1)}, u32[]{:S(2)}) %copy-start) | copy-done | bytes 6291480
  129.7 11.0 %experts.4 = (bf16[128,2048]{1,0:T(8,128)(2,1)S(1)}, bf16[128,2048]{1,0:T(8,128)(2,1)S(1)}, bf16[128,2048]{1,0:T(8,128)(2,1)S(1)}, bf16[128,2048]{1,0:T(8,128)(2,1)S(1)}) custom-call(s32[1]{0:T(128)} %bitcast.1.place, bf16[128,2176]{1,0:T(8,128)(2,1)S(1)} %collective-permute-done.19.refs_0_, bf16[128,2176]{1,0:T(8,128)(2,1)S(1)} %collective-permute-done.20.refs_1_, ...), custom_call_target="tpu_custom_call" | custom-call | flops 4831838208 | bytes 23068672 | tf_op jit(solution)/shard_map/experts/pallas_call | solution.py:320
  144.1 11.0 %experts.5 = (bf16[128,2048]{1,0:T(8,128)(2,1)S(1)}, bf16[128,2048]{1,0:T(8,128)(2,1)S(1)}, bf16[128,2048]{1,0:T(8,128)(2,1)S(1)}, bf16[128,2048]{1,0:T(8,128)(2,1)S(1)}) custom-call(s32[1]{0:T(128)} %bitcast.1.place, bf16[128,2176]{1,0:T(8,128)(2,1)S(1)} %collective-permute-done.27.refs_0_, bf16[128,2176]{1,0:T(8,128)(2,1)S(1)} %collective-permute-done.28.refs_1_, ...), custom_call_target="tpu_custom_call" | custom-call | flops 4831838208 | bytes 23068672 | tf_op jit(solution)/shard_map/experts/pallas_call | solution.py:320
  156.8 2.4 %collective-permute-done.35.refs_0_ = bf16[128,2176]{1,0:T(8,128)(2,1)S(1)} collective-permute-done((bf16[128,2176]{1,0:T(8,128)(2,1)S(1)}, bf16[128,2176]{1,0:T(8,128)(2,1)S(1)}, u32[]{:S(2)}, u32[]{:S(2)}) %collective-permute-start.35) | collective-permute-done | bytes 557088 | tf_op jit(solution)/shard_map/ppermute | solution.py:366
  159.8 10.7 %collective-permute-done.37.refs_2_ = bf16[128,2176]{1,0:T(8,128)(2,1)S(1)} collective-permute-done((bf16[128,2176]{1,0:T(8,128)(2,1)S(1)}, bf16[128,2176]{1,0:T(8,128)(2,1)S(1)}, u32[]{:S(2)}, u32[]{:S(2)}) %collective-permute-start.37) | collective-permute-done | bytes 557088 | tf_op jit(solution)/shard_map/ppermute | solution.py:366
  174.3 11.0 %experts.6 = (bf16[128,2048]{1,0:T(8,128)(2,1)S(1)}, bf16[128,2048]{1,0:T(8,128)(2,1)S(1)}, bf16[128,2048]{1,0:T(8,128)(2,1)S(1)}, bf16[128,2048]{1,0:T(8,128)(2,1)S(1)}) custom-call(s32[1]{0:T(128)} %bitcast.1.place, bf16[128,2176]{1,0:T(8,128)(2,1)S(1)} %collective-permute-done.35.refs_0_, bf16[128,2176]{1,0:T(8,128)(2,1)S(1)} %collective-permute-done.36.refs_1_, ...), custom_call_target="tpu_custom_call" | custom-call | flops 4831838208 | bytes 23068672 | tf_op jit(solution)/shard_map/experts/pallas_call | solution.py:320
  185.4 11.1 %experts.7 = (bf16[128,2048]{1,0:T(8,128)(2,1)S(1)}, bf16[128,2048]{1,0:T(8,128)(2,1)S(1)}, bf16[128,2048]{1,0:T(8,128)(2,1)S(1)}, bf16[128,2048]{1,0:T(8,128)(2,1)S(1)}) custom-call(s32[1]{0:T(128)} %bitcast.1.place, bf16[128,2176]{1,0:T(8,128)(2,1)S(1)} %pad_maximum_fusion.refs_0_, bf16[128,2176]{1,0:T(8,128)(2,1)S(1)} %collective-permute-done.43.refs_1_, ...), custom_call_target="tpu_custom_call" | custom-call | flops 4831838208 | bytes 23068672 | tf_op jit(solution)/shard_map/experts/pallas_call | solution.py:320
  200.1 13.5 %collective-permute-done.34 = bf16[128,2048]{1,0:T(8,128)(2,1)S(1)} collective-permute-done((bf16[128,2048]{1,0:T(8,128)(2,1)S(1)}, bf16[128,2048]{1,0:T(8,128)(2,1)S(1)}, u32[]{:S(2)}, u32[]{:S(2)}) %collective-permute-start.34) | collective-permute-done | bytes 524320 | tf_op jit(solution)/shard_map/ppermute | solution.py:366
  214.0 9.2 %collective-permute-done.48 = bf16[128,2048]{1,0:T(8,128)(2,1)S(1)} collective-permute-done((bf16[128,2048]{1,0:T(8,128)(2,1)S(1)}, bf16[128,2048]{1,0:T(8,128)(2,1)S(1)}, u32[]{:S(2)}, u32[]{:S(2)}) %collective-permute-start.48) | collective-permute-done | bytes 524320 | tf_op jit(solution)/shard_map/ppermute | solution.py:363
  223.3 5.9 %collective-permute-done.42 = bf16[128,2048]{1,0:T(8,128)(2,1)S(1)} collective-permute-done((bf16[128,2048]{1,0:T(8,128)(2,1)S(1)}, bf16[128,2048]{1,0:T(8,128)(2,1)S(1)}, u32[]{:S(2)}, u32[]{:S(2)}) %collective-permute-start.42) | collective-permute-done | bytes 524320 | tf_op jit(solution)/shard_map/ppermute | solution.py:366
  (149 shorter events, 44.6 us)
Async XLA Ops:
  0.0 30.1 %collective-permute-start.8 = (bf16[256,2048]{1,0:T(8,128)(2,1)}, bf16[256,2048]{1,0:T(8,128)(2,1)S(1)}, u32[]{:S(2)}, u32[]{:S(2)}) collective-permute-start(bf16[256,2048]{1,0:T(8,128)(2,1)} %refs_9_.3), channel_id=1, source_target_pairs={{0,2},{1,3},{2,0},{3,1},{4,6},{5,7},{6,4},{7,5},{8,10},{9,11},{10,... | collective-permute-start | bytes 3145736 | tf_op jit(solution)/shard_map/ppermute | solution.py:363
  3.1 30.2 %collective-permute-start.10 = (bf16[256,2048]{1,0:T(8,128)(2,1)}, bf16[256,2048]{1,0:T(8,128)(2,1)S(1)}, u32[]{:S(2)}, u32[]{:S(2)}) collective-permute-start(bf16[256,2048]{1,0:T(8,128)(2,1)} %refs_9_.3), channel_id=1, source_target_pairs={{0,4},{1,5},{2,6},{3,7},{4,0},{5,1},{6,2},{7,3},{8,12},{9,13},{10,... | collective-permute-start | bytes 3145736 | tf_op jit(solution)/shard_map/ppermute | solution.py:363
  19.9 16.3 %collective-permute-start.2 = (bf16[2,128,256]{2,1,0:T(8,128)(2,1)}, bf16[2,128,256]{2,1,0:T(8,128)(2,1)S(1)}, u32[]{:S(2)}, u32[]{:S(2)}) collective-permute-start(bf16[2,128,256]{2,1,0:T(8,128)(2,1)} %get-tuple-element.38), channel_id=1, source_target_pairs={{0,3},{1,2},{2,1},{3,0},{4,7},{5,6},{6,5},{7,4},{8,11},{9,10},{10,... | collective-permute-start | bytes 393224 | tf_op jit(solution)/shard_map/ppermute | solution.py:363
  36.2 16.9 %collective-permute-start.12 = (bf16[128,2048]{1,0:T(8,128)(2,1)}, bf16[128,2048]{1,0:T(8,128)(2,1)}, u32[]{:S(2)}, u32[]{:S(2)}) collective-permute-start(bf16[128,2048]{1,0:T(8,128)(2,1)} %slice.14), channel_id=1, source_target_pairs={{0,4},{1,5},{2,6},{3,7},{4,0},{5,1},{6,2},{7,3},{8,12},{9,13},{10,... | collective-permute-start | bytes 1572872 | tf_op jit(solution)/shard_map/ppermute | solution.py:363
  36.7 17.8 %collective-permute-start.14 = (bf16[128,2048]{1,0:T(8,128)(2,1)}, bf16[128,2048]{1,0:T(8,128)(2,1)}, u32[]{:S(2)}, u32[]{:S(2)}) collective-permute-start(bf16[128,2048]{1,0:T(8,128)(2,1)} %slice.15), channel_id=1, source_target_pairs={{0,2},{1,3},{2,0},{3,1},{4,6},{5,7},{6,4},{7,5},{8,10},{9,11},{10,... | collective-permute-start | bytes 1572872 | tf_op jit(solution)/shard_map/ppermute | solution.py:363
  38.2 19.2 %collective-permute-start.7 = (bf16[256,2048]{1,0:T(8,128)(2,1)S(1)}, bf16[256,2048]{1,0:T(8,128)(2,1)}, u32[]{:S(2)}, u32[]{:S(2)}) collective-permute-start(bf16[256,2048]{1,0:T(8,128)(2,1)S(1)} %copy-done.5), channel_id=1, source_target_pairs={{0,1},{1,0},{2,3},{3,2},{4,5},{5,4},{6,7},{7,6},{8,9},{9,8},{10,11... | collective-permute-start | bytes 3145736 | tf_op jit(solution)/shard_map/ppermute | solution.py:363
  40.6 16.9 %collective-permute-start.9 = (bf16[256,2048]{1,0:T(8,128)(2,1)S(1)}, bf16[256,2048]{1,0:T(8,128)(2,1)}, u32[]{:S(2)}, u32[]{:S(2)}) collective-permute-start(bf16[256,2048]{1,0:T(8,128)(2,1)S(1)} %collective-permute-done.8.refs_11_), channel_id=1, source_target_pairs={{0,1},{1,0},{2,3},{3,2},{4,5},{5,4},{6,7},{7,6},{8,9},{9,8},{10,11... | collective-permute-start | bytes 3145736 | tf_op jit(solution)/shard_map/ppermute | solution.py:363
  62.0 25.0 %collective-permute-start.17 = (bf16[128,1024]{1,0:T(8,128)(2,1)}, bf16[128,1024]{1,0:T(8,128)(2,1)S(1)}, u32[]{:S(2)}, u32[]{:S(2)}) collective-permute-start(bf16[128,1024]{1,0:T(8,128)(2,1)} %get-tuple-element.45), channel_id=1, source_target_pairs={{0,8},{1,9},{2,10},{3,11},{4,12},{5,13},{6,14},{7,15},{8,0},{9,1},... | collective-permute-start | bytes 786440 | tf_op jit(solution)/shard_map/ppermute | solution.py:366
  69.4 16.6 %collective-permute-start.18 = (f32[128,128]{1,0:T(8,128)}, f32[128,128]{1,0:T(8,128)S(1)}, u32[]{:S(2)}, u32[]{:S(2)}) collective-permute-start(f32[128,128]{1,0:T(8,128)} %get-tuple-element.47), channel_id=1, source_target_pairs={{0,8},{1,9},{2,10},{3,11},{4,12},{5,13},{6,14},{7,15},{8,0},{9,1},... | collective-permute-start | bytes 196616 | tf_op jit(solution)/shard_map/ppermute | solution.py:366
  70.0 21.6 %collective-permute-start.16 = (bf16[128,1024]{1,0:T(8,128)(2,1)}, bf16[128,1024]{1,0:T(8,128)(2,1)S(1)}, u32[]{:S(2)}, u32[]{:S(2)}) collective-permute-start(bf16[128,1024]{1,0:T(8,128)(2,1)} %get-tuple-element.43), channel_id=1, source_target_pairs={{0,8},{1,9},{2,10},{3,11},{4,12},{5,13},{6,14},{7,15},{8,0},{9,1},... | collective-permute-start | bytes 786440 | tf_op jit(solution)/shard_map/ppermute | solution.py:366
  93.3 16.4 %collective-permute-start.19 = (bf16[128,2176]{1,0:T(8,128)(2,1)S(1)}, bf16[128,2176]{1,0:T(8,128)(2,1)S(1)}, u32[]{:S(2)}, u32[]{:S(2)}) collective-permute-start(bf16[128,2176]{1,0:T(8,128)(2,1)S(1)} %pad_maximum_fusion.refs_0_), channel_id=1, source_target_pairs={{0,4},{1,5},{2,6},{3,7},{4,8},{5,9},{6,10},{7,11},{8,12},{9,13},{1... | collective-permute-start | bytes 1671176 | tf_op jit(solution)/shard_map/ppermute | solution.py:366
  110.3 16.6 %collective-permute-start.20 = (bf16[128,2176]{1,0:T(8,128)(2,1)S(1)}, bf16[128,2176]{1,0:T(8,128)(2,1)S(1)}, u32[]{:S(2)}, u32[]{:S(2)}) collective-permute-start(bf16[128,2176]{1,0:T(8,128)(2,1)S(1)} %collective-permute-done.19.refs_0_), channel_id=1, source_target_pairs={{0,1},{1,0},{2,3},{3,2},{4,5},{5,4},{6,7},{7,6},{8,9},{9,8},{10,11... | collective-permute-start | bytes 1671176 | tf_op jit(solution)/shard_map/ppermute | solution.py:363
  125.5 16.5 %collective-permute-start.28 = (bf16[128,2176]{1,0:T(8,128)(2,1)S(1)}, bf16[128,2176]{1,0:T(8,128)(2,1)S(1)}, u32[]{:S(2)}, u32[]{:S(2)}) collective-permute-start(bf16[128,2176]{1,0:T(8,128)(2,1)S(1)} %collective-permute-done.27.refs_0_), channel_id=1, source_target_pairs={{0,1},{1,0},{2,3},{3,2},{4,5},{5,4},{6,7},{7,6},{8,9},{9,8},{10,11... | collective-permute-start | bytes 1671176 | tf_op jit(solution)/shard_map/ppermute | solution.py:363
  141.9 17.3 %collective-permute-start.35 = (bf16[128,2176]{1,0:T(8,128)(2,1)S(1)}, bf16[128,2176]{1,0:T(8,128)(2,1)S(1)}, u32[]{:S(2)}, u32[]{:S(2)}) collective-permute-start(bf16[128,2176]{1,0:T(8,128)(2,1)S(1)} %collective-permute-done.27.refs_0_), channel_id=1, source_target_pairs={{0,4},{1,5},{2,6},{3,7},{4,8},{5,9},{6,10},{7,11},{8,12},{9,13},{1... | collective-permute-start | bytes 1671176 | tf_op jit(solution)/shard_map/ppermute | solution.py:366
  142.0 17.3 %collective-permute-start.23 = (bf16[128,2048]{1,0:T(8,128)(2,1)S(1)}, bf16[128,2048]{1,0:T(8,128)(2,1)S(1)}, u32[]{:S(2)}, u32[]{:S(2)}) collective-permute-start(bf16[128,2048]{1,0:T(8,128)(2,1)S(1)} %get-tuple-element.50), channel_id=1, source_target_pairs={{0,1},{1,0},{2,3},{3,2},{4,5},{5,4},{6,7},{7,6},{8,9},{9,8},{10,11... | collective-permute-start | bytes 1572872 | tf_op jit(solution)/shard_map/ppermute | solution.py:363
  142.7 27.7 %collective-permute-start.37 = (bf16[128,2176]{1,0:T(8,128)(2,1)S(1)}, bf16[128,2176]{1,0:T(8,128)(2,1)S(1)}, u32[]{:S(2)}, u32[]{:S(2)}) collective-permute-start(bf16[128,2176]{1,0:T(8,128)(2,1)S(1)} %collective-permute-done.29.refs_2_), channel_id=1, source_target_pairs={{0,4},{1,5},{2,6},{3,7},{4,8},{5,9},{6,10},{7,11},{8,12},{9,13},{1... | collective-permute-start | bytes 1671176 | tf_op jit(solution)/shard_map/ppermute | solution.py:366
  143.5 26.9 %collective-permute-start.25 = (bf16[128,2048]{1,0:T(8,128)(2,1)S(1)}, bf16[128,2048]{1,0:T(8,128)(2,1)S(1)}, u32[]{:S(2)}, u32[]{:S(2)}) collective-permute-start(bf16[128,2048]{1,0:T(8,128)(2,1)S(1)} %add_convert_fusion.13), channel_id=1, source_target_pairs={{0,2},{1,3},{2,0},{3,1},{4,6},{5,7},{6,4},{7,5},{8,10},{9,11},{10,... | collective-permute-start | bytes 1572872 | tf_op jit(solution)/shard_map/ppermute | solution.py:363
  159.2 26.1 %collective-permute-start.43 = (bf16[128,2176]{1,0:T(8,128)(2,1)S(1)}, bf16[128,2176]{1,0:T(8,128)(2,1)S(1)}, u32[]{:S(2)}, u32[]{:S(2)}) collective-permute-start(bf16[128,2176]{1,0:T(8,128)(2,1)S(1)} %pad_maximum_fusion.refs_0_), channel_id=1, source_target_pairs={{0,1},{1,0},{2,3},{3,2},{4,5},{5,4},{6,7},{7,6},{8,9},{9,8},{10,11... | collective-permute-start | bytes 1671176 | tf_op jit(solution)/shard_map/ppermute | solution.py:363
  159.3 26.2 %collective-permute-start.45 = (bf16[128,2176]{1,0:T(8,128)(2,1)S(1)}, bf16[128,2176]{1,0:T(8,128)(2,1)S(1)}, u32[]{:S(2)}, u32[]{:S(2)}) collective-permute-start(bf16[128,2176]{1,0:T(8,128)(2,1)S(1)} %collective-permute-done.44.refs_2_), channel_id=1, source_target_pairs={{0,1},{1,0},{2,3},{3,2},{4,5},{5,4},{6,7},{7,6},{8,9},{9,8},{10,11... | collective-permute-start | bytes 1671176 | tf_op jit(solution)/shard_map/ppermute | solution.py:363
  171.2 25.8 %collective-permute-start.31 = (bf16[128,2048]{1,0:T(8,128)(2,1)S(1)}, bf16[128,2048]{1,0:T(8,128)(2,1)S(1)}, u32[]{:S(2)}, u32[]{:S(2)}) collective-permute-start(bf16[128,2048]{1,0:T(8,128)(2,1)S(1)} %get-tuple-element.54), channel_id=1, source_target_pairs={{0,1},{1,0},{2,3},{3,2},{4,5},{5,4},{6,7},{7,6},{8,9},{9,8},{10,11... | collective-permute-start | bytes 1572872 | tf_op jit(solution)/shard_map/ppermute | solution.py:363
  172.4 24.7 %collective-permute-start.26 = (bf16[128,2048]{1,0:T(8,128)(2,1)S(1)}, bf16[128,2048]{1,0:T(8,128)(2,1)S(1)}, u32[]{:S(2)}, u32[]{:S(2)}) collective-permute-start(bf16[128,2048]{1,0:T(8,128)(2,1)S(1)} %add_convert_fusion.12), channel_id=1, source_target_pairs={{0,4},{1,5},{2,6},{3,7},{4,8},{5,9},{6,10},{7,11},{8,12},{9,13},{1... | collective-permute-start | bytes 1572872 | tf_op jit(solution)/shard_map/ppermute | solution.py:366
  173.2 23.9 %collective-permute-start.33 = (bf16[128,2048]{1,0:T(8,128)(2,1)S(1)}, bf16[128,2048]{1,0:T(8,128)(2,1)S(1)}, u32[]{:S(2)}, u32[]{:S(2)}) collective-permute-start(bf16[128,2048]{1,0:T(8,128)(2,1)S(1)} %add_convert_fusion.10), channel_id=1, source_target_pairs={{0,2},{1,3},{2,0},{3,1},{4,6},{5,7},{6,4},{7,5},{8,10},{9,11},{10,... | collective-permute-start | bytes 1572872 | tf_op jit(solution)/shard_map/ppermute | solution.py:363
  197.5 16.1 %collective-permute-start.34 = (bf16[128,2048]{1,0:T(8,128)(2,1)S(1)}, bf16[128,2048]{1,0:T(8,128)(2,1)S(1)}, u32[]{:S(2)}, u32[]{:S(2)}) collective-permute-start(bf16[128,2048]{1,0:T(8,128)(2,1)S(1)} %add_convert_fusion.8), channel_id=1, source_target_pairs={{0,4},{1,5},{2,6},{3,7},{4,8},{5,9},{6,10},{7,11},{8,12},{9,13},{1... | collective-permute-start | bytes 1572872 | tf_op jit(solution)/shard_map/ppermute | solution.py:366
  199.0 24.3 %collective-permute-start.48 = (bf16[128,2048]{1,0:T(8,128)(2,1)S(1)}, bf16[128,2048]{1,0:T(8,128)(2,1)S(1)}, u32[]{:S(2)}, u32[]{:S(2)}) collective-permute-start(bf16[128,2048]{1,0:T(8,128)(2,1)S(1)} %add_convert_fusion.2), channel_id=1, source_target_pairs={{0,2},{1,3},{2,0},{3,1},{4,6},{5,7},{6,4},{7,5},{8,10},{9,11},{10,... | collective-permute-start | bytes 1572872 | tf_op jit(solution)/shard_map/ppermute | solution.py:363
  (44 other events, 665.2 us)

commit v3 on v2

--- a/solution.py
+++ b/solution.py
@@ -247,12 +247,13 @@
 
 
 def expert_kernel(place, *refs, blocks, cap, slots):
-    x_refs = refs[:blocks]
-    gate_ref, up_ref, down_ref = refs[blocks : blocks + 3]
-    outs = refs[blocks + 3 : 2 * blocks + 3]
-    rows, total, combine, results = refs[2 * blocks + 3 :]
+    firsts, seconds, refs = refs[:blocks], refs[blocks : 2 * blocks], refs[2 * blocks :]
+    gate_ref, up_ref, down_ref = refs[:3]
+    outs = refs[3 : blocks + 3]
+    rows, total, combine, results = refs[blocks + 3 :]
     expert, part = pl.program_id(0), pl.program_id(1)
     tok, model = outs[0].shape
+    half = model // 2
     count = rows.shape[0]
     wide = count * cap
 
@@ -267,14 +268,15 @@
         earlier = jnp.where(across < below, 1.0, 0.0).astype(jnp.bfloat16)
         slot = (lax.broadcasted_iota(jnp.int32, (tok, wide), 1) % cap).astype(jnp.float32)
         for b in range(blocks):
-            weight = mm(x_refs[b][:, model : model + LANES], pick)
+            weight = mm(seconds[b][:, half : half + LANES], pick)
             chosen = weight > 0.0
             rank = mm(earlier, jnp.where(chosen, 1.0, 0.0).astype(jnp.bfloat16))
             match = jnp.logical_and(chosen, rank == slot)
             select = jnp.where(match, 1.0, 0.0).astype(jnp.bfloat16)
-            picked = mm(select, x_refs[b][:, :model], TN).astype(jnp.bfloat16)
-            for e in range(count):
-                rows[e, b * cap : (b + 1) * cap, :] = picked[e * cap : (e + 1) * cap]
+            for at, ref in ((0, firsts[b]), (half, seconds[b])):
+                picked = mm(select, ref[:, :half], TN).astype(jnp.bfloat16)
+                for e in range(count):
+                    rows[e, b * cap : (b + 1) * cap, at : at + half] = picked[e * cap : (e + 1) * cap]
             weight = jnp.where(match, weight, 0.0)
             high = weight.astype(jnp.bfloat16)
             low = (weight - high.astype(jnp.float32)).astype(jnp.bfloat16)
@@ -308,8 +310,8 @@
 
 
 def run_experts(xs, w_gate, w_up, w_down, place, cap, slots, parts):
-    blocks = len(xs)
-    tok, extended = xs[0].shape
+    blocks = len(xs) // 2
+    tok = xs[0].shape[0]
     count, model, hidden = w_gate.shape
     tile = hidden // parts
     cost = pl.CostEstimate(
@@ -323,7 +325,7 @@
         grid_spec=pltpu.PrefetchScalarGridSpec(
             num_scalar_prefetch=1,
             grid=(count, parts),
-            in_specs=[pl.BlockSpec((tok, extended), lambda e, f, place: (0, 0))] * blocks
+            in_specs=[pl.BlockSpec(x.shape, lambda e, f, place: (0, 0)) for x in xs]
             + [
                 pl.BlockSpec((1, model, tile), lambda e, f, place: (e, 0, f)),
                 pl.BlockSpec((1, model, tile), lambda e, f, place: (e, 0, f)),
@@ -337,7 +339,7 @@
                 pltpu.VMEM((blocks, 2 * count * cap, model), jnp.bfloat16),
             ],
         ),
-        compiler_params=pltpu.CompilerParams(vmem_limit_bytes=40 * 1024 * 1024),
+        compiler_params=pltpu.CompilerParams(vmem_limit_bytes=46 * 1024 * 1024),
         cost_estimate=cost,
         name="experts",
     )(place, *xs, w_gate, w_up, w_down)
@@ -358,6 +360,7 @@
     tokens = head_in.shape[0]
     tok = tokens // devices
     width = head_in.shape[1]
+    model = out_proj.shape[1]
 
     def cross(x, mask):
         return lax.ppermute(x, "mix", [(i, i ^ mask) for i in range(devices)])
@@ -414,24 +417,43 @@
     normed = (
         hidden * lax.rsqrt(jnp.mean(hidden * hidden, axis=1, keepdims=True) + epsilon) * moe_gain
     ).astype(jnp.bfloat16)
-    mine = jnp.concatenate([normed, table], axis=1)
+    mine = [normed[:, : model // 2], jnp.concatenate([normed[:, model // 2 :], table], axis=1)]
 
     cap = 2 * tok * expert_ids.shape[1] // slots
+    both = (0, 1)
+    cut = model // 2 + LANES
+    sides = (slice(0, cut), slice(cut, model))
     sums = []
     for dz in range(depth):
         if dz > 0:
-            mine = onward(mine)
-        other = cross(mine, 2) if dz < depth - 1 else onward(other)
-        block = [mine, cross(mine, 1), other, cross(other, 1)]
+            mine = [onward(mine[h]) for h in both]
+        if dz < depth - 1:
+            other = [cross(mine[h], 2) for h in both]
+        else:
+            other = [onward(other[h]) for h in both]
+        block = []
+        for h in both:
+            block += [mine[h], cross(mine[h], 1)]
+            block += [other[h], cross(other[h], 1)]
         outs = run_experts(block, w_gate, w_up, w_down, place, cap, slots, 1)
-        near = add_low(outs[0], cross(outs[1], 1))
-        far = add_low(outs[2], cross(outs[3], 1))
-        sums.append(add_low(near, cross(far, 2)))
-    total = sums[1]
-    for dz in range(2, depth):
-        total = add_low(onward(total), sums[dz])
-    expert_sum = onward(total).astype(jnp.float32) + sums[0].astype(jnp.float32)
-    return (hidden + expert_sum).astype(jnp.bfloat16)
+        near_c, far_c = cross(outs[1], 1), cross(outs[3], 1)
+        parts = []
+        for h in both:
+            columns = sides[h]
+            near = add_low(outs[0][:, columns], near_c[:, columns])
+            far = add_low(outs[2][:, columns], far_c[:, columns])
+            far = cross(far, 2)
+            parts.append(add_low(near, far))
+        sums.append(parts)
+    results = []
+    for h in both:
+        total = sums[1][h]
+        for dz in range(2, depth):
+            total = onward(total)
+            total = add_low(total, sums[dz][h])
+        expert_sum = onward(total).astype(jnp.float32) + sums[0][h].astype(jnp.float32)
+        results.append(hidden[:, sides[h]] + expert_sum)
+    return jnp.concatenate(results, axis=1).astype(jnp.bfloat16)
 
 
 def solution(mesh):

time: 231 us -> 245 us (1.061)
  starting transfers between devices: 28.8 us -> 55.8 us
  waiting for transfers between devices: 114 us -> 99.6 us
  Pallas kernels: 67.9 us -> 71.2 us
    ppermute x10 -> x17, waiting for transfers between devices: 68.9 us -> 37.9 us  [onward(): lax.ppermute(x, 'mix', [(i, (i + stride) % devices) for i in range(device...]
    ppermute x39 -> x54, waiting for transfers between devices: 44.9 us -> 61.7 us  [cross(): return lax.ppermute(x, 'mix', [(i, i ^ mask) for i in range(devices)])]
    ppermute x10 -> x17, starting transfers between devices: 5.88 us -> 22.4 us  [onward(): lax.ppermute(x, 'mix', [(i, (i + stride) % devices) for i in range(device...]
    ppermute x39 -> x54, starting transfers between devices: 22.9 us -> 33.4 us  [cross(): return lax.ppermute(x, 'mix', [(i, i ^ mask) for i in range(devices)])]
    pallas_call x4, Pallas kernels: 44.1 us -> 47.4 us  [run_experts(): pl.pallas_call(functools.partial(expert_kernel, blocks=blocks, cap=cap, s...]
  transfers between devices with their start and end apart: 49 -> 71, of which waited for: 20 -> 20; matrix products, arithmetic and copies ran while one was open for 6% -> 5% of each run, Pallas kernels for 28% -> 27%
where the time goes in v3:
time: 245 us
  waiting for transfers between devices  99.6 us (41%)
  Pallas kernels  71.2 us (29%)
  starting transfers between devices  55.8 us (23%)
  other arithmetic  10 us (4%)
  local copies, waits for them, and re-layouts  7.41 us (3%)
    ppermute x54, waiting for transfers between devices, cross(): return lax.ppermute(x, 'mix', [(i, i ^ mask) for i in range(devices)])  61.7 us
    pallas_call x4, Pallas kernels, run_experts(): pl.pallas_call(functools.partial(expert_kernel, blocks=blocks, cap=cap, s...  47.4 us
    ppermute x17, waiting for transfers between devices, onward(): lax.ppermute(x, 'mix', [(i, (i + stride) % devices) for i in range(device...  37.9 us
    ppermute x54, starting transfers between devices, cross(): return lax.ppermute(x, 'mix', [(i, i ^ mask) for i in range(devices)])  33.4 us
    ppermute x17, starting transfers between devices, onward(): lax.ppermute(x, 'mix', [(i, (i + stride) % devices) for i in range(device...  22.4 us
    pallas_call x1, Pallas kernels, scan_heads(): pl.pallas_call(functools.partial(scan_kernel, span=span, chunks=chunks),...  14.6 us
    pallas_call x2, Pallas kernels, project(): pl.pallas_call(functools.partial(project_kernel, depth=depth, squared=squ...  9.2 us
  transfers between devices with their start and end apart: 71, of which 20 were waited for; matrix products, arithmetic and copies ran while one was open for 5% of the time, Pallas kernels for 27%

profile of v3, /device:TPU:0, one launch (start us, length us, event | category | flops | bytes accessed | tf_op | source)
XLA Modules:
  0.0 244.6 jit_solution(36422324054581797)
XLA Ops:
  0.0 3.1 %collective-permute-start.10 = (bf16[256,2048]{1,0:T(8,128)(2,1)}, bf16[256,2048]{1,0:T(8,128)(2,1)S(1)}, u32[]{:S(2)}, u32[]{:S(2)}) collective-permute-start(bf16[256,2048]{1,0:T(8,128)(2,1)} %refs_9_.7), channel_id=1, source_target_pairs={{0,4},{1,5},{2,6},{3,7},{4,0},{5,1},{6,2},{7,3},{8,12},{9,13},{10,... | collective-permute-start | bytes 3145736 | tf_op jit(solution)/shard_map/ppermute | solution.py:366
  4.6 14.6 %scan.1 = (bf16[2,128,256]{2,1,0:T(8,128)(2,1)}, bf16[2,128,256]{2,1,0:T(8,128)(2,1)}, bf16[2,128,256]{2,1,0:T(8,128)(2,1)}, bf16[2,128,256]{2,1,0:T(8,128)(2,1)...) custom-call(s32[8]{0:T(128)} %lengths.1, ...), custom_call_target="tpu_custom_call" | custom-call | flops 939524096 | bytes 3145728 | tf_op jit(solution)/shard_map/scan/pallas_call | solution.py:165
  21.6 10.5 %collective-permute-done.1.refs_3_ = bf16[2,128,256]{2,1,0:T(8,128)(2,1)S(1)} collective-permute-done((bf16[2,128,256]{2,1,0:T(8,128)(2,1)}, bf16[2,128,256]{2,1,0:T(8,128)(2,1)S(1)}, u32[]{:S(2)}, u32[]{:S(2)}) %collective-permute-start.1) | collective-permute-done | bytes 131104 | tf_op jit(solution)/shard_map/ppermute | solution.py:366
  41.9 2.9 %collective-permute-done.6.refs_8_ = bf16[2,128,256]{2,1,0:T(8,128)(2,1)S(1)} collective-permute-done((bf16[2,128,256]{2,1,0:T(8,128)(2,1)}, bf16[2,128,256]{2,1,0:T(8,128)(2,1)S(1)}, u32[]{:S(2)}, u32[]{:S(2)}) %collective-permute-start.6) | collective-permute-done | bytes 131104 | tf_op jit(solution)/shard_map/ppermute | solution.py:366
  51.6 3.5 %collective-permute-done.14.refs_17_ = bf16[128,2048]{1,0:T(8,128)(2,1)} collective-permute-done((bf16[128,2048]{1,0:T(8,128)(2,1)}, bf16[128,2048]{1,0:T(8,128)(2,1)}, u32[]{:S(2)}, u32[]{:S(2)}) %collective-permute-start.14) | collective-permute-done | bytes 524320 | tf_op jit(solution)/shard_map/ppermute | solution.py:366
  59.5 4.4 %project.3 = (bf16[128,1024]{1,0:T(8,128)(2,1)}, bf16[128,1024]{1,0:T(8,128)(2,1)}) custom-call(f32[8,256]{1,0:T(8,128)} %broadcast_select_fusion.refs_0_, bf16[2,128,256]{2,1,0:T(8,128)(2,1)} %get-tuple-element.35.refs_1_, bf16[2,128,256]{2,1,0:T(8,128)(2,1)} %copy-done.5, bf16[2,128,256]{2,1,0:T(8,128)(2,1)} %copy-done.6, bf16[2,128,256]{2,1,0:T(8,128)(2,1)} %copy-done.7, ...), custom_call_target="tpu_custom_call" | custom-call | flops 1073741824 | bytes 5242880 | tf_op jit(solution)/shard_map/project/pallas_call | solution.py:235
  66.7 4.8 %project.2 = (bf16[128,1024]{1,0:T(8,128)(2,1)}, bf16[128,1024]{1,0:T(8,128)(2,1)}, f32[128,128]{1,0:T(8,128)}, f32[128,128]{1,0:T(8,128)}) custom-call(f32[8,256]{1,0:T(8,128)} %broadcast_select_fusion.refs_0_, bf16[2,128,256]{2,1,0:T(8,128)(2,1)} %get-tuple-element.35.refs_1_, bf16[2,128,256]{2,1,0:T(8,128)(2,1)} %copy-done.5, ...), custom_call_target="tpu_custom_call" | custom-call | flops 1073741824 | bytes 5242880 | tf_op jit(solution)/shard_map/project/pallas_call | solution.py:235
  74.6 13.8 %collective-permute-done.18 = f32[128,128]{1,0:T(8,128)S(1)} collective-permute-done((f32[128,128]{1,0:T(8,128)}, f32[128,128]{1,0:T(8,128)S(1)}, u32[]{:S(2)}, u32[]{:S(2)}) %collective-permute-start.18) | collective-permute-done | bytes 65568 | tf_op jit(solution)/shard_map/ppermute | solution.py:369
  89.4 3.7 %collective-permute-done.16 = bf16[128,1024]{1,0:T(8,128)(2,1)S(1)} collective-permute-done((bf16[128,1024]{1,0:T(8,128)(2,1)}, bf16[128,1024]{1,0:T(8,128)(2,1)S(1)}, u32[]{:S(2)}, u32[]{:S(2)}) %collective-permute-start.16) | collective-permute-done | bytes 262176 | tf_op jit(solution)/shard_map/ppermute | solution.py:369
  97.6 12.1 %collective-permute-done.56.refs_2_ = bf16[128,1024]{1,0:T(8,128)(2,1)S(1)} collective-permute-done((bf16[128,1024]{1,0:T(8,128)(2,1)S(1)}, bf16[128,1024]{1,0:T(8,128)(2,1)S(1)}, u32[]{:S(2)}, u32[]{:S(2)}) %collective-permute-start.56) | collective-permute-done | bytes 262176 | tf_op jit(solution)/shard_map/ppermute | solution.py:366
  112.8 12.0 %collective-permute-done.21.refs_2_ = bf16[128,1024]{1,0:T(8,128)(2,1)S(1)} collective-permute-done((bf16[128,1024]{1,0:T(8,128)(2,1)S(1)}, bf16[128,1024]{1,0:T(8,128)(2,1)S(1)}, u32[]{:S(2)}, u32[]{:S(2)}) %collective-permute-start.21) | collective-permute-done | bytes 262176 | tf_op jit(solution)/shard_map/ppermute | solution.py:366
  125.2 11.9 %experts.7 = (bf16[128,2048]{1,0:T(8,128)(2,1)S(1)}, bf16[128,2048]{1,0:T(8,128)(2,1)S(1)}, bf16[128,2048]{1,0:T(8,128)(2,1)S(1)}, bf16[128,2048]{1,0:T(8,128)(2,1)S(1)}) custom-call(s32[1]{0:T(128)} %bitcast.1.place, bf16[128,1024]{1,0:T(8,128)(2,1)S(1)} %get-tuple-element.68.refs_0_, bf16[128,1024]{1,0:T(8,128)(2,1)S(1)} %collective-permute-done.55.refs_1_, ...), custom_call_target="tpu_custom_call" | custom-call | flops 4831838208 | bytes 23068672 | tf_op jit(solution)/shard_map/experts/pallas_call | solution.py:322
  137.6 3.5 %collective-permute-start.35 = (bf16[128,1152]{1,0:T(8,128)(2,1)S(1)}, bf16[128,1152]{1,0:T(8,128)(2,1)S(1)}, u32[]{:S(2)}, u32[]{:S(2)}) collective-permute-start(bf16[128,1152]{1,0:T(8,128)(2,1)S(1)} %collective-permute-done.23.refs_4_), channel_id=1, source_target_pairs={{0,4},{1,5},{2,6},{3,7},{4,8},{5,9},{6,10},{7,11},{8,12},{9,13},{1... | collective-permute-start | bytes 884744 | tf_op jit(solution)/shard_map/ppermute | solution.py:369
  141.1 11.9 %experts.4 = (bf16[128,2048]{1,0:T(8,128)(2,1)S(1)}, bf16[128,2048]{1,0:T(8,128)(2,1)S(1)}, bf16[128,2048]{1,0:T(8,128)(2,1)S(1)}, bf16[128,2048]{1,0:T(8,128)(2,1)S(1)}) custom-call(s32[1]{0:T(128)} %bitcast.1.place, bf16[128,1024]{1,0:T(8,128)(2,1)S(1)} %collective-permute-done.19.refs_0_, bf16[128,1024]{1,0:T(8,128)(2,1)S(1)} %collective-permute-done.20.refs_1_, ...), custom_call_target="tpu_custom_call" | custom-call | flops 4831838208 | bytes 23068672 | tf_op jit(solution)/shard_map/experts/pallas_call | solution.py:322
  155.7 7.0 %collective-permute-done.33.refs_2_ = bf16[128,1024]{1,0:T(8,128)(2,1)S(1)} collective-permute-done((bf16[128,1024]{1,0:T(8,128)(2,1)S(1)}, bf16[128,1024]{1,0:T(8,128)(2,1)S(1)}, u32[]{:S(2)}, u32[]{:S(2)}) %collective-permute-start.33) | collective-permute-done | bytes 262176 | tf_op jit(solution)/shard_map/ppermute | solution.py:366
  162.7 5.5 %collective-permute-done.37.refs_6_ = bf16[128,1152]{1,0:T(8,128)(2,1)S(1)} collective-permute-done((bf16[128,1152]{1,0:T(8,128)(2,1)S(1)}, bf16[128,1152]{1,0:T(8,128)(2,1)S(1)}, u32[]{:S(2)}, u32[]{:S(2)}) %collective-permute-start.37) | collective-permute-done | bytes 294944 | tf_op jit(solution)/shard_map/ppermute | solution.py:366
  172.1 11.9 %experts.5 = (bf16[128,2048]{1,0:T(8,128)(2,1)S(1)}, bf16[128,2048]{1,0:T(8,128)(2,1)S(1)}, bf16[128,2048]{1,0:T(8,128)(2,1)S(1)}, bf16[128,2048]{1,0:T(8,128)(2,1)S(1)}) custom-call(s32[1]{0:T(128)} %bitcast.1.place, bf16[128,1024]{1,0:T(8,128)(2,1)S(1)} %collective-permute-done.31.refs_0_, bf16[128,1024]{1,0:T(8,128)(2,1)S(1)} %collective-permute-done.32.refs_1_, ...), custom_call_target="tpu_custom_call" | custom-call | flops 4831838208 | bytes 23068672 | tf_op jit(solution)/shard_map/experts/pallas_call | solution.py:322
  184.7 3.5 %collective-permute-start.49 = (bf16[128,1152]{1,0:T(8,128)(2,1)S(1)}, bf16[128,1152]{1,0:T(8,128)(2,1)S(1)}, u32[]{:S(2)}, u32[]{:S(2)}) collective-permute-start(bf16[128,1152]{1,0:T(8,128)(2,1)S(1)} %collective-permute-done.37.refs_6_), channel_id=1, source_target_pairs={{0,4},{1,5},{2,6},{3,7},{4,8},{5,9},{6,10},{7,11},{8,12},{9,13},{1... | collective-permute-start | bytes 884744 | tf_op jit(solution)/shard_map/ppermute | solution.py:369
  188.9 6.7 %collective-permute-done.49.refs_6_ = bf16[128,1152]{1,0:T(8,128)(2,1)S(1)} collective-permute-done((bf16[128,1152]{1,0:T(8,128)(2,1)S(1)}, bf16[128,1152]{1,0:T(8,128)(2,1)S(1)}, u32[]{:S(2)}, u32[]{:S(2)}) %collective-permute-start.49) | collective-permute-done | bytes 294944 | tf_op jit(solution)/shard_map/ppermute | solution.py:369
  200.4 11.9 %experts.6 = (bf16[128,2048]{1,0:T(8,128)(2,1)S(1)}, bf16[128,2048]{1,0:T(8,128)(2,1)S(1)}, bf16[128,2048]{1,0:T(8,128)(2,1)S(1)}, bf16[128,2048]{1,0:T(8,128)(2,1)S(1)}) custom-call(s32[1]{0:T(128)} %bitcast.1.place, bf16[128,1024]{1,0:T(8,128)(2,1)S(1)} %collective-permute-done.43.refs_0_, bf16[128,1024]{1,0:T(8,128)(2,1)S(1)} %collective-permute-done.44.refs_1_, ...), custom_call_target="tpu_custom_call" | custom-call | flops 4831838208 | bytes 23068672 | tf_op jit(solution)/shard_map/experts/pallas_call | solution.py:322
  218.6 4.7 %collective-permute-done.67 = bf16[128,896]{1,0:T(8,128)(2,1)S(1)} collective-permute-done((bf16[128,896]{1,0:T(8,128)(2,1)S(1)}, bf16[128,896]{1,0:T(8,128)(2,1)S(1)}, u32[]{:S(2)}, u32[]{:S(2)}) %collective-permute-start.67) | collective-permute-done | bytes 229408 | tf_op jit(solution)/shard_map/ppermute | solution.py:369
  225.5 3.2 %collective-permute-done.42 = bf16[128,1152]{1,0:T(8,128)(2,1)S(1)} collective-permute-done((bf16[128,1152]{1,0:T(8,128)(2,1)S(1)}, bf16[128,1152]{1,0:T(8,128)(2,1)S(1)}, u32[]{:S(2)}, u32[]{:S(2)}) %collective-permute-start.42) | collective-permute-done | bytes 294944 | tf_op jit(solution)/shard_map/ppermute | solution.py:369
  232.9 3.0 %collective-permute-done.70 = bf16[128,896]{1,0:T(8,128)(2,1)S(1)} collective-permute-done((bf16[128,896]{1,0:T(8,128)(2,1)S(1)}, bf16[128,896]{1,0:T(8,128)(2,1)S(1)}, u32[]{:S(2)}, u32[]{:S(2)}) %collective-permute-start.70) | collective-permute-done | bytes 229408 | tf_op jit(solution)/shard_map/ppermute | solution.py:366
  235.9 3.0 %collective-permute-done.69 = bf16[128,896]{1,0:T(8,128)(2,1)S(1)} collective-permute-done((bf16[128,896]{1,0:T(8,128)(2,1)S(1)}, bf16[128,896]{1,0:T(8,128)(2,1)S(1)}, u32[]{:S(2)}, u32[]{:S(2)}) %collective-permute-start.69) | collective-permute-done | bytes 229408 | tf_op jit(solution)/shard_map/ppermute | solution.py:369
  (203 shorter events, 71.0 us)
Async XLA Ops:
  0.0 32.2 %collective-permute-start.10 = (bf16[256,2048]{1,0:T(8,128)(2,1)}, bf16[256,2048]{1,0:T(8,128)(2,1)S(1)}, u32[]{:S(2)}, u32[]{:S(2)}) collective-permute-start(bf16[256,2048]{1,0:T(8,128)(2,1)} %refs_9_.7), channel_id=1, source_target_pairs={{0,4},{1,5},{2,6},{3,7},{4,0},{5,1},{6,2},{7,3},{8,12},{9,13},{10,... | collective-permute-start | bytes 3145736 | tf_op jit(solution)/shard_map/ppermute | solution.py:366
  3.1 30.5 %collective-permute-start.8 = (bf16[256,2048]{1,0:T(8,128)(2,1)}, bf16[256,2048]{1,0:T(8,128)(2,1)S(1)}, u32[]{:S(2)}, u32[]{:S(2)}) collective-permute-start(bf16[256,2048]{1,0:T(8,128)(2,1)} %refs_9_.7), channel_id=1, source_target_pairs={{0,2},{1,3},{2,0},{3,1},{4,6},{5,7},{6,4},{7,5},{8,10},{9,11},{10,... | collective-permute-start | bytes 3145736 | tf_op jit(solution)/shard_map/ppermute | solution.py:366
  19.9 16.7 %collective-permute-start.2 = (bf16[2,128,256]{2,1,0:T(8,128)(2,1)}, bf16[2,128,256]{2,1,0:T(8,128)(2,1)S(1)}, u32[]{:S(2)}, u32[]{:S(2)}) collective-permute-start(bf16[2,128,256]{2,1,0:T(8,128)(2,1)} %get-tuple-element.38), channel_id=1, source_target_pairs={{0,3},{1,2},{2,1},{3,0},{4,7},{5,6},{6,5},{7,4},{8,11},{9,10},{10,... | collective-permute-start | bytes 393224 | tf_op jit(solution)/shard_map/ppermute | solution.py:366
  21.2 17.0 %collective-permute-start.3 = (bf16[2,128,256]{2,1,0:T(8,128)(2,1)}, bf16[2,128,256]{2,1,0:T(8,128)(2,1)S(1)}, u32[]{:S(2)}, u32[]{:S(2)}) collective-permute-start(bf16[2,128,256]{2,1,0:T(8,128)(2,1)} %get-tuple-element.39), channel_id=1, source_target_pairs={{0,4},{1,5},{2,6},{3,7},{4,0},{5,1},{6,2},{7,3},{8,12},{9,13},{10,... | collective-permute-start | bytes 393224 | tf_op jit(solution)/shard_map/ppermute | solution.py:366
  36.6 18.5 %collective-permute-start.14 = (bf16[128,2048]{1,0:T(8,128)(2,1)}, bf16[128,2048]{1,0:T(8,128)(2,1)}, u32[]{:S(2)}, u32[]{:S(2)}) collective-permute-start(bf16[128,2048]{1,0:T(8,128)(2,1)} %slice.159), channel_id=1, source_target_pairs={{0,2},{1,3},{2,0},{3,1},{4,6},{5,7},{6,4},{7,5},{8,10},{9,11},{10,... | collective-permute-start | bytes 1572872 | tf_op jit(solution)/shard_map/ppermute | solution.py:366
  38.2 17.0 %collective-permute-start.12 = (bf16[128,2048]{1,0:T(8,128)(2,1)}, bf16[128,2048]{1,0:T(8,128)(2,1)}, u32[]{:S(2)}, u32[]{:S(2)}) collective-permute-start(bf16[128,2048]{1,0:T(8,128)(2,1)} %slice.158), channel_id=1, source_target_pairs={{0,4},{1,5},{2,6},{3,7},{4,0},{5,1},{6,2},{7,3},{8,12},{9,13},{10,... | collective-permute-start | bytes 1572872 | tf_op jit(solution)/shard_map/ppermute | solution.py:366
  39.8 18.8 %collective-permute-start.7 = (bf16[256,2048]{1,0:T(8,128)(2,1)S(1)}, bf16[256,2048]{1,0:T(8,128)(2,1)}, u32[]{:S(2)}, u32[]{:S(2)}) collective-permute-start(bf16[256,2048]{1,0:T(8,128)(2,1)S(1)} %copy-done.2), channel_id=1, source_target_pairs={{0,1},{1,0},{2,3},{3,2},{4,5},{5,4},{6,7},{7,6},{8,9},{9,8},{10,11... | collective-permute-start | bytes 3145736 | tf_op jit(solution)/shard_map/ppermute | solution.py:366
  40.0 18.6 %collective-permute-start.11 = (bf16[256,2048]{1,0:T(8,128)(2,1)S(1)}, bf16[256,2048]{1,0:T(8,128)(2,1)}, u32[]{:S(2)}, u32[]{:S(2)}) collective-permute-start(bf16[256,2048]{1,0:T(8,128)(2,1)S(1)} %collective-permute-done.10.refs_13_), channel_id=1, source_target_pairs={{0,1},{1,0},{2,3},{3,2},{4,5},{5,4},{6,7},{7,6},{8,9},{9,8},{10,11... | collective-permute-start | bytes 3145736 | tf_op jit(solution)/shard_map/ppermute | solution.py:366
  64.0 25.3 %collective-permute-start.17 = (bf16[128,1024]{1,0:T(8,128)(2,1)}, bf16[128,1024]{1,0:T(8,128)(2,1)S(1)}, u32[]{:S(2)}, u32[]{:S(2)}) collective-permute-start(bf16[128,1024]{1,0:T(8,128)(2,1)} %get-tuple-element.45), channel_id=1, source_target_pairs={{0,8},{1,9},{2,10},{3,11},{4,12},{5,13},{6,14},{7,15},{8,0},{9,1},... | collective-permute-start | bytes 786440 | tf_op jit(solution)/shard_map/ppermute | solution.py:369
  71.5 16.9 %collective-permute-start.18 = (f32[128,128]{1,0:T(8,128)}, f32[128,128]{1,0:T(8,128)S(1)}, u32[]{:S(2)}, u32[]{:S(2)}) collective-permute-start(f32[128,128]{1,0:T(8,128)} %get-tuple-element.47), channel_id=1, source_target_pairs={{0,8},{1,9},{2,10},{3,11},{4,12},{5,13},{6,14},{7,15},{8,0},{9,1},... | collective-permute-start | bytes 196616 | tf_op jit(solution)/shard_map/ppermute | solution.py:369
  71.9 21.2 %collective-permute-start.16 = (bf16[128,1024]{1,0:T(8,128)(2,1)}, bf16[128,1024]{1,0:T(8,128)(2,1)S(1)}, u32[]{:S(2)}, u32[]{:S(2)}) collective-permute-start(bf16[128,1024]{1,0:T(8,128)(2,1)} %get-tuple-element.43), channel_id=1, source_target_pairs={{0,8},{1,9},{2,10},{3,11},{4,12},{5,13},{6,14},{7,15},{8,0},{9,1},... | collective-permute-start | bytes 786440 | tf_op jit(solution)/shard_map/ppermute | solution.py:369
  112.2 25.0 %collective-permute-start.20 = (bf16[128,1024]{1,0:T(8,128)(2,1)S(1)}, bf16[128,1024]{1,0:T(8,128)(2,1)S(1)}, u32[]{:S(2)}, u32[]{:S(2)}) collective-permute-start(bf16[128,1024]{1,0:T(8,128)(2,1)S(1)} %collective-permute-done.19.refs_0_), channel_id=1, source_target_pairs={{0,1},{1,0},{2,3},{3,2},{4,5},{5,4},{6,7},{7,6},{8,9},{9,8},{10,11... | collective-permute-start | bytes 786440 | tf_op jit(solution)/shard_map/ppermute | solution.py:366
  112.3 25.3 %collective-permute-start.24 = (bf16[128,1152]{1,0:T(8,128)(2,1)S(1)}, bf16[128,1152]{1,0:T(8,128)(2,1)S(1)}, u32[]{:S(2)}, u32[]{:S(2)}) collective-permute-start(bf16[128,1152]{1,0:T(8,128)(2,1)S(1)} %collective-permute-done.23.refs_4_), channel_id=1, source_target_pairs={{0,1},{1,0},{2,3},{3,2},{4,5},{5,4},{6,7},{7,6},{8,9},{9,8},{10,11... | collective-permute-start | bytes 884744 | tf_op jit(solution)/shard_map/ppermute | solution.py:366
  124.7 16.4 %collective-permute-start.22 = (bf16[128,1024]{1,0:T(8,128)(2,1)S(1)}, bf16[128,1024]{1,0:T(8,128)(2,1)S(1)}, u32[]{:S(2)}, u32[]{:S(2)}) collective-permute-start(bf16[128,1024]{1,0:T(8,128)(2,1)S(1)} %collective-permute-done.21.refs_2_), channel_id=1, source_target_pairs={{0,1},{1,0},{2,3},{3,2},{4,5},{5,4},{6,7},{7,6},{8,9},{9,8},{10,11... | collective-permute-start | bytes 786440 | tf_op jit(solution)/shard_map/ppermute | solution.py:366
  124.7 16.4 %collective-permute-start.26 = (bf16[128,1152]{1,0:T(8,128)(2,1)S(1)}, bf16[128,1152]{1,0:T(8,128)(2,1)S(1)}, u32[]{:S(2)}, u32[]{:S(2)}) collective-permute-start(bf16[128,1152]{1,0:T(8,128)(2,1)S(1)} %collective-permute-done.25.refs_6_), channel_id=1, source_target_pairs={{0,1},{1,0},{2,3},{3,2},{4,5},{5,4},{6,7},{7,6},{8,9},{9,8},{10,11... | collective-permute-start | bytes 884744 | tf_op jit(solution)/shard_map/ppermute | solution.py:366
  137.1 17.0 %collective-permute-start.62 = (bf16[128,2048]{1,0:T(8,128)(2,1)S(1)}, bf16[128,2048]{1,0:T(8,128)(2,1)S(1)}, u32[]{:S(2)}, u32[]{:S(2)}) collective-permute-start(bf16[128,2048]{1,0:T(8,128)(2,1)S(1)} %get-tuple-element.64), channel_id=1, source_target_pairs={{0,1},{1,0},{2,3},{3,2},{4,5},{5,4},{6,7},{7,6},{8,9},{9,8},{10,11... | collective-permute-start | bytes 1572872 | tf_op jit(solution)/shard_map/ppermute | solution.py:366
  137.2 15.9 %collective-permute-start.31 = (bf16[128,1024]{1,0:T(8,128)(2,1)S(1)}, bf16[128,1024]{1,0:T(8,128)(2,1)S(1)}, u32[]{:S(2)}, u32[]{:S(2)}) collective-permute-start(bf16[128,1024]{1,0:T(8,128)(2,1)S(1)} %collective-permute-done.19.refs_0_), channel_id=1, source_target_pairs={{0,4},{1,5},{2,6},{3,7},{4,8},{5,9},{6,10},{7,11},{8,12},{9,13},{1... | collective-permute-start | bytes 786440 | tf_op jit(solution)/shard_map/ppermute | solution.py:369
  137.6 16.5 %collective-permute-start.35 = (bf16[128,1152]{1,0:T(8,128)(2,1)S(1)}, bf16[128,1152]{1,0:T(8,128)(2,1)S(1)}, u32[]{:S(2)}, u32[]{:S(2)}) collective-permute-start(bf16[128,1152]{1,0:T(8,128)(2,1)S(1)} %collective-permute-done.23.refs_4_), channel_id=1, source_target_pairs={{0,4},{1,5},{2,6},{3,7},{4,8},{5,9},{6,10},{7,11},{8,12},{9,13},{1... | collective-permute-start | bytes 884744 | tf_op jit(solution)/shard_map/ppermute | solution.py:369
  169.7 18.5 %collective-permute-start.45 = (bf16[128,1024]{1,0:T(8,128)(2,1)S(1)}, bf16[128,1024]{1,0:T(8,128)(2,1)S(1)}, u32[]{:S(2)}, u32[]{:S(2)}) collective-permute-start(bf16[128,1024]{1,0:T(8,128)(2,1)S(1)} %collective-permute-done.33.refs_2_), channel_id=1, source_target_pairs={{0,4},{1,5},{2,6},{3,7},{4,8},{5,9},{6,10},{7,11},{8,12},{9,13},{1... | collective-permute-start | bytes 786440 | tf_op jit(solution)/shard_map/ppermute | solution.py:369
  170.7 17.5 %collective-permute-start.29 = (bf16[128,1152]{1,0:T(8,128)(2,1)S(1)}, bf16[128,1152]{1,0:T(8,128)(2,1)S(1)}, u32[]{:S(2)}, u32[]{:S(2)}) collective-permute-start(bf16[128,1152]{1,0:T(8,128)(2,1)S(1)} %add_convert_fusion.12), channel_id=1, source_target_pairs={{0,2},{1,3},{2,0},{3,1},{4,6},{5,7},{6,4},{7,5},{8,10},{9,11},{10,... | collective-permute-start | bytes 884744 | tf_op jit(solution)/shard_map/ppermute | solution.py:366
  195.5 16.7 %collective-permute-start.39 = (bf16[128,2048]{1,0:T(8,128)(2,1)S(1)}, bf16[128,2048]{1,0:T(8,128)(2,1)S(1)}, u32[]{:S(2)}, u32[]{:S(2)}) collective-permute-start(bf16[128,2048]{1,0:T(8,128)(2,1)S(1)} %get-tuple-element.54), channel_id=1, source_target_pairs={{0,1},{1,0},{2,3},{3,2},{4,5},{5,4},{6,7},{7,6},{8,9},{9,8},{10,11... | collective-permute-start | bytes 1572872 | tf_op jit(solution)/shard_map/ppermute | solution.py:366
  196.2 16.1 %collective-permute-start.65 = (bf16[128,896]{1,0:T(8,128)(2,1)S(1)}, bf16[128,896]{1,0:T(8,128)(2,1)S(1)}, u32[]{:S(2)}, u32[]{:S(2)}) collective-permute-start(bf16[128,896]{1,0:T(8,128)(2,1)S(1)} %add_convert_fusion.25), channel_id=1, source_target_pairs={{0,4},{1,5},{2,6},{3,7},{4,8},{5,9},{6,10},{7,11},{8,12},{9,13},{1... | collective-permute-start | bytes 688136 | tf_op jit(solution)/shard_map/ppermute | solution.py:369
  198.0 15.8 %collective-permute-start.30 = (bf16[128,1152]{1,0:T(8,128)(2,1)S(1)}, bf16[128,1152]{1,0:T(8,128)(2,1)S(1)}, u32[]{:S(2)}, u32[]{:S(2)}) collective-permute-start(bf16[128,1152]{1,0:T(8,128)(2,1)S(1)} %add_convert_fusion.11), channel_id=1, source_target_pairs={{0,4},{1,5},{2,6},{3,7},{4,8},{5,9},{6,10},{7,11},{8,12},{9,13},{1... | collective-permute-start | bytes 884744 | tf_op jit(solution)/shard_map/ppermute | solution.py:369
  224.7 16.1 %collective-permute-start.63 = (bf16[128,1152]{1,0:T(8,128)(2,1)S(1)}, bf16[128,1152]{1,0:T(8,128)(2,1)S(1)}, u32[]{:S(2)}, u32[]{:S(2)}) collective-permute-start(bf16[128,1152]{1,0:T(8,128)(2,1)S(1)} %add_convert_fusion.1), channel_id=1, source_target_pairs={{0,2},{1,3},{2,0},{3,1},{4,6},{5,7},{6,4},{7,5},{8,10},{9,11},{10,... | collective-permute-start | bytes 884744 | tf_op jit(solution)/shard_map/ppermute | solution.py:366
  (66 other events, 888.9 us)

commit v4 on v2

--- a/solution.py
+++ b/solution.py
@@ -192,18 +192,14 @@
 
 def project_kernel(*refs, depth, squared):
     gain_ref, acts, refs = refs[0], refs[1:9], refs[9:]
-    weights, refs = refs[:10], refs[10:]
+    weights, refs = refs[:8], refs[8:]
     outs, squares = refs[:depth], refs[depth:]
     _, tok, width = acts[0].shape
     total = None
     for mask, act in enumerate(acts):
         rows = act[...].reshape(depth * tok, width).astype(jnp.float32)
         rows = (rows * gain_ref[mask : mask + 1, :]).astype(jnp.bfloat16)
-        if mask < 6:
-            part = mm(rows, weights[mask][...])
-        else:
-            halves = weights[6 + mask % 2], weights[8 + mask % 2]
-            part = mm(rows, jnp.concatenate([h[...] for h in halves], axis=0))
+        part = mm(rows, weights[mask][...])
         total = part if total is None else total + part
     for dz in range(depth):
         outs[dz][...] = total[dz * tok : (dz + 1) * tok].astype(jnp.bfloat16)
@@ -217,14 +213,12 @@
                 squares[dz][...] = jnp.broadcast_to(summed, (tok, LANES))
 
 
-def project(gains, acts, weights, half, halves, squared):
+def project(gains, acts, weights, start, steps, columns, squared):
     depth, tok, width = acts[0].shape
-    model = weights[0].shape[1]
-    steps = 2
-    columns = model // halves // steps
+    part = steps * columns
     cost = pl.CostEstimate(
-        flops=16 * depth * tok * width * model // halves,
-        bytes_accessed=2 * (8 * width * model + depth * tok * (model + 8 * width)) // halves,
+        flops=16 * depth * tok * width * part,
+        bytes_accessed=2 * (8 * width * part + depth * tok * (part + 8 * width)),
         transcendentals=0,
     )
     out_shape = [jax.ShapeDtypeStruct((tok, columns * steps), jnp.bfloat16)] * depth
@@ -238,7 +232,7 @@
         grid=(steps,),
         in_specs=[pl.BlockSpec((8, width), lambda i: (0, 0))]
         + [pl.BlockSpec((depth, tok, width), lambda i: (0, 0, 0))] * 8
-        + [pl.BlockSpec((w.shape[0], columns), lambda i: (0, half * steps + i)) for w in weights],
+        + [pl.BlockSpec((w.shape[0], columns), lambda i: (0, start + i)) for w in weights],
         out_specs=out_specs,
         cost_estimate=cost,
         name="project",
@@ -337,7 +331,7 @@
                 pltpu.VMEM((blocks, 2 * count * cap, model), jnp.bfloat16),
             ],
         ),
-        compiler_params=pltpu.CompilerParams(vmem_limit_bytes=40 * 1024 * 1024),
+        compiler_params=pltpu.CompilerParams(vmem_limit_bytes=46 * 1024 * 1024),
         cost_estimate=cost,
         name="experts",
     )(place, *xs, w_gate, w_up, w_down)
@@ -358,6 +352,7 @@
     tokens = head_in.shape[0]
     tok = tokens // devices
     width = head_in.shape[1]
+    model = out_proj.shape[1]
 
     def cross(x, mask):
         return lax.ppermute(x, "mix", [(i, i ^ mask) for i in range(devices)])
@@ -366,7 +361,11 @@
         return lax.ppermute(x, "mix", [(i, (i + stride) % devices) for i in range(devices)])
 
     proj_y, proj_z = cross(out_proj, 2), cross(out_proj, 4)
-    proj_yz = (cross(proj_y[: width // 2], 4), cross(proj_z[width // 2 :], 2))
+    proj_yz = lax.ppermute(
+        jnp.where(me % 2 == 0, proj_y, proj_z),
+        "mix",
+        [(i, i ^ (2 if i % 2 else 4)) for i in range(devices)],
+    )
     gains = jnp.take(norm_gain.reshape(devices, width), me ^ jnp.arange(8), axis=0)
 
     slots = placement.shape[0]
@@ -391,22 +390,21 @@
         place, depth // 2,
     )
     projs = []
-    for block in (out_proj, proj_y, proj_z, *proj_yz):
+    for block in (out_proj, proj_y, proj_z, proj_yz):
         projs += [block, cross(block, 1)]
     acts = [gated[0]] + [cross(gated[mask], mask) for mask in range(1, 8)]
-    halves = 2
     sums = []
-    for half in range(halves):
-        mixed, squares = project(gains, acts, projs, half, halves, half == 0)
+    for half, (start, steps) in enumerate(((0, 1), (1, 3))):
+        mixed, squares = project(gains, acts, projs, start, steps, model // 4, half == 1)
         total = mixed[1]
-        if half == 0:
+        if half == 1:
             norm = squares[1]
         for dz in range(2, depth // 2):
             total = add_low(onward(total, 8), mixed[dz])
-            if half == 0:
+            if half == 1:
                 norm = onward(norm, 8) + squares[dz]
         total = onward(total, 8).astype(jnp.float32) + mixed[0].astype(jnp.float32)
-        if half == 0:
+        if half == 1:
             norm = (onward(norm, 8) + squares[0])[:, 0:1]
         sums.append(total)
     mixer_sum = jnp.concatenate(sums, axis=1)
@@ -417,6 +415,8 @@
     mine = jnp.concatenate([normed, table], axis=1)
 
     cap = 2 * tok * expert_ids.shape[1] // slots
+    cut = model // 2 + LANES
+    sides = (slice(0, cut), slice(cut, model))
     sums = []
     for dz in range(depth):
         if dz > 0:
@@ -424,14 +424,29 @@
         other = cross(mine, 2) if dz < depth - 1 else onward(other)
         block = [mine, cross(mine, 1), other, cross(other, 1)]
         outs = run_experts(block, w_gate, w_up, w_down, place, cap, slots, 1)
-        near = add_low(outs[0], cross(outs[1], 1))
-        far = add_low(outs[2], cross(outs[3], 1))
-        sums.append(add_low(near, cross(far, 2)))
-    total = sums[1]
-    for dz in range(2, depth):
-        total = add_low(onward(total), sums[dz])
-    expert_sum = onward(total).astype(jnp.float32) + sums[0].astype(jnp.float32)
-    return (hidden + expert_sum).astype(jnp.bfloat16)
+        near_c, far_c = cross(outs[1], 1), cross(outs[3], 1)
+        if dz < depth - 1:
+            far = cross(add_low(outs[2], far_c), 2)
+            sums.append((outs[0], near_c, far))
+        else:
+            last = []
+            for side in sides:
+                far = cross(add_low(outs[2][:, side], far_c[:, side]), 2)
+                last.append((outs[0][:, side], near_c[:, side], far))
+
+    def add_all(*terms):
+        return sum(t.astype(jnp.float32) for t in terms)
+
+    total = add_all(*sums[1]).astype(jnp.bfloat16)
+    for dz in range(2, depth - 1):
+        total = add_all(onward(total), *sums[dz]).astype(jnp.bfloat16)
+    results = []
+    for h, side in enumerate(sides):
+        part = onward(total[:, side])
+        part = add_all(part, *last[h]).astype(jnp.bfloat16)
+        part = onward(part)
+        results.append(hidden[:, side] + add_all(part, *(term[:, side] for term in sums[0])))
+    return jnp.concatenate(results, axis=1).astype(jnp.bfloat16)
 
 
 def solution(mesh):

time: 231 us -> 255 us (1.10)
  waiting for transfers between devices: 114 us -> 131 us
  starting transfers between devices: 28.8 us -> 34.3 us
  local copies, waits for them, and re-layouts: 9.21 us -> 4.88 us
  Pallas kernels: 67.9 us -> 71.7 us
    ppermute x39 -> x37, waiting for transfers between devices: 44.9 us -> 63.1 us  [cross(): return lax.ppermute(x, 'mix', [(i, i ^ mask) for i in range(devices)])]
    ppermute x39 -> x37, starting transfers between devices: 22.9 us -> 26.3 us  [cross(): return lax.ppermute(x, 'mix', [(i, i ^ mask) for i in range(devices)])]
    pallas_call x4, Pallas kernels: 44.1 us -> 47.5 us  [run_experts(): pl.pallas_call(functools.partial(expert_kernel, blocks=blocks, cap=cap, s...]
    unnamed x38 -> x28, local copies, waits for them, and re-layouts: 3.34 us -> 0.68 us
    ppermute x10 -> x12, starting transfers between devices: 5.88 us -> 7.64 us  [onward(): lax.ppermute(x, 'mix', [(i, (i + stride) % devices) for i in range(device...]
    ppermute x10 -> x12, waiting for transfers between devices: 68.9 us -> 68.3 us  [onward(): lax.ppermute(x, 'mix', [(i, (i + stride) % devices) for i in range(device...]
  transfers between devices with their start and end apart: 49 -> 50, of which waited for: 20 -> 20; matrix products, arithmetic and copies ran while one was open for 6% -> 5% of each run, Pallas kernels for 28% -> 27%
where the time goes in v4:
time: 255 us; the launch traced here: 254 us
  waiting for transfers between devices  131 us (51%)
  Pallas kernels  71.7 us (28%)
  starting transfers between devices  34.3 us (13%)
  other arithmetic  11.4 us (4%)
  local copies, waits for them, and re-layouts  4.88 us (2%)
    ppermute x12, waiting for transfers between devices, onward(): lax.ppermute(x, 'mix', [(i, (i + stride) % devices) for i in range(device...  68.3 us
    ppermute x37, waiting for transfers between devices, cross(): return lax.ppermute(x, 'mix', [(i, i ^ mask) for i in range(devices)])  63.1 us
    pallas_call x4, Pallas kernels, run_experts(): pl.pallas_call(functools.partial(expert_kernel, blocks=blocks, cap=cap, s...  47.5 us
    ppermute x37, starting transfers between devices, cross(): return lax.ppermute(x, 'mix', [(i, i ^ mask) for i in range(devices)])  26.3 us
    pallas_call x1, Pallas kernels, scan_heads(): pl.pallas_call(functools.partial(scan_kernel, span=span, chunks=chunks),...  14.6 us
    pallas_call x2, Pallas kernels, project(): pl.pallas_call(functools.partial(project_kernel, depth=depth, squared=squ...  9.63 us
    ppermute x12, starting transfers between devices, onward(): lax.ppermute(x, 'mix', [(i, (i + stride) % devices) for i in range(device...  7.64 us
  transfers between devices with their start and end apart: 50, of which 20 were waited for; matrix products, arithmetic and copies ran while one was open for 5% of the time, Pallas kernels for 27%

profile of v4, /device:TPU:0, one launch (start us, length us, event | category | flops | bytes accessed | tf_op | source)
XLA Modules:
  0.0 254.1 jit_solution(13308087891684993407)
XLA Ops:
  0.0 3.1 %collective-permute-start.10 = (bf16[256,2048]{1,0:T(8,128)(2,1)}, bf16[256,2048]{1,0:T(8,128)(2,1)S(1)}, u32[]{:S(2)}, u32[]{:S(2)}) collective-permute-start(bf16[256,2048]{1,0:T(8,128)(2,1)} %refs_9_.3), channel_id=1, source_target_pairs={{0,4},{1,5},{2,6},{3,7},{4,0},{5,1},{6,2},{7,3},{8,12},{9,13},{10,... | collective-permute-start | bytes 3145736 | tf_op jit(solution)/shard_map/ppermute | solution.py:358
  4.6 21.9 %collective-permute-done.10.refs_13_ = bf16[256,2048]{1,0:T(8,128)(2,1)S(1)} collective-permute-done((bf16[256,2048]{1,0:T(8,128)(2,1)}, bf16[256,2048]{1,0:T(8,128)(2,1)S(1)}, u32[]{:S(2)}, u32[]{:S(2)}) %collective-permute-start.10) | collective-permute-done | bytes 1048608 | tf_op jit(solution)/shard_map/ppermute | solution.py:358
  29.6 14.6 %scan.1 = (bf16[2,128,256]{2,1,0:T(8,128)(2,1)}, bf16[2,128,256]{2,1,0:T(8,128)(2,1)}, bf16[2,128,256]{2,1,0:T(8,128)(2,1)}, bf16[2,128,256]{2,1,0:T(8,128)(2,1)...) custom-call(s32[8]{0:T(128)} %lengths.1, ...), custom_call_target="tpu_custom_call" | custom-call | flops 939524096 | bytes 3145728 | tf_op jit(solution)/shard_map/scan/pallas_call | solution.py:165
  46.6 4.3 %collective-permute-done.1.refs_3_ = bf16[2,128,256]{2,1,0:T(8,128)(2,1)S(1)} collective-permute-done((bf16[2,128,256]{2,1,0:T(8,128)(2,1)}, bf16[2,128,256]{2,1,0:T(8,128)(2,1)S(1)}, u32[]{:S(2)}, u32[]{:S(2)}) %collective-permute-start.1) | collective-permute-done | bytes 131104 | tf_op jit(solution)/shard_map/ppermute | solution.py:358
  61.0 3.6 %collective-permute-done.4.refs_6_ = bf16[2,128,256]{2,1,0:T(8,128)(2,1)} collective-permute-done((bf16[2,128,256]{2,1,0:T(8,128)(2,1)}, bf16[2,128,256]{2,1,0:T(8,128)(2,1)}, u32[]{:S(2)}, u32[]{:S(2)}) %collective-permute-start.4) | collective-permute-done | bytes 131104 | tf_op jit(solution)/shard_map/ppermute | solution.py:358
  64.6 2.5 collective-permute-start.5
  73.4 4.7 %collective-permute-done.6.refs_8_ = bf16[2,128,256]{2,1,0:T(8,128)(2,1)S(1)} collective-permute-done((bf16[2,128,256]{2,1,0:T(8,128)(2,1)}, bf16[2,128,256]{2,1,0:T(8,128)(2,1)S(1)}, u32[]{:S(2)}, u32[]{:S(2)}) %collective-permute-start.6) | collective-permute-done | bytes 131104 | tf_op jit(solution)/shard_map/ppermute | solution.py:358
  78.8 3.3 %project.2 = (bf16[128,512]{1,0:T(8,128)(2,1)}, bf16[128,512]{1,0:T(8,128)(2,1)}) custom-call(f32[8,256]{1,0:T(8,128)} %broadcast_select_fusion.1.refs_0_, bf16[2,128,256]{2,1,0:T(8,128)(2,1)} %get-tuple-element.35.refs_1_, bf16[2,128,256]{2,1,0:T(8,128)(2,1)} %copy-done.3, bf16[2,128,256]{2,1,0:T(8,128)(2,1)} %copy-done.4, bf16[2,128,256]{2,1,0:T(8,128)(2,1)} %copy-done.5, ...), custom_call_target="tpu_custom_call" | custom-call | flops 536870912 | bytes 3407872 | tf_op jit(solution)/shard_map/project/pallas_call | solution.py:229
  82.1 2.7 %collective-permute-start.14 = (bf16[128,512]{1,0:T(8,128)(2,1)}, bf16[128,512]{1,0:T(8,128)(2,1)S(1)}, u32[]{:S(2)}, u32[]{:S(2)}) collective-permute-start(bf16[128,512]{1,0:T(8,128)(2,1)} %get-tuple-element.43), channel_id=1, source_target_pairs={{0,8},{1,9},{2,10},{3,11},{4,12},{5,13},{6,14},{7,15},{8,0},{9,1},... | collective-permute-start | bytes 393224 | tf_op jit(solution)/shard_map/ppermute | solution.py:361
  84.8 6.3 %project.3 = (bf16[128,1536]{1,0:T(8,128)(2,1)}, bf16[128,1536]{1,0:T(8,128)(2,1)}, f32[128,128]{1,0:T(8,128)}, f32[128,128]{1,0:T(8,128)}) custom-call(f32[8,256]{1,0:T(8,128)} %broadcast_select_fusion.1.refs_0_, bf16[2,128,256]{2,1,0:T(8,128)(2,1)} %get-tuple-element.35.refs_1_, bf16[2,128,256]{2,1,0:T(8,128)(2,1)} %copy-done.3, ...), custom_call_target="tpu_custom_call" | custom-call | flops 1610612736 | bytes 8126464 | tf_op jit(solution)/shard_map/project/pallas_call | solution.py:229
  91.5 2.6 %collective-permute-start.16 = (f32[128,128]{1,0:T(8,128)}, f32[128,128]{1,0:T(8,128)S(1)}, u32[]{:S(2)}, u32[]{:S(2)}) collective-permute-start(f32[128,128]{1,0:T(8,128)} %get-tuple-element.47), channel_id=1, source_target_pairs={{0,8},{1,9},{2,10},{3,11},{4,12},{5,13},{6,14},{7,15},{8,0},{9,1},... | collective-permute-start | bytes 196616 | tf_op jit(solution)/shard_map/ppermute | solution.py:361
  94.2 19.7 %collective-permute-done.16 = f32[128,128]{1,0:T(8,128)S(1)} collective-permute-done((f32[128,128]{1,0:T(8,128)}, f32[128,128]{1,0:T(8,128)S(1)}, u32[]{:S(2)}, u32[]{:S(2)}) %collective-permute-start.16) | collective-permute-done | bytes 65568 | tf_op jit(solution)/shard_map/ppermute | solution.py:361
  116.6 15.4 %collective-permute-done.17.refs_0_ = bf16[128,2176]{1,0:T(8,128)(2,1)S(1)} collective-permute-done((bf16[128,2176]{1,0:T(8,128)(2,1)S(1)}, bf16[128,2176]{1,0:T(8,128)(2,1)S(1)}, u32[]{:S(2)}, u32[]{:S(2)}) %collective-permute-start.17) | collective-permute-done | bytes 557088 | tf_op jit(solution)/shard_map/ppermute | solution.py:361
  134.0 11.9 %collective-permute-done.19.refs_2_ = bf16[128,2176]{1,0:T(8,128)(2,1)S(1)} collective-permute-done((bf16[128,2176]{1,0:T(8,128)(2,1)S(1)}, bf16[128,2176]{1,0:T(8,128)(2,1)S(1)}, u32[]{:S(2)}, u32[]{:S(2)}) %collective-permute-start.19) | collective-permute-done | bytes 557088 | tf_op jit(solution)/shard_map/ppermute | solution.py:358
  146.0 3.3 %collective-permute-done.25.refs_0_ = bf16[128,2176]{1,0:T(8,128)(2,1)S(1)} collective-permute-done((bf16[128,2176]{1,0:T(8,128)(2,1)S(1)}, bf16[128,2176]{1,0:T(8,128)(2,1)S(1)}, u32[]{:S(2)}, u32[]{:S(2)}) %collective-permute-start.25) | collective-permute-done | bytes 557088 | tf_op jit(solution)/shard_map/ppermute | solution.py:361
  149.5 11.9 %experts.4 = (bf16[128,2048]{1,0:T(8,128)(2,1)S(1)}, bf16[128,2048]{1,0:T(8,128)(2,1)S(1)}, bf16[128,2048]{1,0:T(8,128)(2,1)S(1)}, bf16[128,2048]{1,0:T(8,128)(2,1)S(1)}) custom-call(s32[1]{0:T(128)} %bitcast.1.place, bf16[128,2176]{1,0:T(8,128)(2,1)S(1)} %collective-permute-done.17.refs_0_, bf16[128,2176]{1,0:T(8,128)(2,1)S(1)} %collective-permute-done.18.refs_1_, ...), custom_call_target="tpu_custom_call" | custom-call | flops 4831838208 | bytes 23068672 | tf_op jit(solution)/shard_map/experts/pallas_call | solution.py:314
  166.0 11.9 %experts.5 = (bf16[128,2048]{1,0:T(8,128)(2,1)S(1)}, bf16[128,2048]{1,0:T(8,128)(2,1)S(1)}, bf16[128,2048]{1,0:T(8,128)(2,1)S(1)}, bf16[128,2048]{1,0:T(8,128)(2,1)S(1)}) custom-call(s32[1]{0:T(128)} %bitcast.1.place, bf16[128,2176]{1,0:T(8,128)(2,1)S(1)} %collective-permute-done.25.refs_0_, bf16[128,2176]{1,0:T(8,128)(2,1)S(1)} %collective-permute-done.26.refs_1_, ...), custom_call_target="tpu_custom_call" | custom-call | flops 4831838208 | bytes 23068672 | tf_op jit(solution)/shard_map/experts/pallas_call | solution.py:314
  178.1 3.0 %collective-permute-done.33.refs_0_ = bf16[128,2176]{1,0:T(8,128)(2,1)S(1)} collective-permute-done((bf16[128,2176]{1,0:T(8,128)(2,1)S(1)}, bf16[128,2176]{1,0:T(8,128)(2,1)S(1)}, u32[]{:S(2)}, u32[]{:S(2)}) %collective-permute-start.33) | collective-permute-done | bytes 557088 | tf_op jit(solution)/shard_map/ppermute | solution.py:361
  181.6 10.6 %collective-permute-done.35.refs_2_ = bf16[128,2176]{1,0:T(8,128)(2,1)S(1)} collective-permute-done((bf16[128,2176]{1,0:T(8,128)(2,1)S(1)}, bf16[128,2176]{1,0:T(8,128)(2,1)S(1)}, u32[]{:S(2)}, u32[]{:S(2)}) %collective-permute-start.35) | collective-permute-done | bytes 557088 | tf_op jit(solution)/shard_map/ppermute | solution.py:361
  195.3 11.9 %experts.6 = (bf16[128,2048]{1,0:T(8,128)(2,1)S(1)}, bf16[128,2048]{1,0:T(8,128)(2,1)S(1)}, bf16[128,2048]{1,0:T(8,128)(2,1)S(1)}, bf16[128,2048]{1,0:T(8,128)(2,1)S(1)}) custom-call(s32[1]{0:T(128)} %bitcast.1.place, bf16[128,2176]{1,0:T(8,128)(2,1)S(1)} %collective-permute-done.33.refs_0_, bf16[128,2176]{1,0:T(8,128)(2,1)S(1)} %collective-permute-done.34.refs_1_, ...), custom_call_target="tpu_custom_call" | custom-call | flops 4831838208 | bytes 23068672 | tf_op jit(solution)/shard_map/experts/pallas_call | solution.py:314
  207.2 11.9 %experts.7 = (bf16[128,2048]{1,0:T(8,128)(2,1)S(1)}, bf16[128,2048]{1,0:T(8,128)(2,1)S(1)}, bf16[128,2048]{1,0:T(8,128)(2,1)S(1)}, bf16[128,2048]{1,0:T(8,128)(2,1)S(1)}) custom-call(s32[1]{0:T(128)} %bitcast.1.place, bf16[128,2176]{1,0:T(8,128)(2,1)S(1)} %pad_maximum_fusion.refs_0_, bf16[128,2176]{1,0:T(8,128)(2,1)S(1)} %collective-permute-done.41.refs_1_, ...), custom_call_target="tpu_custom_call" | custom-call | flops 4831838208 | bytes 23068672 | tf_op jit(solution)/shard_map/experts/pallas_call | solution.py:314
  223.2 13.0 %collective-permute-done.47 = bf16[128,896]{1,0:T(8,128)(2,1)S(1)} collective-permute-done((bf16[128,896]{1,0:T(8,128)(2,1)S(1)}, bf16[128,896]{1,0:T(8,128)(2,1)S(1)}, u32[]{:S(2)}, u32[]{:S(2)}) %collective-permute-start.47) | collective-permute-done | bytes 229408 | tf_op jit(solution)/shard_map/ppermute | solution.py:361
  240.1 9.6 %collective-permute-done.46 = bf16[128,2048]{1,0:T(8,128)(2,1)S(1)} collective-permute-done((bf16[128,2048]{1,0:T(8,128)(2,1)S(1)}, bf16[128,2048]{1,0:T(8,128)(2,1)S(1)}, u32[]{:S(2)}, u32[]{:S(2)}) %collective-permute-start.46) | collective-permute-done | bytes 524320 | tf_op jit(solution)/shard_map/ppermute | solution.py:358
  249.8 3.3 %collective-permute-done.40 = bf16[128,1152]{1,0:T(8,128)(2,1)S(1)} collective-permute-done((bf16[128,1152]{1,0:T(8,128)(2,1)S(1)}, bf16[128,1152]{1,0:T(8,128)(2,1)S(1)}, u32[]{:S(2)}, u32[]{:S(2)}) %collective-permute-start.40) | collective-permute-done | bytes 294944 | tf_op jit(solution)/shard_map/ppermute | solution.py:361
  (146 shorter events, 47.0 us)
Async XLA Ops:
  0.0 26.5 %collective-permute-start.10 = (bf16[256,2048]{1,0:T(8,128)(2,1)}, bf16[256,2048]{1,0:T(8,128)(2,1)S(1)}, u32[]{:S(2)}, u32[]{:S(2)}) collective-permute-start(bf16[256,2048]{1,0:T(8,128)(2,1)} %refs_9_.3), channel_id=1, source_target_pairs={{0,4},{1,5},{2,6},{3,7},{4,0},{5,1},{6,2},{7,3},{8,12},{9,13},{10,... | collective-permute-start | bytes 3145736 | tf_op jit(solution)/shard_map/ppermute | solution.py:358
  3.1 24.8 %collective-permute-start.8 = (bf16[256,2048]{1,0:T(8,128)(2,1)}, bf16[256,2048]{1,0:T(8,128)(2,1)S(1)}, u32[]{:S(2)}, u32[]{:S(2)}) collective-permute-start(bf16[256,2048]{1,0:T(8,128)(2,1)} %refs_9_.3), channel_id=1, source_target_pairs={{0,2},{1,3},{2,0},{3,1},{4,6},{5,7},{6,4},{7,5},{8,10},{9,11},{10,... | collective-permute-start | bytes 3145736 | tf_op jit(solution)/shard_map/ppermute | solution.py:358
  29.2 21.7 %collective-permute-start.12 = (bf16[256,2048]{1,0:T(8,128)(2,1)}, bf16[256,2048]{1,0:T(8,128)(2,1)}, u32[]{:S(2)}, u32[]{:S(2)}) collective-permute-start(bf16[256,2048]{1,0:T(8,128)(2,1)} %broadcast_select_fusion), channel_id=1, source_target_pairs={{0,4},{1,3},{2,6},{3,1},{4,0},{5,7},{6,2},{7,5},{8,12},{9,11},{10,... | collective-permute-start | bytes 3145736 | tf_op jit(solution)/shard_map/ppermute | solution.py:364
  46.1 32.0 %collective-permute-start.7 = (bf16[256,2048]{1,0:T(8,128)(2,1)S(1)}, bf16[256,2048]{1,0:T(8,128)(2,1)}, u32[]{:S(2)}, u32[]{:S(2)}) collective-permute-start(bf16[256,2048]{1,0:T(8,128)(2,1)S(1)} %copy-done.2), channel_id=1, source_target_pairs={{0,1},{1,0},{2,3},{3,2},{4,5},{5,4},{6,7},{7,6},{8,9},{9,8},{10,11... | collective-permute-start | bytes 3145736 | tf_op jit(solution)/shard_map/ppermute | solution.py:358
  46.5 31.6 %collective-permute-start.11 = (bf16[256,2048]{1,0:T(8,128)(2,1)S(1)}, bf16[256,2048]{1,0:T(8,128)(2,1)}, u32[]{:S(2)}, u32[]{:S(2)}) collective-permute-start(bf16[256,2048]{1,0:T(8,128)(2,1)S(1)} %collective-permute-done.10.refs_13_), channel_id=1, source_target_pairs={{0,1},{1,0},{2,3},{3,2},{4,5},{5,4},{6,7},{7,6},{8,9},{9,8},{10,11... | collective-permute-start | bytes 3145736 | tf_op jit(solution)/shard_map/ppermute | solution.py:358
  50.9 27.2 %collective-permute-start.9 = (bf16[256,2048]{1,0:T(8,128)(2,1)S(1)}, bf16[256,2048]{1,0:T(8,128)(2,1)}, u32[]{:S(2)}, u32[]{:S(2)}) collective-permute-start(bf16[256,2048]{1,0:T(8,128)(2,1)S(1)} %collective-permute-done.8.refs_11_), channel_id=1, source_target_pairs={{0,1},{1,0},{2,3},{3,2},{4,5},{5,4},{6,7},{7,6},{8,9},{9,8},{10,11... | collective-permute-start | bytes 3145736 | tf_op jit(solution)/shard_map/ppermute | solution.py:358
  50.9 27.8 %collective-permute-start.13 = (bf16[256,2048]{1,0:T(8,128)(2,1)}, bf16[256,2048]{1,0:T(8,128)(2,1)}, u32[]{:S(2)}, u32[]{:S(2)}) collective-permute-start(bf16[256,2048]{1,0:T(8,128)(2,1)} %collective-permute-done.12.refs_15_), channel_id=1, source_target_pairs={{0,1},{1,0},{2,3},{3,2},{4,5},{5,4},{6,7},{7,6},{8,9},{9,8},{10,11... | collective-permute-start | bytes 3145736 | tf_op jit(solution)/shard_map/ppermute | solution.py:358
  82.1 32.7 %collective-permute-start.14 = (bf16[128,512]{1,0:T(8,128)(2,1)}, bf16[128,512]{1,0:T(8,128)(2,1)S(1)}, u32[]{:S(2)}, u32[]{:S(2)}) collective-permute-start(bf16[128,512]{1,0:T(8,128)(2,1)} %get-tuple-element.43), channel_id=1, source_target_pairs={{0,8},{1,9},{2,10},{3,11},{4,12},{5,13},{6,14},{7,15},{8,0},{9,1},... | collective-permute-start | bytes 393224 | tf_op jit(solution)/shard_map/ppermute | solution.py:361
  91.1 23.8 %collective-permute-start.15 = (bf16[128,1536]{1,0:T(8,128)(2,1)}, bf16[128,1536]{1,0:T(8,128)(2,1)S(1)}, u32[]{:S(2)}, u32[]{:S(2)}) collective-permute-start(bf16[128,1536]{1,0:T(8,128)(2,1)} %get-tuple-element.45), channel_id=1, source_target_pairs={{0,8},{1,9},{2,10},{3,11},{4,12},{5,13},{6,14},{7,15},{8,0},{9,1},... | collective-permute-start | bytes 1179656 | tf_op jit(solution)/shard_map/ppermute | solution.py:361
  91.5 22.4 %collective-permute-start.16 = (f32[128,128]{1,0:T(8,128)}, f32[128,128]{1,0:T(8,128)S(1)}, u32[]{:S(2)}, u32[]{:S(2)}) collective-permute-start(f32[128,128]{1,0:T(8,128)} %get-tuple-element.47), channel_id=1, source_target_pairs={{0,8},{1,9},{2,10},{3,11},{4,12},{5,13},{6,14},{7,15},{8,0},{9,1},... | collective-permute-start | bytes 196616 | tf_op jit(solution)/shard_map/ppermute | solution.py:361
  162.1 15.8 %collective-permute-start.42 = (bf16[128,2176]{1,0:T(8,128)(2,1)S(1)}, bf16[128,2176]{1,0:T(8,128)(2,1)S(1)}, u32[]{:S(2)}, u32[]{:S(2)}) collective-permute-start(bf16[128,2176]{1,0:T(8,128)(2,1)S(1)} %pad_maximum_fusion.refs_0_), channel_id=1, source_target_pairs={{0,2},{1,3},{2,0},{3,1},{4,6},{5,7},{6,4},{7,5},{8,10},{9,11},{10,... | collective-permute-start | bytes 1671176 | tf_op jit(solution)/shard_map/ppermute | solution.py:358
  163.8 17.3 %collective-permute-start.33 = (bf16[128,2176]{1,0:T(8,128)(2,1)S(1)}, bf16[128,2176]{1,0:T(8,128)(2,1)S(1)}, u32[]{:S(2)}, u32[]{:S(2)}) collective-permute-start(bf16[128,2176]{1,0:T(8,128)(2,1)S(1)} %collective-permute-done.25.refs_0_), channel_id=1, source_target_pairs={{0,4},{1,5},{2,6},{3,7},{4,8},{5,9},{6,10},{7,11},{8,12},{9,13},{1... | collective-permute-start | bytes 1671176 | tf_op jit(solution)/shard_map/ppermute | solution.py:361
  163.8 17.3 %collective-permute-start.21 = (bf16[128,2048]{1,0:T(8,128)(2,1)S(1)}, bf16[128,2048]{1,0:T(8,128)(2,1)S(1)}, u32[]{:S(2)}, u32[]{:S(2)}) collective-permute-start(bf16[128,2048]{1,0:T(8,128)(2,1)S(1)} %get-tuple-element.50), channel_id=1, source_target_pairs={{0,1},{1,0},{2,3},{3,2},{4,5},{5,4},{6,7},{7,6},{8,9},{9,8},{10,11... | collective-permute-start | bytes 1572872 | tf_op jit(solution)/shard_map/ppermute | solution.py:358
  164.0 28.3 %collective-permute-start.35 = (bf16[128,2176]{1,0:T(8,128)(2,1)S(1)}, bf16[128,2176]{1,0:T(8,128)(2,1)S(1)}, u32[]{:S(2)}, u32[]{:S(2)}) collective-permute-start(bf16[128,2176]{1,0:T(8,128)(2,1)S(1)} %collective-permute-done.27.refs_2_), channel_id=1, source_target_pairs={{0,4},{1,5},{2,6},{3,7},{4,8},{5,9},{6,10},{7,11},{8,12},{9,13},{1... | collective-permute-start | bytes 1671176 | tf_op jit(solution)/shard_map/ppermute | solution.py:361
  164.3 27.9 %collective-permute-start.23 = (bf16[128,2048]{1,0:T(8,128)(2,1)S(1)}, bf16[128,2048]{1,0:T(8,128)(2,1)S(1)}, u32[]{:S(2)}, u32[]{:S(2)}) collective-permute-start(bf16[128,2048]{1,0:T(8,128)(2,1)S(1)} %add_convert_fusion.4), channel_id=1, source_target_pairs={{0,2},{1,3},{2,0},{3,1},{4,6},{5,7},{6,4},{7,5},{8,10},{9,11},{10,... | collective-permute-start | bytes 1572872 | tf_op jit(solution)/shard_map/ppermute | solution.py:358
  181.1 26.0 %collective-permute-start.41 = (bf16[128,2176]{1,0:T(8,128)(2,1)S(1)}, bf16[128,2176]{1,0:T(8,128)(2,1)S(1)}, u32[]{:S(2)}, u32[]{:S(2)}) collective-permute-start(bf16[128,2176]{1,0:T(8,128)(2,1)S(1)} %pad_maximum_fusion.refs_0_), channel_id=1, source_target_pairs={{0,1},{1,0},{2,3},{3,2},{4,5},{5,4},{6,7},{7,6},{8,9},{9,8},{10,11... | collective-permute-start | bytes 1671176 | tf_op jit(solution)/shard_map/ppermute | solution.py:358
  181.1 26.1 %collective-permute-start.43 = (bf16[128,2176]{1,0:T(8,128)(2,1)S(1)}, bf16[128,2176]{1,0:T(8,128)(2,1)S(1)}, u32[]{:S(2)}, u32[]{:S(2)}) collective-permute-start(bf16[128,2176]{1,0:T(8,128)(2,1)S(1)} %collective-permute-done.42.refs_2_), channel_id=1, source_target_pairs={{0,1},{1,0},{2,3},{3,2},{4,5},{5,4},{6,7},{7,6},{8,9},{9,8},{10,11... | collective-permute-start | bytes 1671176 | tf_op jit(solution)/shard_map/ppermute | solution.py:358
  193.0 26.7 %collective-permute-start.29 = (bf16[128,2048]{1,0:T(8,128)(2,1)S(1)}, bf16[128,2048]{1,0:T(8,128)(2,1)S(1)}, u32[]{:S(2)}, u32[]{:S(2)}) collective-permute-start(bf16[128,2048]{1,0:T(8,128)(2,1)S(1)} %get-tuple-element.54), channel_id=1, source_target_pairs={{0,1},{1,0},{2,3},{3,2},{4,5},{5,4},{6,7},{7,6},{8,9},{9,8},{10,11... | collective-permute-start | bytes 1572872 | tf_op jit(solution)/shard_map/ppermute | solution.py:358
  194.2 25.6 %collective-permute-start.24 = (bf16[128,2048]{1,0:T(8,128)(2,1)S(1)}, bf16[128,2048]{1,0:T(8,128)(2,1)S(1)}, u32[]{:S(2)}, u32[]{:S(2)}) collective-permute-start(bf16[128,2048]{1,0:T(8,128)(2,1)S(1)} %add_convert_fusion.3), channel_id=1, source_target_pairs={{0,4},{1,5},{2,6},{3,7},{4,8},{5,9},{6,10},{7,11},{8,12},{9,13},{1... | collective-permute-start | bytes 1572872 | tf_op jit(solution)/shard_map/ppermute | solution.py:361
  195.0 24.8 %collective-permute-start.31 = (bf16[128,2048]{1,0:T(8,128)(2,1)S(1)}, bf16[128,2048]{1,0:T(8,128)(2,1)S(1)}, u32[]{:S(2)}, u32[]{:S(2)}) collective-permute-start(bf16[128,2048]{1,0:T(8,128)(2,1)S(1)} %add_convert_fusion.2), channel_id=1, source_target_pairs={{0,2},{1,3},{2,0},{3,1},{4,6},{5,7},{6,4},{7,5},{8,10},{9,11},{10,... | collective-permute-start | bytes 1572872 | tf_op jit(solution)/shard_map/ppermute | solution.py:358
  220.1 19.3 %collective-permute-start.32 = (bf16[128,1152]{1,0:T(8,128)(2,1)S(1)}, bf16[128,1152]{1,0:T(8,128)(2,1)S(1)}, u32[]{:S(2)}, u32[]{:S(2)}) collective-permute-start(bf16[128,1152]{1,0:T(8,128)(2,1)S(1)} %slice.81), channel_id=1, source_target_pairs={{0,4},{1,5},{2,6},{3,7},{4,8},{5,9},{6,10},{7,11},{8,12},{9,13},{1... | collective-permute-start | bytes 884744 | tf_op jit(solution)/shard_map/ppermute | solution.py:361
  220.2 16.0 %collective-permute-start.47 = (bf16[128,896]{1,0:T(8,128)(2,1)S(1)}, bf16[128,896]{1,0:T(8,128)(2,1)S(1)}, u32[]{:S(2)}, u32[]{:S(2)}) collective-permute-start(bf16[128,896]{1,0:T(8,128)(2,1)S(1)} %slice.87), channel_id=1, source_target_pairs={{0,4},{1,5},{2,6},{3,7},{4,8},{5,9},{6,10},{7,11},{8,12},{9,13},{1... | collective-permute-start | bytes 688136 | tf_op jit(solution)/shard_map/ppermute | solution.py:361
  220.4 19.0 %collective-permute-start.39 = (bf16[128,1152]{1,0:T(8,128)(2,1)S(1)}, bf16[128,1152]{1,0:T(8,128)(2,1)S(1)}, u32[]{:S(2)}, u32[]{:S(2)}) collective-permute-start(bf16[128,1152]{1,0:T(8,128)(2,1)S(1)} %add_convert_fusion.6), channel_id=1, source_target_pairs={{0,2},{1,3},{2,0},{3,1},{4,6},{5,7},{6,4},{7,5},{8,10},{9,11},{10,... | collective-permute-start | bytes 884744 | tf_op jit(solution)/shard_map/ppermute | solution.py:358
  223.1 17.0 %collective-permute-start.44 = (bf16[128,2048]{1,0:T(8,128)(2,1)S(1)}, bf16[128,2048]{1,0:T(8,128)(2,1)S(1)}, u32[]{:S(2)}, u32[]{:S(2)}) collective-permute-start(bf16[128,2048]{1,0:T(8,128)(2,1)S(1)} %get-tuple-element.62), channel_id=1, source_target_pairs={{0,1},{1,0},{2,3},{3,2},{4,5},{5,4},{6,7},{7,6},{8,9},{9,8},{10,11... | collective-permute-start | bytes 1572872 | tf_op jit(solution)/shard_map/ppermute | solution.py:358
  (40 other events, 699.5 us)

commit v5 on v4

--- a/solution.py
+++ b/solution.py
@@ -190,7 +190,7 @@
     )(lengths, place, rate, step, head_in, gate_in, in_basis, out_basis, init)
 
 
-def project_kernel(*refs, depth, squared):
+def project_kernel(place, *refs, depth, squared):
     gain_ref, acts, refs = refs[0], refs[1:9], refs[9:]
     weights, refs = refs[:8], refs[8:]
     outs, squares = refs[:depth], refs[depth:]
@@ -198,7 +198,7 @@
     total = None
     for mask, act in enumerate(acts):
         rows = act[...].reshape(depth * tok, width).astype(jnp.float32)
-        rows = (rows * gain_ref[mask : mask + 1, :]).astype(jnp.bfloat16)
+        rows = (rows * gain_ref[pl.ds(place[0] ^ mask, 1), :]).astype(jnp.bfloat16)
         part = mm(rows, weights[mask][...])
         total = part if total is None else total + part
     for dz in range(depth):
@@ -213,7 +213,7 @@
                 squares[dz][...] = jnp.broadcast_to(summed, (tok, LANES))
 
 
-def project(gains, acts, weights, start, steps, columns, squared):
+def project(place, gains, acts, weights, start, steps, columns, squared):
     depth, tok, width = acts[0].shape
     part = steps * columns
     cost = pl.CostEstimate(
@@ -222,25 +222,29 @@
         transcendentals=0,
     )
     out_shape = [jax.ShapeDtypeStruct((tok, columns * steps), jnp.bfloat16)] * depth
-    out_specs = [pl.BlockSpec((tok, columns), lambda i: (0, i))] * depth
+    out_specs = [pl.BlockSpec((tok, columns), lambda i, place: (0, i))] * depth
     if squared:
         out_shape += [jax.ShapeDtypeStruct((tok, LANES), jnp.float32)] * depth
-        out_specs += [pl.BlockSpec((tok, LANES), lambda i: (0, 0))] * depth
+        out_specs += [pl.BlockSpec((tok, LANES), lambda i, place: (0, 0))] * depth
     out = pl.pallas_call(
         functools.partial(project_kernel, depth=depth, squared=squared),
         out_shape=out_shape,
-        grid=(steps,),
-        in_specs=[pl.BlockSpec((8, width), lambda i: (0, 0))]
-        + [pl.BlockSpec((depth, tok, width), lambda i: (0, 0, 0))] * 8
-        + [pl.BlockSpec((w.shape[0], columns), lambda i: (0, start + i)) for w in weights],
-        out_specs=out_specs,
+        grid_spec=pltpu.PrefetchScalarGridSpec(
+            num_scalar_prefetch=1,
+            grid=(steps,),
+            in_specs=[pl.BlockSpec(gains.shape, lambda i, place: (0, 0))]
+            + [pl.BlockSpec((depth, tok, width), lambda i, place: (0, 0, 0))] * 8
+            + [pl.BlockSpec((width, columns), lambda i, place: (0, start + i))] * 8,
+            out_specs=out_specs,
+        ),
+        compiler_params=pltpu.CompilerParams(vmem_limit_bytes=20 * 1024 * 1024),
         cost_estimate=cost,
         name="project",
-    )(gains, *acts, *weights)
+    )(place, gains, *acts, *weights)
     return out[:depth], out[depth:]
 
 
-def expert_kernel(place, *refs, blocks, cap, slots):
+def expert_kernel(place, owner_ref, *refs, blocks, cap):
     x_refs = refs[:blocks]
     gate_ref, up_ref, down_ref = refs[blocks : blocks + 3]
     outs = refs[blocks + 3 : 2 * blocks + 3]
@@ -253,9 +257,7 @@
     @pl.when(jnp.logical_and(expert == 0, part == 0))
     def _():
         here = place[0] * count + lax.broadcasted_iota(jnp.int32, (LANES, wide), 1) // cap
-        source = lax.broadcasted_iota(jnp.int32, (LANES, wide), 0)
-        pick = jnp.where(jnp.logical_or(source == here, source == here + slots), 1.0, 0.0)
-        pick = pick.astype(jnp.bfloat16)
+        pick = jnp.where(owner_ref[...] == here, 1.0, 0.0).astype(jnp.bfloat16)
         below = lax.broadcasted_iota(jnp.int32, (tok, tok), 0)
         across = lax.broadcasted_iota(jnp.int32, (tok, tok), 1)
         earlier = jnp.where(across < below, 1.0, 0.0).astype(jnp.bfloat16)
@@ -301,7 +303,7 @@
             outs[b][...] = mm(combine[b], results[b]).astype(jnp.bfloat16)
 
 
-def run_experts(xs, w_gate, w_up, w_down, place, cap, slots, parts):
+def run_experts(xs, w_gate, w_up, w_down, place, owner, cap, parts):
     blocks = len(xs)
     tok, extended = xs[0].shape
     count, model, hidden = w_gate.shape
@@ -312,12 +314,13 @@
         transcendentals=count * blocks * cap * hidden,
     )
     return pl.pallas_call(
-        functools.partial(expert_kernel, blocks=blocks, cap=cap, slots=slots),
+        functools.partial(expert_kernel, blocks=blocks, cap=cap),
         out_shape=[jax.ShapeDtypeStruct((tok, model), jnp.bfloat16)] * blocks,
         grid_spec=pltpu.PrefetchScalarGridSpec(
             num_scalar_prefetch=1,
             grid=(count, parts),
-            in_specs=[pl.BlockSpec((tok, extended), lambda e, f, place: (0, 0))] * blocks
+            in_specs=[pl.BlockSpec(owner.shape, lambda e, f, place: (0, 0))]
+            + [pl.BlockSpec((tok, extended), lambda e, f, place: (0, 0))] * blocks
             + [
                 pl.BlockSpec((1, model, tile), lambda e, f, place: (e, 0, f)),
                 pl.BlockSpec((1, model, tile), lambda e, f, place: (e, 0, f)),
@@ -331,10 +334,10 @@
                 pltpu.VMEM((blocks, 2 * count * cap, model), jnp.bfloat16),
             ],
         ),
-        compiler_params=pltpu.CompilerParams(vmem_limit_bytes=46 * 1024 * 1024),
+        compiler_params=pltpu.CompilerParams(vmem_limit_bytes=40 * 1024 * 1024),
         cost_estimate=cost,
         name="experts",
-    )(place, *xs, w_gate, w_up, w_down)
+    )(place, owner, *xs, w_gate, w_up, w_down)
 
 
 def add_low(a, b):
@@ -366,24 +369,19 @@
         "mix",
         [(i, i ^ (2 if i % 2 else 4)) for i in range(devices)],
     )
-    gains = jnp.take(norm_gain.reshape(devices, width), me ^ jnp.arange(8), axis=0)
+    gains = norm_gain.reshape(devices, width)
 
     slots = placement.shape[0]
-    slot_of = jnp.sum(
-        jnp.where(
-            expert_ids[:, :, None] == jnp.arange(slots, dtype=jnp.int32), placement[None, None, :], 0
-        ),
-        axis=2,
-    )
-    route = jnp.sum(
-        jnp.where(
-            slot_of[:, :, None] == jnp.arange(slots, dtype=jnp.int32), route_weight[:, :, None], 0.0
-        ),
-        axis=1,
-    )
-    route_high = lax.reduce_precision(route, 8, 7)
-    table = jnp.concatenate([route_high, route - route_high], axis=1)
-    table = jnp.pad(table, ((0, 0), (0, LANES - 2 * slots))).astype(jnp.bfloat16)
+    column = lax.broadcasted_iota(jnp.int32, (tok, LANES), 1)
+    route = jnp.zeros((tok, LANES), jnp.float32)
+    for k in range(expert_ids.shape[1]):
+        named = expert_ids[:, k : k + 1] == column % slots
+        route = route + jnp.where(named, route_weight[:, k : k + 1], 0.0)
+    high = lax.reduce_precision(route, 8, 7)
+    table = jnp.where(column < slots, high, jnp.where(column < 2 * slots, route - high, 0.0))
+    table = table.astype(jnp.bfloat16)
+    owner = jnp.concatenate([placement, placement])
+    owner = jnp.pad(owner, (0, LANES - 2 * slots), constant_values=-1)[:, None]
 
     gated = scan_heads(
         head_in, gate_in, in_basis, out_basis, step_size, decay_rate, init_state, lengths,
@@ -394,8 +392,8 @@
         projs += [block, cross(block, 1)]
     acts = [gated[0]] + [cross(gated[mask], mask) for mask in range(1, 8)]
     sums = []
-    for half, (start, steps) in enumerate(((0, 1), (1, 3))):
-        mixed, squares = project(gains, acts, projs, start, steps, model // 4, half == 1)
+    for half, (start, steps) in enumerate(((0, 2), (2, 2))):
+        mixed, squares = project(place, gains, acts, projs, start, steps, model // 4, half == 1)
         total = mixed[1]
         if half == 1:
             norm = squares[1]
@@ -423,16 +421,17 @@
             mine = onward(mine)
         other = cross(mine, 2) if dz < depth - 1 else onward(other)
         block = [mine, cross(mine, 1), other, cross(other, 1)]
-        outs = run_experts(block, w_gate, w_up, w_down, place, cap, slots, 1)
+        outs = run_experts(block, w_gate, w_up, w_down, place, owner, cap, 1)
         near_c, far_c = cross(outs[1], 1), cross(outs[3], 1)
-        if dz < depth - 1:
+        if 0 < dz < depth - 1:
             far = cross(add_low(outs[2], far_c), 2)
             sums.append((outs[0], near_c, far))
         else:
-            last = []
+            parts = []
             for side in sides:
                 far = cross(add_low(outs[2][:, side], far_c[:, side]), 2)
-                last.append((outs[0][:, side], near_c[:, side], far))
+                parts.append((outs[0][:, side], near_c[:, side], far))
+            sums.append(parts)
 
     def add_all(*terms):
         return sum(t.astype(jnp.float32) for t in terms)
@@ -443,9 +442,9 @@
     results = []
     for h, side in enumerate(sides):
         part = onward(total[:, side])
-        part = add_all(part, *last[h]).astype(jnp.bfloat16)
+        part = add_all(part, *sums[-1][h]).astype(jnp.bfloat16)
         part = onward(part)
-        results.append(hidden[:, side] + add_all(part, *(term[:, side] for term in sums[0])))
+        results.append(hidden[:, side] + add_all(part, *sums[0][h]))
     return jnp.concatenate(results, axis=1).astype(jnp.bfloat16)
 
 

time: 255 us -> 253 us (level)
  Pallas kernels: 71.7 us -> 64.8 us
  starting transfers between devices: 34.3 us -> 40.4 us
  local copies, waits for them, and re-layouts: 4.88 us -> 10.6 us
  other arithmetic: 11.4 us -> 5.99 us
    ppermute x12, waiting for transfers between devices: 68.3 us -> 54 us  [onward(): lax.ppermute(x, 'mix', [(i, (i + stride) % devices) for i in range(device...]
    ppermute x37 -> x38, waiting for transfers between devices: 63.1 us -> 75.9 us  [cross(): return lax.ppermute(x, 'mix', [(i, i ^ mask) for i in range(devices)])]
    unnamed x28 -> x74, local copies, waits for them, and re-layouts: 0.68 us -> 8.5 us
    ppermute x12, starting transfers between devices: 7.64 us -> 13.2 us  [onward(): lax.ppermute(x, 'mix', [(i, (i + stride) % devices) for i in range(device...]
    pallas_call x2, Pallas kernels: 9.63 us -> 6.09 us  [project(): pl.pallas_call(functools.partial(project_kernel, depth=depth, squared=squ...]
    pallas_call x4, Pallas kernels: 47.5 us -> 44.1 us  [run_experts(): pl.pallas_call(functools.partial(expert_kernel, blocks=blocks, cap=cap),...]
    ppermute x37 -> x38, starting transfers between devices: 26.3 us -> 26.8 us  [cross(): return lax.ppermute(x, 'mix', [(i, i ^ mask) for i in range(devices)])]
  transfers between devices with their start and end apart: 50 -> 51, of which waited for: 20 -> 21; matrix products, arithmetic and copies ran while one was open for 5% -> 2% of each run, Pallas kernels for 27% -> 25%
where the time goes in v5:
time: 253 us; the launch traced here: 252 us
  waiting for transfers between devices  130 us (51%)
  Pallas kernels  64.8 us (26%)
  starting transfers between devices  40.4 us (16%)
  local copies, waits for them, and re-layouts  10.6 us (4%)
  other arithmetic  5.99 us (2%)
    ppermute x38, waiting for transfers between devices, cross(): return lax.ppermute(x, 'mix', [(i, i ^ mask) for i in range(devices)])  75.9 us
    ppermute x12, waiting for transfers between devices, onward(): lax.ppermute(x, 'mix', [(i, (i + stride) % devices) for i in range(device...  54 us
    pallas_call x4, Pallas kernels, run_experts(): pl.pallas_call(functools.partial(expert_kernel, blocks=blocks, cap=cap),...  44.1 us
    ppermute x38, starting transfers between devices, cross(): return lax.ppermute(x, 'mix', [(i, i ^ mask) for i in range(devices)])  26.8 us
    pallas_call x1, Pallas kernels, scan_heads(): pl.pallas_call(functools.partial(scan_kernel, span=span, chunks=chunks),...  14.6 us
    ppermute x12, starting transfers between devices, onward(): lax.ppermute(x, 'mix', [(i, (i + stride) % devices) for i in range(device...  13.2 us
    unnamed x74, local copies, waits for them, and re-layouts  8.5 us
    pallas_call x2, Pallas kernels, project(): pl.pallas_call(functools.partial(project_kernel, depth=depth, squared=squ...  6.09 us
  transfers between devices with their start and end apart: 51, of which 21 were waited for; matrix products, arithmetic and copies ran while one was open for 2% of the time, Pallas kernels for 25%

profile of v5, /device:TPU:0, one launch (start us, length us, event | category | flops | bytes accessed | tf_op | source)
XLA Modules:
  0.0 252.4 jit_solution(10960202120133683722)
XLA Ops:
  0.0 3.1 %collective-permute-start.10 = (bf16[256,2048]{1,0:T(8,128)(2,1)}, bf16[256,2048]{1,0:T(8,128)(2,1)S(1)}, u32[]{:S(2)}, u32[]{:S(2)}) collective-permute-start(bf16[256,2048]{1,0:T(8,128)(2,1)} %refs_9_.3), channel_id=1, source_target_pairs={{0,4},{1,5},{2,6},{3,7},{4,0},{5,1},{6,2},{7,3},{8,12},{9,13},{10,... | collective-permute-start | bytes 3145736 | tf_op jit(solution)/shard_map/ppermute | solution.py:361
  4.6 21.8 %collective-permute-done.10.refs_13_ = bf16[256,2048]{1,0:T(8,128)(2,1)S(1)} collective-permute-done((bf16[256,2048]{1,0:T(8,128)(2,1)}, bf16[256,2048]{1,0:T(8,128)(2,1)S(1)}, u32[]{:S(2)}, u32[]{:S(2)}) %collective-permute-start.10) | collective-permute-done | bytes 1048608 | tf_op jit(solution)/shard_map/ppermute | solution.py:361
  29.4 14.6 %scan.1 = (bf16[2,128,256]{2,1,0:T(8,128)(2,1)}, bf16[2,128,256]{2,1,0:T(8,128)(2,1)}, bf16[2,128,256]{2,1,0:T(8,128)(2,1)}, bf16[2,128,256]{2,1,0:T(8,128)(2,1)...) custom-call(s32[8]{0:T(128)} %lengths.1, ...), custom_call_target="tpu_custom_call" | custom-call | flops 939524096 | bytes 3145728 | tf_op jit(solution)/shard_map/scan/pallas_call | solution.py:165
  46.8 3.4 %collective-permute-done.1.refs_3_ = bf16[2,128,256]{2,1,0:T(8,128)(2,1)S(1)} collective-permute-done((bf16[2,128,256]{2,1,0:T(8,128)(2,1)}, bf16[2,128,256]{2,1,0:T(8,128)(2,1)S(1)}, u32[]{:S(2)}, u32[]{:S(2)}) %collective-permute-start.1) | collective-permute-done | bytes 131104 | tf_op jit(solution)/shard_map/ppermute | solution.py:361
  51.0 5.1 %collective-permute-done.2.refs_4_ = bf16[2,128,256]{2,1,0:T(8,128)(2,1)S(1)} collective-permute-done((bf16[2,128,256]{2,1,0:T(8,128)(2,1)}, bf16[2,128,256]{2,1,0:T(8,128)(2,1)S(1)}, u32[]{:S(2)}, u32[]{:S(2)}) %collective-permute-start.2) | collective-permute-done | bytes 131104 | tf_op jit(solution)/shard_map/ppermute | solution.py:361
  57.9 4.0 %collective-permute-done.3.refs_5_ = bf16[2,128,256]{2,1,0:T(8,128)(2,1)S(1)} collective-permute-done((bf16[2,128,256]{2,1,0:T(8,128)(2,1)}, bf16[2,128,256]{2,1,0:T(8,128)(2,1)S(1)}, u32[]{:S(2)}, u32[]{:S(2)}) %collective-permute-start.3) | collective-permute-done | bytes 131104 | tf_op jit(solution)/shard_map/ppermute | solution.py:361
  63.7 4.5 %collective-permute-done.4.refs_6_ = bf16[2,128,256]{2,1,0:T(8,128)(2,1)S(1)} collective-permute-done((bf16[2,128,256]{2,1,0:T(8,128)(2,1)}, bf16[2,128,256]{2,1,0:T(8,128)(2,1)S(1)}, u32[]{:S(2)}, u32[]{:S(2)}) %collective-permute-start.4) | collective-permute-done | bytes 131104 | tf_op jit(solution)/shard_map/ppermute | solution.py:361
  71.8 3.7 %collective-permute-done.5.refs_7_ = bf16[2,128,256]{2,1,0:T(8,128)(2,1)S(1)} collective-permute-done((bf16[2,128,256]{2,1,0:T(8,128)(2,1)}, bf16[2,128,256]{2,1,0:T(8,128)(2,1)S(1)}, u32[]{:S(2)}, u32[]{:S(2)}) %collective-permute-start.5) | collective-permute-done | bytes 131104 | tf_op jit(solution)/shard_map/ppermute | solution.py:361
  77.5 5.1 %collective-permute-done.6.refs_8_ = bf16[2,128,256]{2,1,0:T(8,128)(2,1)} collective-permute-done((bf16[2,128,256]{2,1,0:T(8,128)(2,1)}, bf16[2,128,256]{2,1,0:T(8,128)(2,1)}, u32[]{:S(2)}, u32[]{:S(2)}) %collective-permute-start.6) | collective-permute-done | bytes 131104 | tf_op jit(solution)/shard_map/ppermute | solution.py:361
  89.3 2.9 %collective-permute-start.14 = (bf16[128,1024]{1,0:T(8,128)(2,1)S(1)}, bf16[128,1024]{1,0:T(8,128)(2,1)S(1)}, u32[]{:S(2)}, u32[]{:S(2)}) collective-permute-start(bf16[128,1024]{1,0:T(8,128)(2,1)S(1)} %get-tuple-element.43), channel_id=1, source_target_pairs={{0,8},{1,9},{2,10},{3,11},{4,12},{5,13},{6,14},{7,15},{8,0},{9,1},... | collective-permute-start | bytes 786440 | tf_op jit(solution)/shard_map/ppermute | solution.py:364
  92.2 3.2 %project.3 = (bf16[128,1024]{1,0:T(8,128)(2,1)S(1)}, bf16[128,1024]{1,0:T(8,128)(2,1)S(1)}, f32[128,128]{1,0:T(8,128)S(1)}, f32[128,128]{1,0:T(8,128)S(1)}) custom-call(s32[1]{0:T(128)} %bitcast.place, f32[16,256]{1,0:T(8,128)S(1)} %reshape.15.refs_0_, bf16[2,128,256]{2,1,0:T(8,128)(2,1)S(1)} %copy-done.2, ...), custom_call_target="tpu_custom_call" | custom-call | flops 1073741824 | bytes 5767168 | tf_op jit(solution)/shard_map/project/pallas_call | solution.py:229
  99.1 13.8 %collective-permute-done.16 = f32[128,128]{1,0:T(8,128)S(1)} collective-permute-done((f32[128,128]{1,0:T(8,128)S(1)}, f32[128,128]{1,0:T(8,128)S(1)}, u32[]{:S(2)}, u32[]{:S(2)}) %collective-permute-start.16) | collective-permute-done | bytes 65568 | tf_op jit(solution)/shard_map/ppermute | solution.py:364
  113.0 4.9 %collective-permute-done.15 = bf16[128,1024]{1,0:T(8,128)(2,1)S(1)} collective-permute-done((bf16[128,1024]{1,0:T(8,128)(2,1)S(1)}, bf16[128,1024]{1,0:T(8,128)(2,1)S(1)}, u32[]{:S(2)}, u32[]{:S(2)}) %collective-permute-start.15) | collective-permute-done | bytes 262176 | tf_op jit(solution)/shard_map/ppermute | solution.py:364
  118.9 15.6 %collective-permute-done.17.refs_0_ = bf16[128,2176]{1,0:T(8,128)(2,1)S(1)} collective-permute-done((bf16[128,2176]{1,0:T(8,128)(2,1)S(1)}, bf16[128,2176]{1,0:T(8,128)(2,1)S(1)}, u32[]{:S(2)}, u32[]{:S(2)}) %collective-permute-start.17) | collective-permute-done | bytes 557088 | tf_op jit(solution)/shard_map/ppermute | solution.py:364
  136.0 11.8 %collective-permute-done.19.refs_2_ = bf16[128,2176]{1,0:T(8,128)(2,1)S(1)} collective-permute-done((bf16[128,2176]{1,0:T(8,128)(2,1)S(1)}, bf16[128,2176]{1,0:T(8,128)(2,1)S(1)}, u32[]{:S(2)}, u32[]{:S(2)}) %collective-permute-start.19) | collective-permute-done | bytes 557088 | tf_op jit(solution)/shard_map/ppermute | solution.py:361
  154.1 11.0 %experts.4 = (bf16[128,2048]{1,0:T(8,128)(2,1)S(1)}, bf16[128,2048]{1,0:T(8,128)(2,1)S(1)}, bf16[128,2048]{1,0:T(8,128)(2,1)S(1)}, bf16[128,2048]{1,0:T(8,128)(2,1)S(1)}) custom-call(s32[1]{0:T(128)} %bitcast.place, s32[128,1]{1,0:T(8,128)S(1)} %copy.23.owner_ref, bf16[128,2176]{1,0:T(8,128)(2,1)S(1)} %collective-permute-done.17.refs_0_, ...), custom_call_target="tpu_custom_call" | custom-call | flops 4831838208 | bytes 23068672 | tf_op jit(solution)/shard_map/experts/pallas_call | solution.py:316
  165.8 9.2 %collective-permute-done.27.refs_2_ = bf16[128,2176]{1,0:T(8,128)(2,1)S(1)} collective-permute-done((bf16[128,2176]{1,0:T(8,128)(2,1)S(1)}, bf16[128,2176]{1,0:T(8,128)(2,1)S(1)}, u32[]{:S(2)}, u32[]{:S(2)}) %collective-permute-start.27) | collective-permute-done | bytes 557088 | tf_op jit(solution)/shard_map/ppermute | solution.py:361
  178.7 11.0 %experts.5 = (bf16[128,2048]{1,0:T(8,128)(2,1)S(1)}, bf16[128,2048]{1,0:T(8,128)(2,1)S(1)}, bf16[128,2048]{1,0:T(8,128)(2,1)S(1)}, bf16[128,2048]{1,0:T(8,128)(2,1)S(1)}) custom-call(s32[1]{0:T(128)} %bitcast.place, s32[128,1]{1,0:T(8,128)S(1)} %copy.23.owner_ref, bf16[128,2176]{1,0:T(8,128)(2,1)S(1)} %collective-permute-done.25.refs_0_, ...), custom_call_target="tpu_custom_call" | custom-call | flops 4831838208 | bytes 23068672 | tf_op jit(solution)/shard_map/experts/pallas_call | solution.py:316
  189.9 11.0 %experts.7 = (bf16[128,2048]{1,0:T(8,128)(2,1)S(1)}, bf16[128,2048]{1,0:T(8,128)(2,1)S(1)}, bf16[128,2048]{1,0:T(8,128)(2,1)S(1)}, bf16[128,2048]{1,0:T(8,128)(2,1)S(1)}) custom-call(s32[1]{0:T(128)} %bitcast.place, s32[128,1]{1,0:T(8,128)S(1)} %copy.23.owner_ref, bf16[128,2176]{1,0:T(8,128)(2,1)S(1)} %pad_maximum_fusion.refs_0_, ...), custom_call_target="tpu_custom_call" | custom-call | flops 4831838208 | bytes 23068672 | tf_op jit(solution)/shard_map/experts/pallas_call | solution.py:316
  206.9 11.0 %experts.6 = (bf16[128,2048]{1,0:T(8,128)(2,1)S(1)}, bf16[128,2048]{1,0:T(8,128)(2,1)S(1)}, bf16[128,2048]{1,0:T(8,128)(2,1)S(1)}, bf16[128,2048]{1,0:T(8,128)(2,1)S(1)}) custom-call(s32[1]{0:T(128)} %bitcast.place, s32[128,1]{1,0:T(8,128)S(1)} %copy.23.owner_ref, bf16[128,2176]{1,0:T(8,128)(2,1)S(1)} %collective-permute-done.33.refs_0_, ...), custom_call_target="tpu_custom_call" | custom-call | flops 4831838208 | bytes 23068672 | tf_op jit(solution)/shard_map/experts/pallas_call | solution.py:316
  224.9 10.9 %collective-permute-done.47 = bf16[128,896]{1,0:T(8,128)(2,1)S(1)} collective-permute-done((bf16[128,896]{1,0:T(8,128)(2,1)S(1)}, bf16[128,896]{1,0:T(8,128)(2,1)S(1)}, u32[]{:S(2)}, u32[]{:S(2)}) %collective-permute-start.47) | collective-permute-done | bytes 229408 | tf_op jit(solution)/shard_map/ppermute | solution.py:364
  239.4 3.7 %collective-permute-start.40 = (bf16[128,1152]{1,0:T(8,128)(2,1)S(1)}, bf16[128,1152]{1,0:T(8,128)(2,1)S(1)}, u32[]{:S(2)}, u32[]{:S(2)}) collective-permute-start(bf16[128,1152]{1,0:T(8,128)(2,1)S(1)} %add_convert_fusion.5), channel_id=1, source_target_pairs={{0,4},{1,5},{2,6},{3,7},{4,8},{5,9},{6,10},{7,11},{8,12},{9,13},{1... | collective-permute-start | bytes 884744 | tf_op jit(solution)/shard_map/ppermute | solution.py:364
  243.1 4.9 %collective-permute-done.50 = bf16[128,896]{1,0:T(8,128)(2,1)S(1)} collective-permute-done((bf16[128,896]{1,0:T(8,128)(2,1)S(1)}, bf16[128,896]{1,0:T(8,128)(2,1)S(1)}, u32[]{:S(2)}, u32[]{:S(2)}) %collective-permute-start.50) | collective-permute-done | bytes 229408 | tf_op jit(solution)/shard_map/ppermute | solution.py:361
  248.4 3.0 %collective-permute-done.40 = bf16[128,1152]{1,0:T(8,128)(2,1)S(1)} collective-permute-done((bf16[128,1152]{1,0:T(8,128)(2,1)S(1)}, bf16[128,1152]{1,0:T(8,128)(2,1)S(1)}, u32[]{:S(2)}, u32[]{:S(2)}) %collective-permute-start.40) | collective-permute-done | bytes 294944 | tf_op jit(solution)/shard_map/ppermute | solution.py:364
  (193 shorter events, 58.5 us)
Async XLA Ops:
  0.0 26.5 %collective-permute-start.10 = (bf16[256,2048]{1,0:T(8,128)(2,1)}, bf16[256,2048]{1,0:T(8,128)(2,1)S(1)}, u32[]{:S(2)}, u32[]{:S(2)}) collective-permute-start(bf16[256,2048]{1,0:T(8,128)(2,1)} %refs_9_.3), channel_id=1, source_target_pairs={{0,4},{1,5},{2,6},{3,7},{4,0},{5,1},{6,2},{7,3},{8,12},{9,13},{10,... | collective-permute-start | bytes 3145736 | tf_op jit(solution)/shard_map/ppermute | solution.py:361
  3.1 24.8 %collective-permute-start.8 = (bf16[256,2048]{1,0:T(8,128)(2,1)}, bf16[256,2048]{1,0:T(8,128)(2,1)S(1)}, u32[]{:S(2)}, u32[]{:S(2)}) collective-permute-start(bf16[256,2048]{1,0:T(8,128)(2,1)} %refs_9_.3), channel_id=1, source_target_pairs={{0,2},{1,3},{2,0},{3,1},{4,6},{5,7},{6,4},{7,5},{8,10},{9,11},{10,... | collective-permute-start | bytes 3145736 | tf_op jit(solution)/shard_map/ppermute | solution.py:361
  29.1 17.4 %collective-permute-start.12 = (bf16[256,2048]{1,0:T(8,128)(2,1)}, bf16[256,2048]{1,0:T(8,128)(2,1)}, u32[]{:S(2)}, u32[]{:S(2)}) collective-permute-start(bf16[256,2048]{1,0:T(8,128)(2,1)} %broadcast_select_fusion), channel_id=1, source_target_pairs={{0,4},{1,3},{2,6},{3,1},{4,0},{5,7},{6,2},{7,5},{8,12},{9,11},{10,... | collective-permute-start | bytes 3145736 | tf_op jit(solution)/shard_map/ppermute | solution.py:367
  45.8 36.8 %collective-permute-start.7 = (bf16[256,2048]{1,0:T(8,128)(2,1)S(1)}, bf16[256,2048]{1,0:T(8,128)(2,1)}, u32[]{:S(2)}, u32[]{:S(2)}) collective-permute-start(bf16[256,2048]{1,0:T(8,128)(2,1)S(1)} %copy-done.1), channel_id=1, source_target_pairs={{0,1},{1,0},{2,3},{3,2},{4,5},{5,4},{6,7},{7,6},{8,9},{9,8},{10,11... | collective-permute-start | bytes 3145736 | tf_op jit(solution)/shard_map/ppermute | solution.py:361
  45.9 36.7 %collective-permute-start.11 = (bf16[256,2048]{1,0:T(8,128)(2,1)S(1)}, bf16[256,2048]{1,0:T(8,128)(2,1)}, u32[]{:S(2)}, u32[]{:S(2)}) collective-permute-start(bf16[256,2048]{1,0:T(8,128)(2,1)S(1)} %collective-permute-done.10.refs_13_), channel_id=1, source_target_pairs={{0,1},{1,0},{2,3},{3,2},{4,5},{5,4},{6,7},{7,6},{8,9},{9,8},{10,11... | collective-permute-start | bytes 3145736 | tf_op jit(solution)/shard_map/ppermute | solution.py:361
  46.3 36.3 %collective-permute-start.9 = (bf16[256,2048]{1,0:T(8,128)(2,1)S(1)}, bf16[256,2048]{1,0:T(8,128)(2,1)}, u32[]{:S(2)}, u32[]{:S(2)}) collective-permute-start(bf16[256,2048]{1,0:T(8,128)(2,1)S(1)} %collective-permute-done.8.refs_11_), channel_id=1, source_target_pairs={{0,1},{1,0},{2,3},{3,2},{4,5},{5,4},{6,7},{7,6},{8,9},{9,8},{10,11... | collective-permute-start | bytes 3145736 | tf_op jit(solution)/shard_map/ppermute | solution.py:361
  46.4 36.2 %collective-permute-start.13 = (bf16[256,2048]{1,0:T(8,128)(2,1)}, bf16[256,2048]{1,0:T(8,128)(2,1)}, u32[]{:S(2)}, u32[]{:S(2)}) collective-permute-start(bf16[256,2048]{1,0:T(8,128)(2,1)} %collective-permute-done.12.refs_15_), channel_id=1, source_target_pairs={{0,1},{1,0},{2,3},{3,2},{4,5},{5,4},{6,7},{7,6},{8,9},{9,8},{10,11... | collective-permute-start | bytes 3145736 | tf_op jit(solution)/shard_map/ppermute | solution.py:361
  89.3 23.6 %collective-permute-start.14 = (bf16[128,1024]{1,0:T(8,128)(2,1)S(1)}, bf16[128,1024]{1,0:T(8,128)(2,1)S(1)}, u32[]{:S(2)}, u32[]{:S(2)}) collective-permute-start(bf16[128,1024]{1,0:T(8,128)(2,1)S(1)} %get-tuple-element.43), channel_id=1, source_target_pairs={{0,8},{1,9},{2,10},{3,11},{4,12},{5,13},{6,14},{7,15},{8,0},{9,1},... | collective-permute-start | bytes 786440 | tf_op jit(solution)/shard_map/ppermute | solution.py:364
  95.5 17.4 %collective-permute-start.16 = (f32[128,128]{1,0:T(8,128)S(1)}, f32[128,128]{1,0:T(8,128)S(1)}, u32[]{:S(2)}, u32[]{:S(2)}) collective-permute-start(f32[128,128]{1,0:T(8,128)S(1)} %get-tuple-element.47), channel_id=1, source_target_pairs={{0,8},{1,9},{2,10},{3,11},{4,12},{5,13},{6,14},{7,15},{8,0},{9,1},... | collective-permute-start | bytes 196616 | tf_op jit(solution)/shard_map/ppermute | solution.py:364
  96.2 21.7 %collective-permute-start.15 = (bf16[128,1024]{1,0:T(8,128)(2,1)S(1)}, bf16[128,1024]{1,0:T(8,128)(2,1)S(1)}, u32[]{:S(2)}, u32[]{:S(2)}) collective-permute-start(bf16[128,1024]{1,0:T(8,128)(2,1)S(1)} %get-tuple-element.45), channel_id=1, source_target_pairs={{0,8},{1,9},{2,10},{3,11},{4,12},{5,13},{6,14},{7,15},{8,0},{9,1},... | collective-permute-start | bytes 786440 | tf_op jit(solution)/shard_map/ppermute | solution.py:364
  118.6 15.9 %collective-permute-start.17 = (bf16[128,2176]{1,0:T(8,128)(2,1)S(1)}, bf16[128,2176]{1,0:T(8,128)(2,1)S(1)}, u32[]{:S(2)}, u32[]{:S(2)}) collective-permute-start(bf16[128,2176]{1,0:T(8,128)(2,1)S(1)} %pad_maximum_fusion.refs_0_), channel_id=1, source_target_pairs={{0,4},{1,5},{2,6},{3,7},{4,8},{5,9},{6,10},{7,11},{8,12},{9,13},{1... | collective-permute-start | bytes 1671176 | tf_op jit(solution)/shard_map/ppermute | solution.py:364
  136.0 15.3 %collective-permute-start.18 = (bf16[128,2176]{1,0:T(8,128)(2,1)S(1)}, bf16[128,2176]{1,0:T(8,128)(2,1)S(1)}, u32[]{:S(2)}, u32[]{:S(2)}) collective-permute-start(bf16[128,2176]{1,0:T(8,128)(2,1)S(1)} %collective-permute-done.17.refs_0_), channel_id=1, source_target_pairs={{0,1},{1,0},{2,3},{3,2},{4,5},{5,4},{6,7},{7,6},{8,9},{9,8},{10,11... | collective-permute-start | bytes 1671176 | tf_op jit(solution)/shard_map/ppermute | solution.py:361
  148.0 27.0 %collective-permute-start.42 = (bf16[128,2176]{1,0:T(8,128)(2,1)S(1)}, bf16[128,2176]{1,0:T(8,128)(2,1)S(1)}, u32[]{:S(2)}, u32[]{:S(2)}) collective-permute-start(bf16[128,2176]{1,0:T(8,128)(2,1)S(1)} %pad_maximum_fusion.refs_0_), channel_id=1, source_target_pairs={{0,2},{1,3},{2,0},{3,1},{4,6},{5,7},{6,4},{7,5},{8,10},{9,11},{10,... | collective-permute-start | bytes 1671176 | tf_op jit(solution)/shard_map/ppermute | solution.py:361
  151.1 24.0 %collective-permute-start.27 = (bf16[128,2176]{1,0:T(8,128)(2,1)S(1)}, bf16[128,2176]{1,0:T(8,128)(2,1)S(1)}, u32[]{:S(2)}, u32[]{:S(2)}) collective-permute-start(bf16[128,2176]{1,0:T(8,128)(2,1)S(1)} %collective-permute-done.25.refs_0_), channel_id=1, source_target_pairs={{0,2},{1,3},{2,0},{3,1},{4,6},{5,7},{6,4},{7,5},{8,10},{9,11},{10,... | collective-permute-start | bytes 1671176 | tf_op jit(solution)/shard_map/ppermute | solution.py:361
  175.6 25.4 %collective-permute-start.33 = (bf16[128,2176]{1,0:T(8,128)(2,1)S(1)}, bf16[128,2176]{1,0:T(8,128)(2,1)S(1)}, u32[]{:S(2)}, u32[]{:S(2)}) collective-permute-start(bf16[128,2176]{1,0:T(8,128)(2,1)S(1)} %collective-permute-done.25.refs_0_), channel_id=1, source_target_pairs={{0,4},{1,5},{2,6},{3,7},{4,8},{5,9},{6,10},{7,11},{8,12},{9,13},{1... | collective-permute-start | bytes 1671176 | tf_op jit(solution)/shard_map/ppermute | solution.py:364
  175.7 25.7 %collective-permute-start.21 = (bf16[128,2048]{1,0:T(8,128)(2,1)S(1)}, bf16[128,2048]{1,0:T(8,128)(2,1)S(1)}, u32[]{:S(2)}, u32[]{:S(2)}) collective-permute-start(bf16[128,2048]{1,0:T(8,128)(2,1)S(1)} %get-tuple-element.50), channel_id=1, source_target_pairs={{0,1},{1,0},{2,3},{3,2},{4,5},{5,4},{6,7},{7,6},{8,9},{9,8},{10,11... | collective-permute-start | bytes 1572872 | tf_op jit(solution)/shard_map/ppermute | solution.py:361
  175.9 28.0 %collective-permute-start.35 = (bf16[128,2176]{1,0:T(8,128)(2,1)S(1)}, bf16[128,2176]{1,0:T(8,128)(2,1)S(1)}, u32[]{:S(2)}, u32[]{:S(2)}) collective-permute-start(bf16[128,2176]{1,0:T(8,128)(2,1)S(1)} %collective-permute-done.27.refs_2_), channel_id=1, source_target_pairs={{0,4},{1,5},{2,6},{3,7},{4,8},{5,9},{6,10},{7,11},{8,12},{9,13},{1... | collective-permute-start | bytes 1671176 | tf_op jit(solution)/shard_map/ppermute | solution.py:364
  177.0 26.9 %collective-permute-start.23 = (bf16[128,2048]{1,0:T(8,128)(2,1)S(1)}, bf16[128,2048]{1,0:T(8,128)(2,1)S(1)}, u32[]{:S(2)}, u32[]{:S(2)}) collective-permute-start(bf16[128,2048]{1,0:T(8,128)(2,1)S(1)} %add_convert_fusion.3), channel_id=1, source_target_pairs={{0,2},{1,3},{2,0},{3,1},{4,6},{5,7},{6,4},{7,5},{8,10},{9,11},{10,... | collective-permute-start | bytes 1572872 | tf_op jit(solution)/shard_map/ppermute | solution.py:361
  200.9 17.1 %collective-permute-start.45 = (bf16[128,2048]{1,0:T(8,128)(2,1)S(1)}, bf16[128,2048]{1,0:T(8,128)(2,1)S(1)}, u32[]{:S(2)}, u32[]{:S(2)}) collective-permute-start(bf16[128,2048]{1,0:T(8,128)(2,1)S(1)} %get-tuple-element.64), channel_id=1, source_target_pairs={{0,1},{1,0},{2,3},{3,2},{4,5},{5,4},{6,7},{7,6},{8,9},{9,8},{10,11... | collective-permute-start | bytes 1572872 | tf_op jit(solution)/shard_map/ppermute | solution.py:361
  204.7 15.9 %collective-permute-start.24 = (bf16[128,2048]{1,0:T(8,128)(2,1)S(1)}, bf16[128,2048]{1,0:T(8,128)(2,1)S(1)}, u32[]{:S(2)}, u32[]{:S(2)}) collective-permute-start(bf16[128,2048]{1,0:T(8,128)(2,1)S(1)} %add_convert_fusion.2), channel_id=1, source_target_pairs={{0,4},{1,5},{2,6},{3,7},{4,8},{5,9},{6,10},{7,11},{8,12},{9,13},{1... | collective-permute-start | bytes 1572872 | tf_op jit(solution)/shard_map/ppermute | solution.py:364
  205.1 15.5 %collective-permute-start.31 = (bf16[128,2048]{1,0:T(8,128)(2,1)S(1)}, bf16[128,2048]{1,0:T(8,128)(2,1)S(1)}, u32[]{:S(2)}, u32[]{:S(2)}) collective-permute-start(bf16[128,2048]{1,0:T(8,128)(2,1)S(1)} %add_convert_fusion.1), channel_id=1, source_target_pairs={{0,2},{1,3},{2,0},{3,1},{4,6},{5,7},{6,4},{7,5},{8,10},{9,11},{10,... | collective-permute-start | bytes 1572872 | tf_op jit(solution)/shard_map/ppermute | solution.py:361
  221.0 17.0 %collective-permute-start.32 = (bf16[128,1152]{1,0:T(8,128)(2,1)S(1)}, bf16[128,1152]{1,0:T(8,128)(2,1)S(1)}, u32[]{:S(2)}, u32[]{:S(2)}) collective-permute-start(bf16[128,1152]{1,0:T(8,128)(2,1)S(1)} %slice.151), channel_id=1, source_target_pairs={{0,4},{1,5},{2,6},{3,7},{4,8},{5,9},{6,10},{7,11},{8,12},{9,13},{1... | collective-permute-start | bytes 884744 | tf_op jit(solution)/shard_map/ppermute | solution.py:364
  222.6 16.7 %collective-permute-start.39 = (bf16[128,1152]{1,0:T(8,128)(2,1)S(1)}, bf16[128,1152]{1,0:T(8,128)(2,1)S(1)}, u32[]{:S(2)}, u32[]{:S(2)}) collective-permute-start(bf16[128,1152]{1,0:T(8,128)(2,1)S(1)} %add_convert_fusion.6), channel_id=1, source_target_pairs={{0,2},{1,3},{2,0},{3,1},{4,6},{5,7},{6,4},{7,5},{8,10},{9,11},{10,... | collective-permute-start | bytes 884744 | tf_op jit(solution)/shard_map/ppermute | solution.py:361
  224.9 18.2 %collective-permute-start.44 = (bf16[128,2048]{1,0:T(8,128)(2,1)S(1)}, bf16[128,2048]{1,0:T(8,128)(2,1)S(1)}, u32[]{:S(2)}, u32[]{:S(2)}) collective-permute-start(bf16[128,2048]{1,0:T(8,128)(2,1)S(1)} %get-tuple-element.62), channel_id=1, source_target_pairs={{0,1},{1,0},{2,3},{3,2},{4,5},{5,4},{6,7},{7,6},{8,9},{9,8},{10,11... | collective-permute-start | bytes 1572872 | tf_op jit(solution)/shard_map/ppermute | solution.py:361
  (64 other events, 756.0 us)

commit v6 on v5

--- a/solution.py
+++ b/solution.py
@@ -215,6 +215,7 @@
 
 def project(place, gains, acts, weights, start, steps, columns, squared):
     depth, tok, width = acts[0].shape
+    model = weights[0].shape[1]
     part = steps * columns
     cost = pl.CostEstimate(
         flops=16 * depth * tok * width * part,
@@ -234,7 +235,15 @@
             grid=(steps,),
             in_specs=[pl.BlockSpec(gains.shape, lambda i, place: (0, 0))]
             + [pl.BlockSpec((depth, tok, width), lambda i, place: (0, 0, 0))] * 8
-            + [pl.BlockSpec((width, columns), lambda i, place: (0, start + i))] * 8,
+            + [
+                pl.BlockSpec(
+                    (width, columns),
+                    functools.partial(
+                        lambda first, i, place: (0, first + i), start if w.shape[1] == model else 0
+                    ),
+                )
+                for w in weights
+            ],
             out_specs=out_specs,
         ),
         compiler_params=pltpu.CompilerParams(vmem_limit_bytes=20 * 1024 * 1024),
@@ -364,11 +373,16 @@
         return lax.ppermute(x, "mix", [(i, (i + stride) % devices) for i in range(devices)])
 
     proj_y, proj_z = cross(out_proj, 2), cross(out_proj, 4)
-    proj_yz = lax.ppermute(
-        jnp.where(me % 2 == 0, proj_y, proj_z),
-        "mix",
-        [(i, i ^ (2 if i % 2 else 4)) for i in range(devices)],
-    )
+    proj_yz = jnp.where(me % 2 == 0, proj_y, proj_z)
+    diagonal = []
+    for half in range(2):
+        diagonal.append(
+            lax.ppermute(
+                proj_yz[:, half * model // 2 : (half + 1) * model // 2],
+                "mix",
+                [(i, i ^ (2 if i % 2 else 4)) for i in range(devices)],
+            )
+        )
     gains = norm_gain.reshape(devices, width)
 
     slots = placement.shape[0]
@@ -388,12 +402,13 @@
         place, depth // 2,
     )
     projs = []
-    for block in (out_proj, proj_y, proj_z, proj_yz):
+    for block in (out_proj, proj_y, proj_z):
         projs += [block, cross(block, 1)]
     acts = [gated[0]] + [cross(gated[mask], mask) for mask in range(1, 8)]
     sums = []
     for half, (start, steps) in enumerate(((0, 2), (2, 2))):
-        mixed, squares = project(place, gains, acts, projs, start, steps, model // 4, half == 1)
+        across = [diagonal[half], cross(diagonal[half], 1)]
+        mixed, squares = project(place, gains, acts, projs + across, start, steps, model // 4, half == 1)
         total = mixed[1]
         if half == 1:
             norm = squares[1]

time: 253 us -> 226 us (0.89)
  waiting for transfers between devices: 130 us -> 99.4 us
  local copies, waits for them, and re-layouts: 10.6 us -> 13.8 us
  starting transfers between devices: 40.4 us -> 43.3 us
    ppermute x38 -> x39, waiting for transfers between devices: 75.9 us -> 37.3 us  [cross(): return lax.ppermute(x, 'mix', [(i, i ^ mask) for i in range(devices)])]
    ppermute x1 -> x2, waiting for transfers between devices: 0.01 us -> 7.12 us  [local(): lax.ppermute(proj_yz[:, half * model // 2:(half + 1) * model // 2], 'mix'...]
    unnamed x74 -> x36, local copies, waits for them, and re-layouts: 8.5 us -> 9.94 us
    ppermute x38 -> x39, starting transfers between devices: 26.8 us -> 27.4 us  [cross(): return lax.ppermute(x, 'mix', [(i, i ^ mask) for i in range(devices)])]
  transfers between devices with their start and end apart: 51 -> 53, of which waited for: 21 -> 20; matrix products, arithmetic and copies ran while one was open for 2% -> 3% of each run, Pallas kernels for 25% -> 29%
where the time goes in v6:
time: 226 us; the launch traced here: 225 us
  waiting for transfers between devices  99.4 us (44%)
  Pallas kernels  64.5 us (29%)
  starting transfers between devices  43.3 us (19%)
  local copies, waits for them, and re-layouts  13.8 us (6%)
  other arithmetic  3.84 us (2%)
    ppermute x12, waiting for transfers between devices, onward(): lax.ppermute(x, 'mix', [(i, (i + stride) % devices) for i in range(device...  55 us
    pallas_call x4, Pallas kernels, run_experts(): pl.pallas_call(functools.partial(expert_kernel, blocks=blocks, cap=cap),...  44.1 us
    ppermute x39, waiting for transfers between devices, cross(): return lax.ppermute(x, 'mix', [(i, i ^ mask) for i in range(devices)])  37.3 us
    ppermute x39, starting transfers between devices, cross(): return lax.ppermute(x, 'mix', [(i, i ^ mask) for i in range(devices)])  27.4 us
    pallas_call x1, Pallas kernels, scan_heads(): pl.pallas_call(functools.partial(scan_kernel, span=span, chunks=chunks),...  14.6 us
    ppermute x12, starting transfers between devices, onward(): lax.ppermute(x, 'mix', [(i, (i + stride) % devices) for i in range(device...  13.8 us
    unnamed x36, local copies, waits for them, and re-layouts  9.94 us
    ppermute x2, waiting for transfers between devices, local(): lax.ppermute(proj_yz[:, half * model // 2:(half + 1) * model // 2], 'mix'...  7.12 us
  transfers between devices with their start and end apart: 53, of which 20 were waited for; matrix products, arithmetic and copies ran while one was open for 3% of the time, Pallas kernels for 29%

profile of v6, /device:TPU:0, one launch (start us, length us, event | category | flops | bytes accessed | tf_op | source)
XLA Modules:
  0.0 225.4 jit_solution(13833884094837372804)
XLA Ops:
  0.0 3.1 %collective-permute-start.10 = (bf16[256,2048]{1,0:T(8,128)(2,1)}, bf16[256,2048]{1,0:T(8,128)(2,1)S(1)}, u32[]{:S(2)}, u32[]{:S(2)}) collective-permute-start(bf16[256,2048]{1,0:T(8,128)(2,1)} %refs_9_.3), channel_id=1, source_target_pairs={{0,4},{1,5},{2,6},{3,7},{4,0},{5,1},{6,2},{7,3},{8,12},{9,13},{10,... | collective-permute-start | bytes 3145736 | tf_op jit(solution)/shard_map/ppermute | solution.py:370
  4.6 14.6 %scan.1 = (bf16[2,128,256]{2,1,0:T(8,128)(2,1)}, bf16[2,128,256]{2,1,0:T(8,128)(2,1)}, bf16[2,128,256]{2,1,0:T(8,128)(2,1)}, bf16[2,128,256]{2,1,0:T(8,128)(2,1)...) custom-call(s32[8]{0:T(128)} %lengths.1, ...), custom_call_target="tpu_custom_call" | custom-call | flops 939524096 | bytes 3145728 | tf_op jit(solution)/shard_map/scan/pallas_call | solution.py:165
  21.1 5.4 %collective-permute-done.10.refs_13_ = bf16[256,2048]{1,0:T(8,128)(2,1)S(1)} collective-permute-done((bf16[256,2048]{1,0:T(8,128)(2,1)}, bf16[256,2048]{1,0:T(8,128)(2,1)S(1)}, u32[]{:S(2)}, u32[]{:S(2)}) %collective-permute-start.10) | collective-permute-done | bytes 1048608 | tf_op jit(solution)/shard_map/ppermute | solution.py:370
  39.6 2.3 %collective-permute-done.6.refs_8_ = bf16[2,128,256]{2,1,0:T(8,128)(2,1)S(1)} collective-permute-done((bf16[2,128,256]{2,1,0:T(8,128)(2,1)}, bf16[2,128,256]{2,1,0:T(8,128)(2,1)S(1)}, u32[]{:S(2)}, u32[]{:S(2)}) %collective-permute-start.6) | collective-permute-done | bytes 131104 | tf_op jit(solution)/shard_map/ppermute | solution.py:370
  47.0 5.1 %collective-permute-done.15.refs_15_ = bf16[256,1024]{1,0:T(8,128)(2,1)} collective-permute-done((bf16[256,1024]{1,0:T(8,128)(2,1)}, bf16[256,1024]{1,0:T(8,128)(2,1)}, u32[]{:S(2)}, u32[]{:S(2)}) %collective-permute-start.15) | collective-permute-done | bytes 524320 | tf_op jit(solution)/shard_map/ppermute | solution.py:380
  58.8 2.7 %project.2 = (bf16[128,1024]{1,0:T(8,128)(2,1)S(1)}, bf16[128,1024]{1,0:T(8,128)(2,1)S(1)}) custom-call(s32[1]{0:T(128)} %bitcast.place, f32[16,256]{1,0:T(8,128)S(1)} %reshape.15.refs_0_, bf16[2,128,256]{2,1,0:T(8,128)(2,1)S(1)} %copy-done.2, bf16[2,128,256]{2,1,0:T(8,128)(2,1)S(1)} %collective-permute-done.refs_2_, ...), custom_call_target="tpu_custom_call" | custom-call | flops 1073741824 | bytes 5767168 | tf_op jit(solution)/shard_map/project/pallas_call | solution.py:230
  61.6 2.7 %collective-permute-start.14 = (bf16[128,1024]{1,0:T(8,128)(2,1)S(1)}, bf16[128,1024]{1,0:T(8,128)(2,1)S(1)}, u32[]{:S(2)}, u32[]{:S(2)}) collective-permute-start(bf16[128,1024]{1,0:T(8,128)(2,1)S(1)} %get-tuple-element.43), channel_id=1, source_target_pairs={{0,8},{1,9},{2,10},{3,11},{4,12},{5,13},{6,14},{7,15},{8,0},{9,1},... | collective-permute-start | bytes 786440 | tf_op jit(solution)/shard_map/ppermute | solution.py:373
  64.3 3.1 %project.3 = (bf16[128,1024]{1,0:T(8,128)(2,1)S(1)}, bf16[128,1024]{1,0:T(8,128)(2,1)S(1)}, f32[128,128]{1,0:T(8,128)S(1)}, f32[128,128]{1,0:T(8,128)S(1)}) custom-call(s32[1]{0:T(128)} %bitcast.place, f32[16,256]{1,0:T(8,128)S(1)} %reshape.15.refs_0_, bf16[2,128,256]{2,1,0:T(8,128)(2,1)S(1)} %copy-done.2, ...), custom_call_target="tpu_custom_call" | custom-call | flops 1073741824 | bytes 5767168 | tf_op jit(solution)/shard_map/project/pallas_call | solution.py:230
  68.2 2.7 %collective-permute-start.17 = (bf16[128,1024]{1,0:T(8,128)(2,1)S(1)}, bf16[128,1024]{1,0:T(8,128)(2,1)S(1)}, u32[]{:S(2)}, u32[]{:S(2)}) collective-permute-start(bf16[128,1024]{1,0:T(8,128)(2,1)S(1)} %get-tuple-element.45), channel_id=1, source_target_pairs={{0,8},{1,9},{2,10},{3,11},{4,12},{5,13},{6,14},{7,15},{8,0},{9,1},... | collective-permute-start | bytes 786440 | tf_op jit(solution)/shard_map/ppermute | solution.py:373
  70.8 15.0 %collective-permute-done.18 = f32[128,128]{1,0:T(8,128)S(1)} collective-permute-done((f32[128,128]{1,0:T(8,128)S(1)}, f32[128,128]{1,0:T(8,128)S(1)}, u32[]{:S(2)}, u32[]{:S(2)}) %collective-permute-start.18) | collective-permute-done | bytes 65568 | tf_op jit(solution)/shard_map/ppermute | solution.py:373
  86.0 4.7 %collective-permute-done.17 = bf16[128,1024]{1,0:T(8,128)(2,1)S(1)} collective-permute-done((bf16[128,1024]{1,0:T(8,128)(2,1)S(1)}, bf16[128,1024]{1,0:T(8,128)(2,1)S(1)}, u32[]{:S(2)}, u32[]{:S(2)}) %collective-permute-start.17) | collective-permute-done | bytes 262176 | tf_op jit(solution)/shard_map/ppermute | solution.py:373
  92.0 15.5 %collective-permute-done.19.refs_0_ = bf16[128,2176]{1,0:T(8,128)(2,1)S(1)} collective-permute-done((bf16[128,2176]{1,0:T(8,128)(2,1)S(1)}, bf16[128,2176]{1,0:T(8,128)(2,1)S(1)}, u32[]{:S(2)}, u32[]{:S(2)}) %collective-permute-start.19) | collective-permute-done | bytes 557088 | tf_op jit(solution)/shard_map/ppermute | solution.py:373
  108.8 12.0 %collective-permute-done.21.refs_2_ = bf16[128,2176]{1,0:T(8,128)(2,1)S(1)} collective-permute-done((bf16[128,2176]{1,0:T(8,128)(2,1)S(1)}, bf16[128,2176]{1,0:T(8,128)(2,1)S(1)}, u32[]{:S(2)}, u32[]{:S(2)}) %collective-permute-start.21) | collective-permute-done | bytes 557088 | tf_op jit(solution)/shard_map/ppermute | solution.py:370
  124.3 2.8 %copy-done = bf16[2,2048,768]{2,1,0:T(8,128)(2,1)S(1)} copy-done((bf16[2,2048,768]{2,1,0:T(8,128)(2,1)S(1)}, bf16[2,2048,768]{2,1,0:T(8,128)(2,1)}, u32[]{:S(2)}) %copy-start) | copy-done | bytes 6291480
  127.1 11.0 %experts.4 = (bf16[128,2048]{1,0:T(8,128)(2,1)S(1)}, bf16[128,2048]{1,0:T(8,128)(2,1)S(1)}, bf16[128,2048]{1,0:T(8,128)(2,1)S(1)}, bf16[128,2048]{1,0:T(8,128)(2,1)S(1)}) custom-call(s32[1]{0:T(128)} %bitcast.place, s32[128,1]{1,0:T(8,128)S(1)} %copy.23.owner_ref, bf16[128,2176]{1,0:T(8,128)(2,1)S(1)} %collective-permute-done.19.refs_0_, ...), custom_call_target="tpu_custom_call" | custom-call | flops 4831838208 | bytes 23068672 | tf_op jit(solution)/shard_map/experts/pallas_call | solution.py:325
  138.8 9.2 %collective-permute-done.29.refs_2_ = bf16[128,2176]{1,0:T(8,128)(2,1)S(1)} collective-permute-done((bf16[128,2176]{1,0:T(8,128)(2,1)S(1)}, bf16[128,2176]{1,0:T(8,128)(2,1)S(1)}, u32[]{:S(2)}, u32[]{:S(2)}) %collective-permute-start.29) | collective-permute-done | bytes 557088 | tf_op jit(solution)/shard_map/ppermute | solution.py:370
  151.7 11.0 %experts.5 = (bf16[128,2048]{1,0:T(8,128)(2,1)S(1)}, bf16[128,2048]{1,0:T(8,128)(2,1)S(1)}, bf16[128,2048]{1,0:T(8,128)(2,1)S(1)}, bf16[128,2048]{1,0:T(8,128)(2,1)S(1)}) custom-call(s32[1]{0:T(128)} %bitcast.place, s32[128,1]{1,0:T(8,128)S(1)} %copy.23.owner_ref, bf16[128,2176]{1,0:T(8,128)(2,1)S(1)} %collective-permute-done.27.refs_0_, ...), custom_call_target="tpu_custom_call" | custom-call | flops 4831838208 | bytes 23068672 | tf_op jit(solution)/shard_map/experts/pallas_call | solution.py:325
  162.8 11.0 %experts.7 = (bf16[128,2048]{1,0:T(8,128)(2,1)S(1)}, bf16[128,2048]{1,0:T(8,128)(2,1)S(1)}, bf16[128,2048]{1,0:T(8,128)(2,1)S(1)}, bf16[128,2048]{1,0:T(8,128)(2,1)S(1)}) custom-call(s32[1]{0:T(128)} %bitcast.place, s32[128,1]{1,0:T(8,128)S(1)} %copy.23.owner_ref, bf16[128,2176]{1,0:T(8,128)(2,1)S(1)} %pad_maximum_fusion.refs_0_, ...), custom_call_target="tpu_custom_call" | custom-call | flops 4831838208 | bytes 23068672 | tf_op jit(solution)/shard_map/experts/pallas_call | solution.py:325
  174.5 2.4 %collective-permute-done.37.refs_2_ = bf16[128,2176]{1,0:T(8,128)(2,1)S(1)} collective-permute-done((bf16[128,2176]{1,0:T(8,128)(2,1)S(1)}, bf16[128,2176]{1,0:T(8,128)(2,1)S(1)}, u32[]{:S(2)}, u32[]{:S(2)}) %collective-permute-start.37) | collective-permute-done | bytes 557088 | tf_op jit(solution)/shard_map/ppermute | solution.py:373
  179.9 11.0 %experts.6 = (bf16[128,2048]{1,0:T(8,128)(2,1)S(1)}, bf16[128,2048]{1,0:T(8,128)(2,1)S(1)}, bf16[128,2048]{1,0:T(8,128)(2,1)S(1)}, bf16[128,2048]{1,0:T(8,128)(2,1)S(1)}) custom-call(s32[1]{0:T(128)} %bitcast.place, s32[128,1]{1,0:T(8,128)S(1)} %copy.23.owner_ref, bf16[128,2176]{1,0:T(8,128)(2,1)S(1)} %collective-permute-done.35.refs_0_, ...), custom_call_target="tpu_custom_call" | custom-call | flops 4831838208 | bytes 23068672 | tf_op jit(solution)/shard_map/experts/pallas_call | solution.py:325
  197.9 10.9 %collective-permute-done.49 = bf16[128,896]{1,0:T(8,128)(2,1)S(1)} collective-permute-done((bf16[128,896]{1,0:T(8,128)(2,1)S(1)}, bf16[128,896]{1,0:T(8,128)(2,1)S(1)}, u32[]{:S(2)}, u32[]{:S(2)}) %collective-permute-start.49) | collective-permute-done | bytes 229408 | tf_op jit(solution)/shard_map/ppermute | solution.py:373
  212.4 3.6 %collective-permute-start.42 = (bf16[128,1152]{1,0:T(8,128)(2,1)S(1)}, bf16[128,1152]{1,0:T(8,128)(2,1)S(1)}, u32[]{:S(2)}, u32[]{:S(2)}) collective-permute-start(bf16[128,1152]{1,0:T(8,128)(2,1)S(1)} %add_convert_fusion.5), channel_id=1, source_target_pairs={{0,4},{1,5},{2,6},{3,7},{4,8},{5,9},{6,10},{7,11},{8,12},{9,13},{1... | collective-permute-start | bytes 884744 | tf_op jit(solution)/shard_map/ppermute | solution.py:373
  216.0 4.9 %collective-permute-done.52 = bf16[128,896]{1,0:T(8,128)(2,1)S(1)} collective-permute-done((bf16[128,896]{1,0:T(8,128)(2,1)S(1)}, bf16[128,896]{1,0:T(8,128)(2,1)S(1)}, u32[]{:S(2)}, u32[]{:S(2)}) %collective-permute-start.52) | collective-permute-done | bytes 229408 | tf_op jit(solution)/shard_map/ppermute | solution.py:370
  221.4 3.0 %collective-permute-done.42 = bf16[128,1152]{1,0:T(8,128)(2,1)S(1)} collective-permute-done((bf16[128,1152]{1,0:T(8,128)(2,1)S(1)}, bf16[128,1152]{1,0:T(8,128)(2,1)S(1)}, u32[]{:S(2)}, u32[]{:S(2)}) %collective-permute-start.42) | collective-permute-done | bytes 294944 | tf_op jit(solution)/shard_map/ppermute | solution.py:373
  (160 shorter events, 55.3 us)
Async XLA Ops:
  0.0 26.5 %collective-permute-start.10 = (bf16[256,2048]{1,0:T(8,128)(2,1)}, bf16[256,2048]{1,0:T(8,128)(2,1)S(1)}, u32[]{:S(2)}, u32[]{:S(2)}) collective-permute-start(bf16[256,2048]{1,0:T(8,128)(2,1)} %refs_9_.3), channel_id=1, source_target_pairs={{0,4},{1,5},{2,6},{3,7},{4,0},{5,1},{6,2},{7,3},{8,12},{9,13},{10,... | collective-permute-start | bytes 3145736 | tf_op jit(solution)/shard_map/ppermute | solution.py:370
  3.1 26.2 %collective-permute-start.8 = (bf16[256,2048]{1,0:T(8,128)(2,1)}, bf16[256,2048]{1,0:T(8,128)(2,1)S(1)}, u32[]{:S(2)}, u32[]{:S(2)}) collective-permute-start(bf16[256,2048]{1,0:T(8,128)(2,1)} %refs_9_.3), channel_id=1, source_target_pairs={{0,2},{1,3},{2,0},{3,1},{4,6},{5,7},{6,4},{7,5},{8,10},{9,11},{10,... | collective-permute-start | bytes 3145736 | tf_op jit(solution)/shard_map/ppermute | solution.py:370
  35.6 18.7 %collective-permute-start.7 = (bf16[256,2048]{1,0:T(8,128)(2,1)S(1)}, bf16[256,2048]{1,0:T(8,128)(2,1)}, u32[]{:S(2)}, u32[]{:S(2)}) collective-permute-start(bf16[256,2048]{1,0:T(8,128)(2,1)S(1)} %copy-done.1), channel_id=1, source_target_pairs={{0,1},{1,0},{2,3},{3,2},{4,5},{5,4},{6,7},{7,6},{8,9},{9,8},{10,11... | collective-permute-start | bytes 3145736 | tf_op jit(solution)/shard_map/ppermute | solution.py:370
  36.3 18.0 %collective-permute-start.11 = (bf16[256,2048]{1,0:T(8,128)(2,1)S(1)}, bf16[256,2048]{1,0:T(8,128)(2,1)}, u32[]{:S(2)}, u32[]{:S(2)}) collective-permute-start(bf16[256,2048]{1,0:T(8,128)(2,1)S(1)} %collective-permute-done.10.refs_13_), channel_id=1, source_target_pairs={{0,1},{1,0},{2,3},{3,2},{4,5},{5,4},{6,7},{7,6},{8,9},{9,8},{10,11... | collective-permute-start | bytes 3145736 | tf_op jit(solution)/shard_map/ppermute | solution.py:370
  38.3 16.0 %collective-permute-start.9 = (bf16[256,2048]{1,0:T(8,128)(2,1)S(1)}, bf16[256,2048]{1,0:T(8,128)(2,1)}, u32[]{:S(2)}, u32[]{:S(2)}) collective-permute-start(bf16[256,2048]{1,0:T(8,128)(2,1)S(1)} %collective-permute-done.8.refs_11_), channel_id=1, source_target_pairs={{0,1},{1,0},{2,3},{3,2},{4,5},{5,4},{6,7},{7,6},{8,9},{9,8},{10,11... | collective-permute-start | bytes 3145736 | tf_op jit(solution)/shard_map/ppermute | solution.py:370
  61.6 24.3 %collective-permute-start.14 = (bf16[128,1024]{1,0:T(8,128)(2,1)S(1)}, bf16[128,1024]{1,0:T(8,128)(2,1)S(1)}, u32[]{:S(2)}, u32[]{:S(2)}) collective-permute-start(bf16[128,1024]{1,0:T(8,128)(2,1)S(1)} %get-tuple-element.43), channel_id=1, source_target_pairs={{0,8},{1,9},{2,10},{3,11},{4,12},{5,13},{6,14},{7,15},{8,0},{9,1},... | collective-permute-start | bytes 786440 | tf_op jit(solution)/shard_map/ppermute | solution.py:373
  67.4 18.4 %collective-permute-start.18 = (f32[128,128]{1,0:T(8,128)S(1)}, f32[128,128]{1,0:T(8,128)S(1)}, u32[]{:S(2)}, u32[]{:S(2)}) collective-permute-start(f32[128,128]{1,0:T(8,128)S(1)} %get-tuple-element.47), channel_id=1, source_target_pairs={{0,8},{1,9},{2,10},{3,11},{4,12},{5,13},{6,14},{7,15},{8,0},{9,1},... | collective-permute-start | bytes 196616 | tf_op jit(solution)/shard_map/ppermute | solution.py:373
  68.2 22.6 %collective-permute-start.17 = (bf16[128,1024]{1,0:T(8,128)(2,1)S(1)}, bf16[128,1024]{1,0:T(8,128)(2,1)S(1)}, u32[]{:S(2)}, u32[]{:S(2)}) collective-permute-start(bf16[128,1024]{1,0:T(8,128)(2,1)S(1)} %get-tuple-element.45), channel_id=1, source_target_pairs={{0,8},{1,9},{2,10},{3,11},{4,12},{5,13},{6,14},{7,15},{8,0},{9,1},... | collective-permute-start | bytes 786440 | tf_op jit(solution)/shard_map/ppermute | solution.py:373
  91.4 16.1 %collective-permute-start.19 = (bf16[128,2176]{1,0:T(8,128)(2,1)S(1)}, bf16[128,2176]{1,0:T(8,128)(2,1)S(1)}, u32[]{:S(2)}, u32[]{:S(2)}) collective-permute-start(bf16[128,2176]{1,0:T(8,128)(2,1)S(1)} %pad_maximum_fusion.refs_0_), channel_id=1, source_target_pairs={{0,4},{1,5},{2,6},{3,7},{4,8},{5,9},{6,10},{7,11},{8,12},{9,13},{1... | collective-permute-start | bytes 1671176 | tf_op jit(solution)/shard_map/ppermute | solution.py:373
  108.8 15.2 %collective-permute-start.27 = (bf16[128,2176]{1,0:T(8,128)(2,1)S(1)}, bf16[128,2176]{1,0:T(8,128)(2,1)S(1)}, u32[]{:S(2)}, u32[]{:S(2)}) collective-permute-start(bf16[128,2176]{1,0:T(8,128)(2,1)S(1)} %collective-permute-done.19.refs_0_), channel_id=1, source_target_pairs={{0,4},{1,5},{2,6},{3,7},{4,8},{5,9},{6,10},{7,11},{8,12},{9,13},{1... | collective-permute-start | bytes 1671176 | tf_op jit(solution)/shard_map/ppermute | solution.py:373
  108.8 15.5 %collective-permute-start.20 = (bf16[128,2176]{1,0:T(8,128)(2,1)S(1)}, bf16[128,2176]{1,0:T(8,128)(2,1)S(1)}, u32[]{:S(2)}, u32[]{:S(2)}) collective-permute-start(bf16[128,2176]{1,0:T(8,128)(2,1)S(1)} %collective-permute-done.19.refs_0_), channel_id=1, source_target_pairs={{0,1},{1,0},{2,3},{3,2},{4,5},{5,4},{6,7},{7,6},{8,9},{9,8},{10,11... | collective-permute-start | bytes 1671176 | tf_op jit(solution)/shard_map/ppermute | solution.py:370
  121.0 27.0 %collective-permute-start.44 = (bf16[128,2176]{1,0:T(8,128)(2,1)S(1)}, bf16[128,2176]{1,0:T(8,128)(2,1)S(1)}, u32[]{:S(2)}, u32[]{:S(2)}) collective-permute-start(bf16[128,2176]{1,0:T(8,128)(2,1)S(1)} %pad_maximum_fusion.refs_0_), channel_id=1, source_target_pairs={{0,2},{1,3},{2,0},{3,1},{4,6},{5,7},{6,4},{7,5},{8,10},{9,11},{10,... | collective-permute-start | bytes 1671176 | tf_op jit(solution)/shard_map/ppermute | solution.py:370
  124.0 24.0 %collective-permute-start.29 = (bf16[128,2176]{1,0:T(8,128)(2,1)S(1)}, bf16[128,2176]{1,0:T(8,128)(2,1)S(1)}, u32[]{:S(2)}, u32[]{:S(2)}) collective-permute-start(bf16[128,2176]{1,0:T(8,128)(2,1)S(1)} %collective-permute-done.27.refs_0_), channel_id=1, source_target_pairs={{0,2},{1,3},{2,0},{3,1},{4,6},{5,7},{6,4},{7,5},{8,10},{9,11},{10,... | collective-permute-start | bytes 1671176 | tf_op jit(solution)/shard_map/ppermute | solution.py:370
  148.5 25.3 %collective-permute-start.35 = (bf16[128,2176]{1,0:T(8,128)(2,1)S(1)}, bf16[128,2176]{1,0:T(8,128)(2,1)S(1)}, u32[]{:S(2)}, u32[]{:S(2)}) collective-permute-start(bf16[128,2176]{1,0:T(8,128)(2,1)S(1)} %collective-permute-done.27.refs_0_), channel_id=1, source_target_pairs={{0,4},{1,5},{2,6},{3,7},{4,8},{5,9},{6,10},{7,11},{8,12},{9,13},{1... | collective-permute-start | bytes 1671176 | tf_op jit(solution)/shard_map/ppermute | solution.py:373
  148.7 25.7 %collective-permute-start.23 = (bf16[128,2048]{1,0:T(8,128)(2,1)S(1)}, bf16[128,2048]{1,0:T(8,128)(2,1)S(1)}, u32[]{:S(2)}, u32[]{:S(2)}) collective-permute-start(bf16[128,2048]{1,0:T(8,128)(2,1)S(1)} %get-tuple-element.50), channel_id=1, source_target_pairs={{0,1},{1,0},{2,3},{3,2},{4,5},{5,4},{6,7},{7,6},{8,9},{9,8},{10,11... | collective-permute-start | bytes 1572872 | tf_op jit(solution)/shard_map/ppermute | solution.py:370
  148.8 28.0 %collective-permute-start.37 = (bf16[128,2176]{1,0:T(8,128)(2,1)S(1)}, bf16[128,2176]{1,0:T(8,128)(2,1)S(1)}, u32[]{:S(2)}, u32[]{:S(2)}) collective-permute-start(bf16[128,2176]{1,0:T(8,128)(2,1)S(1)} %collective-permute-done.29.refs_2_), channel_id=1, source_target_pairs={{0,4},{1,5},{2,6},{3,7},{4,8},{5,9},{6,10},{7,11},{8,12},{9,13},{1... | collective-permute-start | bytes 1671176 | tf_op jit(solution)/shard_map/ppermute | solution.py:373
  150.0 26.9 %collective-permute-start.25 = (bf16[128,2048]{1,0:T(8,128)(2,1)S(1)}, bf16[128,2048]{1,0:T(8,128)(2,1)S(1)}, u32[]{:S(2)}, u32[]{:S(2)}) collective-permute-start(bf16[128,2048]{1,0:T(8,128)(2,1)S(1)} %add_convert_fusion.3), channel_id=1, source_target_pairs={{0,2},{1,3},{2,0},{3,1},{4,6},{5,7},{6,4},{7,5},{8,10},{9,11},{10,... | collective-permute-start | bytes 1572872 | tf_op jit(solution)/shard_map/ppermute | solution.py:370
  162.7 14.9 %collective-permute-start.32 = (bf16[128,2048]{1,0:T(8,128)(2,1)S(1)}, bf16[128,2048]{1,0:T(8,128)(2,1)S(1)}, u32[]{:S(2)}, u32[]{:S(2)}) collective-permute-start(bf16[128,2048]{1,0:T(8,128)(2,1)S(1)} %get-tuple-element.56), channel_id=1, source_target_pairs={{0,1},{1,0},{2,3},{3,2},{4,5},{5,4},{6,7},{7,6},{8,9},{9,8},{10,11... | collective-permute-start | bytes 1572872 | tf_op jit(solution)/shard_map/ppermute | solution.py:370
  173.9 17.1 %collective-permute-start.47 = (bf16[128,2048]{1,0:T(8,128)(2,1)S(1)}, bf16[128,2048]{1,0:T(8,128)(2,1)S(1)}, u32[]{:S(2)}, u32[]{:S(2)}) collective-permute-start(bf16[128,2048]{1,0:T(8,128)(2,1)S(1)} %get-tuple-element.64), channel_id=1, source_target_pairs={{0,1},{1,0},{2,3},{3,2},{4,5},{5,4},{6,7},{7,6},{8,9},{9,8},{10,11... | collective-permute-start | bytes 1572872 | tf_op jit(solution)/shard_map/ppermute | solution.py:370
  177.6 15.9 %collective-permute-start.26 = (bf16[128,2048]{1,0:T(8,128)(2,1)S(1)}, bf16[128,2048]{1,0:T(8,128)(2,1)S(1)}, u32[]{:S(2)}, u32[]{:S(2)}) collective-permute-start(bf16[128,2048]{1,0:T(8,128)(2,1)S(1)} %add_convert_fusion.2), channel_id=1, source_target_pairs={{0,4},{1,5},{2,6},{3,7},{4,8},{5,9},{6,10},{7,11},{8,12},{9,13},{1... | collective-permute-start | bytes 1572872 | tf_op jit(solution)/shard_map/ppermute | solution.py:373
  178.1 15.5 %collective-permute-start.33 = (bf16[128,2048]{1,0:T(8,128)(2,1)S(1)}, bf16[128,2048]{1,0:T(8,128)(2,1)S(1)}, u32[]{:S(2)}, u32[]{:S(2)}) collective-permute-start(bf16[128,2048]{1,0:T(8,128)(2,1)S(1)} %add_convert_fusion.1), channel_id=1, source_target_pairs={{0,2},{1,3},{2,0},{3,1},{4,6},{5,7},{6,4},{7,5},{8,10},{9,11},{10,... | collective-permute-start | bytes 1572872 | tf_op jit(solution)/shard_map/ppermute | solution.py:370
  194.0 17.0 %collective-permute-start.34 = (bf16[128,1152]{1,0:T(8,128)(2,1)S(1)}, bf16[128,1152]{1,0:T(8,128)(2,1)S(1)}, u32[]{:S(2)}, u32[]{:S(2)}) collective-permute-start(bf16[128,1152]{1,0:T(8,128)(2,1)S(1)} %slice.161), channel_id=1, source_target_pairs={{0,4},{1,5},{2,6},{3,7},{4,8},{5,9},{6,10},{7,11},{8,12},{9,13},{1... | collective-permute-start | bytes 884744 | tf_op jit(solution)/shard_map/ppermute | solution.py:373
  195.5 16.7 %collective-permute-start.41 = (bf16[128,1152]{1,0:T(8,128)(2,1)S(1)}, bf16[128,1152]{1,0:T(8,128)(2,1)S(1)}, u32[]{:S(2)}, u32[]{:S(2)}) collective-permute-start(bf16[128,1152]{1,0:T(8,128)(2,1)S(1)} %add_convert_fusion.6), channel_id=1, source_target_pairs={{0,2},{1,3},{2,0},{3,1},{4,6},{5,7},{6,4},{7,5},{8,10},{9,11},{10,... | collective-permute-start | bytes 884744 | tf_op jit(solution)/shard_map/ppermute | solution.py:370
  197.8 18.2 %collective-permute-start.46 = (bf16[128,2048]{1,0:T(8,128)(2,1)S(1)}, bf16[128,2048]{1,0:T(8,128)(2,1)S(1)}, u32[]{:S(2)}, u32[]{:S(2)}) collective-permute-start(bf16[128,2048]{1,0:T(8,128)(2,1)S(1)} %get-tuple-element.62), channel_id=1, source_target_pairs={{0,1},{1,0},{2,3},{3,2},{4,5},{5,4},{6,7},{7,6},{8,9},{9,8},{10,11... | collective-permute-start | bytes 1572872 | tf_op jit(solution)/shard_map/ppermute | solution.py:370
  (47 other events, 535.1 us)
